TPU v7x, 32 devices: a whole 2x2x4 slice. The times are simulated.
32 devices in a mesh: dp: 8 (over y, x, core), fsdp: 4 (over z).
Axes of the slice: x: 2, y: 2, z: 4, core: 2. Of those that a mesh axis runs over, the one named last changes fastest.
Arguments:
- x_prompt: bfloat16 [8, 1024, 1024], P('dp', 'fsdp'), may hold values from -6 to 6
- x_cont: bfloat16 [8, 1024, 1024], P('dp', 'fsdp'), may hold values from -6 to 6
- cot_prompt: bfloat16 [8, 1024, 1024], P('dp', 'fsdp'), may hold values from -6 to 6
- cot_cont: bfloat16 [8, 1024, 1024], P('dp', 'fsdp'), may hold values from -6 to 6
- gain_attn: float32 [1024], replicated, may hold values from 0.25 to 1.75
- gain_mem: float32 [1024], replicated, may hold values from 0.25 to 1.75
- w_qkv: bfloat16 [3, 1024, 1024], P(None, 'fsdp'), may hold values from -0.1875 to 0.1875
- w_attn_out: bfloat16 [1024, 1024], P('fsdp'), may hold values from -2 to 2
- w_mem_query: bfloat16 [1024, 4096], P('fsdp'), may hold values from -0.1875 to 0.1875
- sub_keys: bfloat16 [2048, 512], P('fsdp'), may hold values from -0.25 to 0.25
- w_gate: bfloat16 [1024, 1024], P('fsdp'), may hold values from -0.1875 to 0.1875
- w_mem_out: bfloat16 [1024, 1024], P('fsdp'), may hold values from -0.1875 to 0.1875
- value_rows: bfloat16 [65536, 1024], P(('dp', 'fsdp')), may hold values from -9 to 9
- request: int32 [2, 32, 32, 16], P(None, ('dp', 'fsdp')), may hold values from -1 to 2047, as said below
- slot_prompt: int32 [8, 1024, 4, 32], P('dp', 'fsdp'), may hold values from 0 to 511, as said below
- slot_cont: int32 [8, 1024, 4, 32], P('dp', 'fsdp'), may hold values from 0 to 511, as said below
Outputs:
- out_prompt: bfloat16 [8, 1024, 1024], P('dp', 'fsdp')
- out_cont: bfloat16 [8, 1024, 1024], P('dp', 'fsdp')
- grad_prompt: float32 [8, 1024, 1024], P('dp', 'fsdp')
- grad_cont: float32 [8, 1024, 1024], P('dp', 'fsdp')
- grad_gain_attn: float32 [1024], P(('dp', 'fsdp'))
- grad_gain_mem: float32 [1024], P(('dp', 'fsdp'))
- grad_qkv: float32 [3, 1024, 1024], P(None, ('dp', 'fsdp'))
- grad_attn_out: float32 [1024, 1024], P(('dp', 'fsdp'))
- grad_mem_query: float32 [1024, 4096], P(('dp', 'fsdp'))
- grad_sub_keys: float32 [2048, 512], P(('dp', 'fsdp'))
- grad_gate: float32 [1024, 1024], P(('dp', 'fsdp'))
- grad_mem_out: float32 [1024, 1024], P(('dp', 'fsdp'))
- grad_values: float32 [65536, 1024], P(('dp', 'fsdp'))
Inputs may be any that keep to these rules, and one draw needn't show every extreme that they name: request[u, s, o, j] is an offset into owner o's 2048 value rows, or -1 for an empty slot. In each list the offsets come first, are distinct, and number 1 to 16. In each micro-batch 32 // 4 owners receive a full list from every device. `slot_prompt`: A slot o * 16 + j names entry j of the list from the token's own device to owner o in micro-batch 0; that entry is not -1. Every non-empty entry of a device's lists is named by some pick of that device. `slot_cont`: as slot_prompt, for micro-batch 1.
All inputs are finite; a program needn't handle non-finite values.
Results may differ from a plain program's by a relative error of at most 0.015.
The roundings to bfloat16 on the way count: a program that leaves them out, or rounds other values in their place, can miss the bound.
Values may be sent and summed in bfloat16 or wider, within the bound.
A program may use at most 192 MiB of HBM per device.

v0:
```python
import jax
import jax.numpy as jnp
from jax import lax
from jax.sharding import PartitionSpec as P

HEADS = 16
HDIM = 64
MH = 4
HALF = 512
SUB = 256
PL = 1024


def normalize(matrix, gain_vec):
    inverse = lax.rsqrt(jnp.mean(matrix * matrix, axis=-1, keepdims=True) + 1e-05)
    return (matrix * inverse * gain_vec, inverse)


def norm_backward(matrix, inverse, gain_vec, grad_normed):
    scaled = gain_vec * grad_normed
    cubed = inverse * inverse * inverse
    grad_matrix = inverse * scaled - matrix * cubed * jnp.mean(
        matrix * scaled, axis=-1, keepdims=True
    )
    return (grad_matrix, jnp.sum(grad_normed * matrix * inverse, axis=0))


def head_pairs(matrix):
    row_count = matrix.shape[0]
    return matrix.reshape(row_count, HEADS // 2, 2, HDIM).transpose(1, 0, 2, 3)


def merge_pairs(matrix):
    row_count = matrix.shape[1]
    return matrix.transpose(1, 0, 2, 3).reshape(row_count, HEADS * HDIM)


def attend_forward(queries, key_rows, val_rows, visible):

    def one_pair(pieces):
        q_pair, k_pair, v_pair = pieces
        scores = (
            jnp.einsum("qhd,khd->hqk", q_pair, k_pair, preferred_element_type=jnp.float32) * 0.125
        )
        scores = jnp.where(visible[None], scores, -1e30)
        row_max = jnp.max(scores, axis=-1, keepdims=True)
        expo_rows = jnp.exp(scores - row_max)
        row_total = jnp.sum(expo_rows, axis=-1, keepdims=True)
        weights = (expo_rows / row_total).astype(jnp.bfloat16)
        blended = jnp.einsum("hqk,khd->qhd", weights, v_pair, preferred_element_type=jnp.float32)
        return (blended.astype(jnp.bfloat16), (row_max + jnp.log(row_total))[..., 0])

    blended, logsum = lax.map(
        one_pair, (head_pairs(queries), head_pairs(key_rows), head_pairs(val_rows))
    )
    return (merge_pairs(blended), logsum)


def attend_backward(queries, key_rows, val_rows, visible, logsum, grad_out):

    def one_pair(pieces):
        q_pair, k_pair, v_pair, lse_pair, g_pair = pieces
        scores = (
            jnp.einsum("qhd,khd->hqk", q_pair, k_pair, preferred_element_type=jnp.float32) * 0.125
        )
        scores = jnp.where(visible[None], scores, -1e30)
        weights = jnp.exp(scores - lse_pair[..., None])
        grad_weights = jnp.einsum(
            "qhd,khd->hqk", g_pair, v_pair, preferred_element_type=jnp.float32
        )
        row_dot = jnp.sum(weights * grad_weights, axis=-1, keepdims=True)
        grad_scores = (weights * (grad_weights - row_dot)).astype(jnp.bfloat16)
        grad_q = (
            jnp.einsum("hqk,khd->qhd", grad_scores, k_pair, preferred_element_type=jnp.float32)
            * 0.125
        )
        grad_k = (
            jnp.einsum("hqk,qhd->khd", grad_scores, q_pair, preferred_element_type=jnp.float32)
            * 0.125
        )
        grad_v = jnp.einsum(
            "hqk,qhd->khd", weights.astype(jnp.bfloat16), g_pair, preferred_element_type=jnp.float32
        )
        return (grad_q, grad_k, grad_v)

    results = lax.map(
        one_pair,
        (
            head_pairs(queries),
            head_pairs(key_rows),
            head_pairs(val_rows),
            logsum,
            head_pairs(grad_out),
        ),
    )
    return (merge_pairs(results[0]), merge_pairs(results[1]), merge_pairs(results[2]))


def attention_inputs(x_rows, gain_vec, w_qkv_full):
    normed, inverse = normalize(x_rows, gain_vec)
    normed_b = normed.astype(jnp.bfloat16)
    projected = [
        jnp.dot(normed_b, w_qkv_full[number], preferred_element_type=jnp.float32).astype(
            jnp.bfloat16
        )
        for number in range(3)
    ]
    return (normed_b, inverse, projected)


def qkv_backward(x_rows, inverse, normed_b, gain_vec, w_qkv_full, grads_wide):
    rounded = [one_grad.astype(jnp.bfloat16) for one_grad in grads_wide]
    grad_normed = jnp.dot(rounded[0], w_qkv_full[0].T, preferred_element_type=jnp.float32)
    grad_normed = grad_normed + jnp.dot(
        rounded[1], w_qkv_full[1].T, preferred_element_type=jnp.float32
    )
    grad_normed = grad_normed + jnp.dot(
        rounded[2], w_qkv_full[2].T, preferred_element_type=jnp.float32
    )
    weight_grad = jnp.stack(
        [
            jnp.dot(normed_b.T, rounded[number], preferred_element_type=jnp.float32)
            for number in range(3)
        ]
    )
    grad_x, grad_gain = norm_backward(x_rows, inverse, gain_vec, grad_normed)
    return (grad_x, weight_grad, grad_gain)


def fetch_weights(shards):
    return (
        lax.all_gather(shards[0], "fsdp", axis=1, tiled=True),
        lax.all_gather(shards[1], "fsdp", axis=0, tiled=True),
        lax.all_gather(shards[2], "fsdp", axis=0, tiled=True),
        lax.all_gather(shards[3], "fsdp", axis=0, tiled=True),
        lax.all_gather(shards[4], "fsdp", axis=0, tiled=True),
        lax.all_gather(shards[5], "fsdp", axis=0, tiled=True),
    )


def serve_rows(asked, value_rows):
    found_rows = value_rows[jnp.maximum(asked, 0)]
    return jnp.where((asked >= 0)[..., None], found_rows, jnp.zeros_like(found_rows))


def fetch_table(asked_rows, value_rows):
    owners, capacity = asked_rows.shape
    served = lax.all_to_all(asked_rows, ("dp", "fsdp"), split_axis=0, concat_axis=0, tiled=True)
    replies, served = (
        lax.all_to_all(
            serve_rows(served, value_rows), ("dp", "fsdp"), split_axis=0, concat_axis=0, tiled=True
        ),
        served,
    )
    return (replies.reshape(owners * capacity, -1), served)


def return_grads(slot_grads, served, grad_rows):
    owners, capacity = served.shape
    arrived = lax.all_to_all(
        slot_grads.reshape(owners, capacity, -1).astype(jnp.bfloat16),
        ("dp", "fsdp"),
        split_axis=0,
        concat_axis=0,
        tiled=True,
    ).astype(jnp.float32)
    arrived = jnp.where((served >= 0)[..., None], arrived, 0.0)
    return grad_rows.at[jnp.maximum(served, 0)].add(arrived)


def memory_forward(normed_b, asked_rows, slot_ids, mem_weights, value_table, shard_rows):
    w_mem_query, sub_keys, w_gate, w_mem_out = mem_weights
    row_count = normed_b.shape[0]
    owners, capacity = asked_rows.shape
    query_all = jnp.dot(normed_b, w_mem_query, preferred_element_type=jnp.float32).astype(
        jnp.bfloat16
    )
    query_heads = query_all.reshape(row_count, MH, 2, HALF)
    key_heads = sub_keys.reshape(MH, 2, SUB, HALF)
    sub_scores = jnp.einsum(
        "rmah,mash->rmas", query_heads, key_heads, preferred_element_type=jnp.float32
    )
    owner_of = slot_ids // capacity
    picked = owner_of * shard_rows + asked_rows[owner_of, slot_ids % capacity]
    first_half = picked // SUB
    second_half = picked % SUB
    pick_scores = jnp.take_along_axis(
        sub_scores[:, :, 0], first_half, axis=2
    ) + jnp.take_along_axis(sub_scores[:, :, 1], second_half, axis=2)
    pick_weight = jax.nn.softmax(pick_scores, axis=-1)
    row_ids = jnp.arange(row_count)[:, None, None]
    mixing = (
        jnp.zeros((row_count, owners * capacity), jnp.float32)
        .at[row_ids, slot_ids]
        .add(pick_weight)
        .astype(jnp.bfloat16)
    )
    memory_out = jnp.dot(mixing, value_table, preferred_element_type=jnp.float32)
    gate_pre = jnp.dot(normed_b, w_gate, preferred_element_type=jnp.float32)
    blended = (memory_out * jax.nn.silu(gate_pre)).astype(jnp.bfloat16)
    branch = jnp.dot(blended, w_mem_out, preferred_element_type=jnp.float32)
    return (
        branch,
        (query_heads, first_half, second_half, pick_weight, mixing, memory_out, gate_pre, blended),
    )


def memory_backward(grad_branch, normed_b, slot_ids, mem_weights, value_table, saved):
    w_mem_query, sub_keys, w_gate, w_mem_out = mem_weights
    query_heads, first_half, second_half, pick_weight, mixing, memory_out, gate_pre, blended = saved
    row_count = normed_b.shape[0]
    grad_blend = jnp.dot(grad_branch, w_mem_out.T, preferred_element_type=jnp.float32)
    grad_mem_out = jnp.dot(blended.T, grad_branch, preferred_element_type=jnp.float32)
    sigmoid_gate = jax.nn.sigmoid(gate_pre)
    grad_memory = (grad_blend * gate_pre * sigmoid_gate).astype(jnp.bfloat16)
    grad_gate = (
        grad_blend * memory_out * sigmoid_gate * (1.0 + gate_pre * (1.0 - sigmoid_gate))
    ).astype(jnp.bfloat16)
    grad_mixing = jnp.dot(grad_memory, value_table.T, preferred_element_type=jnp.float32)
    slot_grads = jnp.dot(mixing.T, grad_memory, preferred_element_type=jnp.float32)
    grad_pick = jnp.take_along_axis(grad_mixing, slot_ids.reshape(row_count, -1), axis=1).reshape(
        pick_weight.shape
    )
    grad_scores = pick_weight * (
        grad_pick - jnp.sum(pick_weight * grad_pick, axis=-1, keepdims=True)
    )
    row_ids = jnp.arange(row_count)[:, None, None]
    head_ids = jnp.arange(MH)[None, :, None]
    grad_first = (
        jnp.zeros((row_count, MH, SUB), jnp.float32)
        .at[row_ids, head_ids, first_half]
        .add(grad_scores)
    )
    grad_second = (
        jnp.zeros((row_count, MH, SUB), jnp.float32)
        .at[row_ids, head_ids, second_half]
        .add(grad_scores)
    )
    grad_sub = jnp.stack([grad_first, grad_second], axis=2).astype(jnp.bfloat16)
    key_heads = sub_keys.reshape(MH, 2, SUB, HALF)
    grad_query = jnp.einsum(
        "rmas,mash->rmah", grad_sub, key_heads, preferred_element_type=jnp.float32
    )
    grad_query = grad_query.reshape(row_count, MH * 2 * HALF).astype(jnp.bfloat16)
    grad_keys = jnp.einsum(
        "rmas,rmah->mash", grad_sub, query_heads, preferred_element_type=jnp.float32
    ).reshape(MH * 2 * SUB, HALF)
    grad_normed = jnp.dot(grad_query, w_mem_query.T, preferred_element_type=jnp.float32)
    grad_normed = grad_normed + jnp.dot(grad_gate, w_gate.T, preferred_element_type=jnp.float32)
    grad_query_w = jnp.dot(normed_b.T, grad_query, preferred_element_type=jnp.float32)
    grad_gate_w = jnp.dot(normed_b.T, grad_gate, preferred_element_type=jnp.float32)
    return (grad_normed, slot_grads, (grad_query_w, grad_keys, grad_gate_w, grad_mem_out))


def per_device(
    x_prompt,
    x_cont,
    cot_prompt,
    cot_cont,
    gain_attn,
    gain_mem,
    w_qkv,
    w_attn_out,
    w_mem_query,
    sub_keys,
    w_gate,
    w_mem_out,
    value_rows,
    request,
    slot_prompt,
    slot_cont,
):
    shards = (w_qkv, w_attn_out, w_mem_query, sub_keys, w_gate, w_mem_out)

    def current():
        return fetch_weights(shards)

    shard_rows = value_rows.shape[0]
    prompt_x = x_prompt[0].astype(jnp.float32)
    cont_x = x_cont[0].astype(jnp.float32)
    prompt_rows = prompt_x.shape[0]
    cont_rows = cont_x.shape[0]
    gathered = current()
    normed_p, inverse_p, (query_p, key_p, val_p) = attention_inputs(
        prompt_x, gain_attn, gathered[0]
    )
    all_keys, all_vals = (
        lax.all_gather(key_p, "fsdp", axis=0, tiled=True),
        lax.all_gather(val_p, "fsdp", axis=0, tiled=True),
    )
    start_row = lax.axis_index("fsdp") * prompt_rows
    visible_p = jnp.arange(PL)[None, :] <= start_row + jnp.arange(prompt_rows)[:, None]
    att_p, logsum_p = attend_forward(query_p, all_keys, all_vals, visible_p)
    hidden_p = prompt_x + jnp.dot(att_p, gathered[1], preferred_element_type=jnp.float32)
    normed2_p, inverse2_p = normalize(hidden_p, gain_mem)
    normed2_pb = normed2_p.astype(jnp.bfloat16)
    table_p, served_p = fetch_table(request[0, 0], value_rows)
    branch_p, saved_p = memory_forward(
        normed2_pb, request[0, 0], slot_prompt[0], gathered[2:], table_p, shard_rows
    )
    out_p = (hidden_p + branch_p).astype(jnp.bfloat16)
    gathered = current()
    normed_c, inverse_c, (query_c, key_c, val_c) = attention_inputs(cont_x, gain_attn, gathered[0])
    key_join = jnp.concatenate([all_keys, key_c], axis=0)
    val_join = jnp.concatenate([all_vals, val_c], axis=0)
    visible_c = jnp.concatenate(
        [
            jnp.ones((cont_rows, PL), jnp.bool_),
            jnp.arange(cont_rows)[None, :] <= jnp.arange(cont_rows)[:, None],
        ],
        axis=1,
    )
    att_c, logsum_c = attend_forward(query_c, key_join, val_join, visible_c)
    hidden_c = cont_x + jnp.dot(att_c, gathered[1], preferred_element_type=jnp.float32)
    normed2_c, inverse2_c = normalize(hidden_c, gain_mem)
    normed2_cb = normed2_c.astype(jnp.bfloat16)
    table_c, served_c = fetch_table(request[1, 0], value_rows)
    branch_c, saved_c = memory_forward(
        normed2_cb, request[1, 0], slot_cont[0], gathered[2:], table_c, shard_rows
    )
    out_c = (hidden_c + branch_c).astype(jnp.bfloat16)
    gathered = current()
    grad_norm2_c, slot_grads_c, mem_grads_c = memory_backward(
        cot_cont[0], normed2_cb, slot_cont[0], gathered[2:], table_c, saved_c
    )
    grad_rows = return_grads(slot_grads_c, served_c, jnp.zeros(value_rows.shape, jnp.float32))
    back_c, gain_mem_c = norm_backward(hidden_c, inverse2_c, gain_mem, grad_norm2_c)
    grad_hidden_c = cot_cont[0].astype(jnp.float32) + back_c
    hidden_cb = grad_hidden_c.astype(jnp.bfloat16)
    grad_wo_c = jnp.dot(att_c.T, hidden_cb, preferred_element_type=jnp.float32)
    grad_att_c = jnp.dot(hidden_cb, gathered[1].T, preferred_element_type=jnp.float32).astype(
        jnp.bfloat16
    )
    grad_q_c, grad_k_join, grad_v_join = attend_backward(
        query_c, key_join, val_join, visible_c, logsum_c, grad_att_c
    )
    grad_x_c, qkv_grad_c, gain_attn_c = qkv_backward(
        cont_x,
        inverse_c,
        normed_c,
        gain_attn,
        gathered[0],
        [grad_q_c, grad_k_join[PL:], grad_v_join[PL:]],
    )
    grad_cont = grad_hidden_c + grad_x_c
    gathered = current()
    grad_norm2_p, slot_grads_p, mem_grads_p = memory_backward(
        cot_prompt[0], normed2_pb, slot_prompt[0], gathered[2:], table_p, saved_p
    )
    grad_rows = return_grads(slot_grads_p, served_p, grad_rows)
    back_p, gain_mem_p = norm_backward(hidden_p, inverse2_p, gain_mem, grad_norm2_p)
    grad_hidden_p = cot_prompt[0].astype(jnp.float32) + back_p
    hidden_pb = grad_hidden_p.astype(jnp.bfloat16)
    grad_wo_p = jnp.dot(att_p.T, hidden_pb, preferred_element_type=jnp.float32)
    grad_att_p = jnp.dot(hidden_pb, gathered[1].T, preferred_element_type=jnp.float32).astype(
        jnp.bfloat16
    )
    grad_q_p, grad_k_span, grad_v_span = attend_backward(
        query_p, all_keys, all_vals, visible_p, logsum_p, grad_att_p
    )
    key_grads = grad_k_join[:PL] + grad_k_span
    val_grads = grad_v_join[:PL] + grad_v_span
    own_keys, own_vals = (
        lax.psum_scatter(
            key_grads.astype(jnp.bfloat16), "fsdp", scatter_dimension=0, tiled=True
        ).astype(jnp.float32),
        lax.psum_scatter(
            val_grads.astype(jnp.bfloat16), "fsdp", scatter_dimension=0, tiled=True
        ).astype(jnp.float32),
    )
    grad_x_p, qkv_grad_p, gain_attn_p = qkv_backward(
        prompt_x, inverse_p, normed_p, gain_attn, gathered[0], [grad_q_p, own_keys, own_vals]
    )
    grad_prompt = grad_hidden_p + grad_x_p
    reduced = (
        lax.psum_scatter(qkv_grad_c + qkv_grad_p, ("dp", "fsdp"), scatter_dimension=1, tiled=True),
        lax.psum_scatter(grad_wo_c + grad_wo_p, ("dp", "fsdp"), scatter_dimension=0, tiled=True),
        lax.psum_scatter(
            mem_grads_c[0] + mem_grads_p[0], ("dp", "fsdp"), scatter_dimension=0, tiled=True
        ),
        lax.psum_scatter(
            mem_grads_c[1] + mem_grads_p[1], ("dp", "fsdp"), scatter_dimension=0, tiled=True
        ),
        lax.psum_scatter(
            mem_grads_c[2] + mem_grads_p[2], ("dp", "fsdp"), scatter_dimension=0, tiled=True
        ),
        lax.psum_scatter(
            mem_grads_c[3] + mem_grads_p[3], ("dp", "fsdp"), scatter_dimension=0, tiled=True
        ),
        lax.psum_scatter(
            gain_attn_c + gain_attn_p, ("dp", "fsdp"), scatter_dimension=0, tiled=True
        ),
        lax.psum_scatter(gain_mem_c + gain_mem_p, ("dp", "fsdp"), scatter_dimension=0, tiled=True),
    )
    return (
        out_p[None],
        out_c[None],
        grad_prompt[None],
        grad_cont[None],
        reduced[6],
        reduced[7],
        reduced[0],
        reduced[1],
        reduced[2],
        reduced[3],
        reduced[4],
        reduced[5],
        grad_rows,
    )


def solution(mesh):
    in_specs = (
        P("dp", "fsdp", None),
        P("dp", "fsdp", None),
        P("dp", "fsdp", None),
        P("dp", "fsdp", None),
        P(),
        P(),
        P(None, "fsdp", None),
        P("fsdp", None),
        P("fsdp", None),
        P("fsdp", None),
        P("fsdp", None),
        P("fsdp", None),
        P(("dp", "fsdp"), None),
        P(None, ("dp", "fsdp"), None, None),
        P("dp", "fsdp", None, None),
        P("dp", "fsdp", None, None),
    )
    out_specs = (
        P("dp", "fsdp", None),
        P("dp", "fsdp", None),
        P("dp", "fsdp", None),
        P("dp", "fsdp", None),
        P(("dp", "fsdp")),
        P(("dp", "fsdp")),
        P(None, ("dp", "fsdp"), None),
        P(("dp", "fsdp"), None),
        P(("dp", "fsdp"), None),
        P(("dp", "fsdp"), None),
        P(("dp", "fsdp"), None),
        P(("dp", "fsdp"), None),
        P(("dp", "fsdp"), None),
    )
    return jax.shard_map(
        per_device, mesh=mesh, in_specs=in_specs, out_specs=out_specs, check_vma=False
    )
```

profile of v0, /device:TPU:0, one launch (start us, length us, event | category | flops | bytes accessed | tf_op | source)
XLA Modules:
  0.0 5515.5 jit_solution(16066706638488382413)
XLA Ops:
  9.8 117.9 %all-gather.9.cloned.1.call-done = bf16[3,1024,1024]{2,1,0:T(8,128)(2,1)} async-done(((bf16[3,256,1024]{2,1,0:T(8,128)(2,1)}), bf16[3,1024,1024]{2,1,0:T(8,128)(2,1)}) %all-gather.9.cloned.1.call-update) | async-done | bytes 6291472 | tf_op jit(solution)/shard_map/all_gather | solution.py:132
  147.9 217.1 %gather_fusion.2 = s32[32768]{0:T(1024)S(1)} fusion(s32[32,16]{0,1:T(8,128)S(1)} %get-tuple-element.369, s32[32768]{0:T(1024)S(1)} %reshape.1100), kind=kCustom, calls=%fused_computation.8 | custom fusion | bytes 524288 | tf_op jit(solution)/shard_map/gather | solution.py:184
  368.8 217.2 %gather_fusion = s32[32768]{0:T(1024)S(1)} fusion(s32[32,16]{0,1:T(8,128)S(1)} %copy-done, s32[32768]{0:T(1024)S(1)} %reshape.1086), kind=kCustom, calls=%fused_computation.6 | custom fusion | bytes 524288 | tf_op jit(solution)/shard_map/gather | solution.py:184
  680.5 37.8 while.56
  719.8 37.6 while.54
  777.7 258.6 %gather_fusion.8 = f32[32768]{0:T(1024)S(1)} fusion(f32[256,512]{1,0:T(8,128)S(1)} %fusion.238, s32[32768]{0:T(1024)S(1)} %bitcast.661), kind=kCustom, calls=%fused_computation.1.clone | custom fusion | bytes 524288 | tf_op jit(solution)/shard_map/jit(take_along_axis)/gather | solution.py:221
  1042.4 258.4 %gather_fusion.9 = f32[32768]{0:T(1024)S(1)} fusion(f32[256,512]{1,0:T(8,128)S(1)} %fusion.240, s32[32768]{0:T(1024)S(1)} %bitcast.660), kind=kCustom, calls=%fused_computation.5.clone | custom fusion | bytes 524288 | tf_op jit(solution)/shard_map/jit(take_along_axis)/gather | solution.py:221
  1316.9 313.9 %gather_fusion.7 = f32[32768]{0:T(1024)S(1)} fusion(f32[256,4,256]{2,0,1:T(8,128)S(1)} %get-tuple-element.360, s32[32768]{0:T(1024)S(1)} %copy-done.6), kind=kCustom, calls=%fused_computation.4.clone | custom fusion | bytes 655360 | tf_op jit(solution)/shard_map/jit(take_along_axis)/gather | solution.py:189
  1632.1 313.9 %gather_fusion.6 = f32[32768]{0:T(1024)S(1)} fusion(f32[256,4,256]{2,0,1:T(8,128)S(1)} %copy-done.1, s32[32768]{0:T(1024)S(1)} %copy-done.5), kind=kCustom, calls=%fused_computation.3.clone | custom fusion | bytes 655360 | tf_op jit(solution)/shard_map/jit(take_along_axis)/gather | solution.py:187
  1947.6 226.8 %scatter_custom_fusion.3 = f32[131072]{0:T(1024)S(1)} fusion(s32[32768]{0:T(1024)} %reshape.1136, f32[32768]{0:T(1024)S(1)} %reshape.1138, f32[]{:T(128)} %constant.223.clone.1), kind=kCustom, calls=%fused_computation.365 | custom fusion | flops 32768 | bytes 524800
  2175.8 226.7 %scatter_custom_fusion.7 = f32[262144]{0:T(1024)S(1)} fusion(s32[32768]{0:T(1024)} %reshape.1160, f32[32768]{0:T(1024)S(1)} %reshape.1156, f32[]{:T(128)} %constant.223.clone.1), kind=kCustom, calls=%fused_computation.328 | custom fusion | flops 32768 | bytes 1049088
  2403.7 226.3 %scatter_custom_fusion.6 = f32[262144]{0:T(1024)S(1)} fusion(s32[32768]{0:T(1024)} %reshape.1154, f32[32768]{0:T(1024)S(1)} %reshape.1156, f32[]{:T(128)} %constant.223.clone.1), kind=kCustom, calls=%fused_computation.330 | custom fusion | flops 32768 | bytes 1049088
  2655.9 313.9 %gather_fusion.5 = f32[32768]{0:T(1024)S(1)} fusion(f32[256,4,256]{2,0,1:T(8,128)S(1)} %get-tuple-element.362, s32[32768]{0:T(1024)S(1)} %copy-done.4), kind=kCustom, calls=%fused_computation.2.clone | custom fusion | bytes 655360 | tf_op jit(solution)/shard_map/jit(take_along_axis)/gather | solution.py:189
  2971.0 313.9 %gather_fusion.4 = f32[32768]{0:T(1024)S(1)} fusion(f32[256,4,256]{2,0,1:T(8,128)S(1)} %copy-done.2, s32[32768]{0:T(1024)S(1)} %copy-done.3), kind=kCustom, calls=%fused_computation.clone | custom fusion | bytes 655360 | tf_op jit(solution)/shard_map/jit(take_along_axis)/gather | solution.py:187
  3286.6 226.8 %scatter_custom_fusion.2 = f32[131072]{0:T(1024)S(1)} fusion(s32[32768]{0:T(1024)} %reshape.1130, f32[32768]{0:T(1024)S(1)} %reshape.1132, f32[]{:T(128)} %constant.223.clone.1), kind=kCustom, calls=%fused_computation.367 | custom fusion | flops 32768 | bytes 524800
  3514.8 226.5 %scatter_custom_fusion.5 = f32[262144]{0:T(1024)S(1)} fusion(s32[32768]{0:T(1024)} %reshape.1148, f32[32768]{0:T(1024)S(1)} %reshape.1144, f32[]{:T(128)} %constant.223.clone.1), kind=kCustom, calls=%fused_computation.332 | custom fusion | flops 32768 | bytes 1049088
  3742.5 226.3 %scatter_custom_fusion.4 = f32[262144]{0:T(1024)S(1)} fusion(s32[32768]{0:T(1024)} %reshape.1142, f32[32768]{0:T(1024)S(1)} %reshape.1144, f32[]{:T(128)} %constant.223.clone.1), kind=kCustom, calls=%fused_computation.334 | custom fusion | flops 32768 | bytes 1049088
  4005.8 79.6 %while.57 = (s32[]{:T(128)}, bf16[8,256,2,64]{1,3,2,0:T(8,128)(2,1)S(1)}, f32[8,1024,2,64]{1,3,2,0:T(8,128)}, f32[8,1024,2,64]{1,3,2,0:T(8,128)}, bf16[8,1024,2,...) while((s32[]{:T(128)}, ...), condition=%wide.region_24.27_spmd.clone, body=%wide.region_22.26_spmd.clone.sunk | while | flops 340688384 | bytes 18497656 | solution.py:86
  4086.2 74.9 %while.55 = (s32[]{:T(128)}, bf16[8,256,2,64]{1,3,2,0:T(8,128)(2,1)S(1)}, f32[8,1280,2,64]{1,3,2,0:T(8,128)}, f32[8,1280,2,64]{1,3,2,0:T(8,128)}, bf16[8,1280,2,...) while((s32[]{:T(128)}, ...), condition=%wide.region_31.34_spmd, body=%wide.region_29.33_spmd.sunk | while | flops 425524736 | bytes 22690936 | solution.py:86
  4216.0 41.5 reduce-scatter.9.cloned.1.call-done
  4259.8 12.4 maximum_add_fusion
  4272.5 10.2 fusion.242
  4282.7 14.1 convolution_add_fusion
  4310.4 37.8 all-to-all-done.4
  4380.3 18.5 all-to-all-done.5
  4401.6 12.5 scatter_fusion
  4421.1 43.9 all-reduce.3
  4468.7 103.3 %reduce-scatter.15.cloned.1.call-done = f32[32,1024]{1,0:T(8,128)} async-done(((f32[1024,1024]{1,0:T(8,128)}), f32[32,1024]{1,0:T(8,128)}) %reduce-scatter.15.cloned.1.call-update) | async-done | bytes 131088 | tf_op jit(solution)/shard_map/reduce_scatter | solution.py:377
  4572.0 149.1 %reduce-scatter.21.cloned.1.call-done = f32[32,1024]{1,0:T(8,128)} async-done(((f32[1024,1024]{1,0:T(8,128)}), f32[32,1024]{1,0:T(8,128)}) %reduce-scatter.21.cloned.1.call-update) | async-done | bytes 131088 | tf_op jit(solution)/shard_map/reduce_scatter | solution.py:384
  4721.1 149.3 %reduce-scatter.23.cloned.1.call-done = f32[32,1024]{1,0:T(8,128)} async-done(((f32[1024,1024]{1,0:T(8,128)}), f32[32,1024]{1,0:T(8,128)}) %reduce-scatter.23.cloned.1.call-update) | async-done | bytes 131088 | tf_op jit(solution)/shard_map/reduce_scatter | solution.py:387
  4870.4 273.8 %reduce-scatter.13.cloned.1.call-done = f32[3,32,1024]{2,1,0:T(8,128)} async-done(((f32[3,1024,1024]{2,1,0:T(8,128)}), f32[3,32,1024]{2,1,0:T(8,128)}) %reduce-scatter.13.cloned.1.call-update) | async-done | bytes 393232 | tf_op jit(solution)/shard_map/reduce_scatter | solution.py:376
  5144.2 364.4 %reduce-scatter.17.cloned.1.call-done = f32[32,4096]{1,0:T(8,128)} async-done(((f32[1024,4096]{1,0:T(8,128)}), f32[32,4096]{1,0:T(8,128)}) %reduce-scatter.17.cloned.1.call-update) | async-done | bytes 524304 | tf_op jit(solution)/shard_map/reduce_scatter | solution.py:378
  (765 shorter events, 583.1 us)
Async XLA Ops:
  7.2 120.5 %all-gather.9.cloned.1.call-start = ((), (), s32[]{:S(2)}) async-start(), calls=%async_computation.14 | async-start | bytes 7864320 | tf_op jit(solution)/shard_map/all_gather | solution.py:132
  7.9 650.7 %all-gather.11.cloned.1.call-start = ((), (), s32[]{:S(2)}) async-start(), calls=%async_computation.15 | async-start | bytes 2621440 | tf_op jit(solution)/shard_map/all_gather | solution.py:289
  131.1 535.3 %all-gather.13.cloned.1.call-start = ((), (), s32[]{:S(2)}) async-start(), calls=%async_computation.16 | async-start | bytes 2621440 | tf_op jit(solution)/shard_map/all_gather | solution.py:288
  134.3 623.1 %all-gather.15.cloned.1.call-start = ((), (), s32[]{:S(2)}) async-start(), calls=%async_computation.17 | async-start | bytes 2621440 | tf_op jit(solution)/shard_map/all_gather | solution.py:133
  134.9 634.5 %all-gather.21.cloned.1.call-start = ((), (), s32[]{:S(2)}) async-start(), calls=%async_computation.20 | async-start | bytes 2621440 | tf_op jit(solution)/shard_map/all_gather | solution.py:136
  135.5 636.5 %all-gather.23.cloned.1.call-start = ((), (), s32[]{:S(2)}) async-start(), calls=%async_computation.21 | async-start | bytes 2621440 | tf_op jit(solution)/shard_map/all_gather | solution.py:137
  136.1 1165.5 %all-gather.17.cloned.1.call-start = ((), (), s32[]{:S(2)}) async-start(), calls=%async_computation.18 | async-start | bytes 10485760 | tf_op jit(solution)/shard_map/all_gather | solution.py:134
  138.1 476.5 %all-to-all-start = ((s32[32,1,16]{2,1,0:T(1,128)}), s32[32,1,16]{2,1,0:T(1,128)}, u32[]{:S(2)}, u32[]{:S(2)}) async-start(s32[32,1,16]{2,1,0:T(1,128)} %copy.212), calls=%async_computation | async-start | bytes 32768 | tf_op jit(solution)/shard_map/all_to_all | solution.py:148
  141.3 1170.7 %all-gather.19.cloned.1.call-start = ((), (), s32[]{:S(2)}) async-start(), calls=%async_computation.19 | async-start | bytes 2621440 | tf_op jit(solution)/shard_map/all_gather | solution.py:135
  147.9 219.2 %copy-start.53 = (s32[1,256,4,32]{3,2,1,0:T(4,128)S(1)}, s32[1,256,4,32]{3,2,1,0:T(4,128)}, u32[]{:S(2)}) copy-start(s32[1,256,4,32]{3,2,1,0:T(4,128)} %copy.202) | copy-start | bytes 393220
  368.8 218.6 %copy-start.77 = (s32[256,4,32]{2,1,0:T(4,128)S(1)}, s32[256,4,32]{2,1,0:T(4,128)}, u32[]{:S(2)}) copy-start(s32[256,4,32]{2,1,0:T(4,128)} %reshape.1103) | copy-start | bytes 393220
  368.8 218.8 %copy-start.60 = (s32[1,256,4,32]{1,3,2,0:T(8,128)S(1)}, s32[1,256,4,32]{1,3,2,0:T(8,128)}, u32[]{:S(2)}) copy-start(s32[1,256,4,32]{1,3,2,0:T(8,128)} %param.43) | copy-start | bytes 393220
  614.6 12.9 all-to-all-start.2
  642.1 119.0 %all-to-all-start.1 = ((bf16[32,16,1024]{2,1,0:T(8,128)(2,1)}), bf16[32,16,1024]{2,1,0:T(8,128)(2,1)}, u32[]{:S(2)}, u32[]{:S(2)}) async-start(bf16[32,16,1024]{2,1,0:T(8,128)(2,1)} %broadcast_select_fusion.1), calls=%async_computation.1 | async-start | bytes 2097152 | tf_op jit(solution)/shard_map/all_to_all | solution.py:150
  761.1 279.4 %all-to-all-start.3 = ((bf16[32,16,1024]{2,1,0:T(8,128)(2,1)}), bf16[32,16,1024]{2,1,0:T(8,128)(2,1)}, u32[]{:S(2)}, u32[]{:S(2)}) async-start(bf16[32,16,1024]{2,1,0:T(8,128)(2,1)} %broadcast_select_fusion), calls=%async_computation.3 | async-start | bytes 2097152 | tf_op jit(solution)/shard_map/all_to_all | solution.py:150
  767.2 3444.9 %reduce-scatter.11.cloned.1.call-start = ((), (), s32[]{:S(2)}) async-start(), calls=%async_computation.23 | async-start | bytes 2621440 | tf_op jit(solution)/shard_map/reduce_scatter | solution.py:367
  777.6 259.4 %copy-start.13 = (bf16[1024,1024]{1,0:T(8,128)(2,1)S(1)}, bf16[1024,1024]{1,0:T(8,128)(2,1)}, u32[]{:S(2)}) copy-start(bf16[1024,1024]{1,0:T(8,128)(2,1)} %all-gather.21.cloned.1.call-done) | copy-start | bytes 6291460
  777.6 259.4 %copy-start.36 = (bf16[256,1024]{1,0:T(8,128)(2,1)S(1)}, bf16[256,1024]{1,0:T(8,128)(2,1)}, u32[]{:S(2)}) copy-start(bf16[256,1024]{1,0:T(8,128)(2,1)} %get-tuple-element.378) | copy-start | bytes 1572868
  1040.5 260.3 %copy-start.83 = (bf16[256,1024]{1,0:T(8,128)(2,1)}, bf16[256,1024]{1,0:T(8,128)(2,1)S(1)}, u32[]{:S(2)}) copy-start(bf16[256,1024]{1,0:T(8,128)(2,1)S(1)} %get-tuple-element.396) | copy-start | bytes 1572868
  1632.1 314.4 %copy-start.107 = (s32[256,4,32]{0,2,1:T(8,128)S(1)}, s32[256,4,32]{0,2,1:T(8,128)}, u32[]{:S(2)}) copy-start(s32[256,4,32]{0,2,1:T(8,128)} %copy-done.106) | copy-start | bytes 393220
  1632.1 314.4 %copy-start.114 = (f32[256,4,32]{0,2,1:T(8,128)S(1)}, f32[256,4,32]{0,2,1:T(8,128)}, u32[]{:S(2)}) copy-start(f32[256,4,32]{0,2,1:T(8,128)} %copy.228) | copy-start | bytes 393220
  2971.0 314.4 %copy-start.105 = (s32[256,4,32]{0,2,1:T(8,128)S(1)}, s32[256,4,32]{0,2,1:T(8,128)}, u32[]{:S(2)}) copy-start(s32[256,4,32]{0,2,1:T(8,128)} %copy-done.104) | copy-start | bytes 393220
  2971.0 314.4 %copy-start.115 = (f32[256,4,32]{0,2,1:T(8,128)S(1)}, f32[256,4,32]{0,2,1:T(8,128)}, u32[]{:S(2)}) copy-start(f32[256,4,32]{0,2,1:T(8,128)} %copy.210) | copy-start | bytes 393220
  4166.8 90.7 %reduce-scatter.9.cloned.1.call-start = ((), (), s32[]{:S(2)}) async-start(), calls=%async_computation.22 | async-start | bytes 2621440 | tf_op jit(solution)/shard_map/reduce_scatter | solution.py:364
  4172.4 296.3 %reduce-scatter.19.cloned.1.call-start = ((), (), s32[]{:S(2)}) async-start(), calls=%async_computation.27 | async-start | bytes 4325376 | tf_op jit(solution)/shard_map/reduce_scatter | solution.py:381
  4180.7 391.3 %reduce-scatter.15.cloned.1.call-start = ((), (), s32[]{:S(2)}) async-start(), calls=%async_computation.25 | async-start | bytes 4325376 | tf_op jit(solution)/shard_map/reduce_scatter | solution.py:377
  4185.5 535.6 %reduce-scatter.21.cloned.1.call-start = ((), (), s32[]{:S(2)}) async-start(), calls=%async_computation.28 | async-start | bytes 4325376 | tf_op jit(solution)/shard_map/reduce_scatter | solution.py:384
  4191.2 679.3 %reduce-scatter.23.cloned.1.call-start = ((), (), s32[]{:S(2)}) async-start(), calls=%async_computation.29 | async-start | bytes 4325376 | tf_op jit(solution)/shard_map/reduce_scatter | solution.py:387
  4196.3 947.9 %reduce-scatter.13.cloned.1.call-start = ((), (), s32[]{:S(2)}) async-start(), calls=%async_computation.24 | async-start | bytes 12976128 | tf_op jit(solution)/shard_map/reduce_scatter | solution.py:376
  4272.3 1236.3 %reduce-scatter.17.cloned.1.call-start = ((), (), s32[]{:S(2)}) async-start(), calls=%async_computation.26 | async-start | bytes 17301504 | tf_op jit(solution)/shard_map/reduce_scatter | solution.py:378
  4300.3 47.9 all-to-all-start.4
  4348.1 50.7 all-to-all-start.5
  (139 other events, 1040.7 us)
Sparse Core Ops, SparseCore 0:
  9.6 118.0 all-gather.8
  131.2 44.4 all-gather.10
  177.8 44.6 all-gather.12
  224.0 44.6 all-gather.14
  270.0 44.7 all-gather.20
  316.2 44.5 all-gather.22
  362.4 148.3 all-gather.16
  512.4 44.1 all-gather.18
  4167.0 45.0 reduce-scatter.10
  4214.3 43.1 reduce-scatter.8
  4260.4 163.0 reduce-scatter.18
  4426.2 145.7 reduce-scatter.14
  4574.9 146.2 reduce-scatter.20
  4723.8 146.5 reduce-scatter.22
  4873.2 271.0 reduce-scatter.12
  5146.9 361.6 reduce-scatter.16
where the time goes:
time: 5530 us; the launch traced here: 5520 us
  local copies, waits for them, and re-layouts  2330 us (42%)
  other arithmetic  1470 us (27%)
  waiting for transfers between devices  1270 us (23%)
  matrix products  365 us (7%)
    unnamed x14, other arithmetic  1360 us
    gather x10, local copies, waits for them, and re-layouts, memory_forward(): jnp.take_along_axis(sub_scores[:, :, 1], second_half, axis=2)  632 us
    gather x10, local copies, waits for them, and re-layouts, memory_forward(): jnp.take_along_axis(sub_scores[:, :, 0], first_half, axis=2)  631 us
    gather x6, local copies, waits for them, and re-layouts, memory_backward(): jnp.take_along_axis(grad_mixing, slot_ids.reshape(row_count, -1), axis=1)  519 us
    gather x8, local copies, waits for them, and re-layouts, memory_forward(): picked = owner_of * shard_rows + asked_rows[owner_of, slot_ids % capacity]  437 us
    reduce_scatter x1, waiting for transfers between devices, per_device(): lax.psum_scatter(mem_grads_c[0] + mem_grads_p[0], ('dp', 'fsdp'), scatter...  364 us
    reduce_scatter x1, waiting for transfers between devices, per_device(): lax.psum_scatter(qkv_grad_c + qkv_grad_p, ('dp', 'fsdp'), scatter_dimensi...  274 us
    reduce_scatter x1, waiting for transfers between devices, per_device(): lax.psum_scatter(mem_grads_c[3] + mem_grads_p[3], ('dp', 'fsdp'), scatter...  149 us
  transfers between devices with their start and end apart: 22, of which 10 were waited for; matrix products, arithmetic and copies ran while one was open for 23% of the time, Pallas kernels for 0%

commit v1 on v0

v1 whole, which is shorter than its diff:
```python
import jax
import jax.numpy as jnp
from jax import lax
from jax.sharding import PartitionSpec as P

HEADS = 16
HDIM = 64
MH = 4
HALF = 512
SUB = 256
PL = 1024


BF = jnp.bfloat16
F32 = jnp.float32
ALL = ("dp", "fsdp")


def mm(left, right):
    return jnp.dot(left, right, preferred_element_type=F32)


def mm_t(left, right):
    return lax.dot_general(left, right, (((1,), (1,)), ((), ())), preferred_element_type=F32)


def mm_l(left, right):
    return lax.dot_general(left, right, (((0,), (0,)), ((), ())), preferred_element_type=F32)


def normalize(matrix, gain_vec):
    inverse = lax.rsqrt(jnp.mean(matrix * matrix, axis=-1, keepdims=True) + 1e-05)
    return (matrix * inverse * gain_vec, inverse)


def norm_backward(matrix, inverse, gain_vec, grad_normed):
    scaled = gain_vec * grad_normed
    cubed = inverse * inverse * inverse
    grad_matrix = inverse * scaled - matrix * cubed * jnp.mean(
        matrix * scaled, axis=-1, keepdims=True
    )
    return (grad_matrix, jnp.sum(grad_normed * matrix * inverse, axis=0))


def head_pairs(matrix):
    row_count = matrix.shape[0]
    return matrix.reshape(row_count, HEADS // 2, 2, HDIM).transpose(1, 0, 2, 3)


def merge_pairs(matrix):
    row_count = matrix.shape[1]
    return matrix.transpose(1, 0, 2, 3).reshape(row_count, HEADS * HDIM)


def attend_forward(queries, key_rows, val_rows, visible):

    def one_pair(pieces):
        q_pair, k_pair, v_pair = pieces
        scores = (
            jnp.einsum("qhd,khd->hqk", q_pair, k_pair, preferred_element_type=jnp.float32) * 0.125
        )
        scores = jnp.where(visible[None], scores, -1e30)
        row_max = jnp.max(scores, axis=-1, keepdims=True)
        expo_rows = jnp.exp(scores - row_max)
        row_total = jnp.sum(expo_rows, axis=-1, keepdims=True)
        weights = (expo_rows / row_total).astype(jnp.bfloat16)
        blended = jnp.einsum("hqk,khd->qhd", weights, v_pair, preferred_element_type=jnp.float32)
        return (blended.astype(jnp.bfloat16), (row_max + jnp.log(row_total))[..., 0])

    blended, logsum = lax.map(
        one_pair, (head_pairs(queries), head_pairs(key_rows), head_pairs(val_rows))
    )
    return (merge_pairs(blended), logsum)


def attend_backward(queries, key_rows, val_rows, visible, logsum, grad_out):

    def one_pair(pieces):
        q_pair, k_pair, v_pair, lse_pair, g_pair = pieces
        scores = (
            jnp.einsum("qhd,khd->hqk", q_pair, k_pair, preferred_element_type=jnp.float32) * 0.125
        )
        scores = jnp.where(visible[None], scores, -1e30)
        weights = jnp.exp(scores - lse_pair[..., None])
        grad_weights = jnp.einsum(
            "qhd,khd->hqk", g_pair, v_pair, preferred_element_type=jnp.float32
        )
        row_dot = jnp.sum(weights * grad_weights, axis=-1, keepdims=True)
        grad_scores = (weights * (grad_weights - row_dot)).astype(jnp.bfloat16)
        grad_q = (
            jnp.einsum("hqk,khd->qhd", grad_scores, k_pair, preferred_element_type=jnp.float32)
            * 0.125
        )
        grad_k = (
            jnp.einsum("hqk,qhd->khd", grad_scores, q_pair, preferred_element_type=jnp.float32)
            * 0.125
        )
        grad_v = jnp.einsum(
            "hqk,qhd->khd", weights.astype(jnp.bfloat16), g_pair, preferred_element_type=jnp.float32
        )
        return (grad_q, grad_k, grad_v)

    results = lax.map(
        one_pair,
        (
            head_pairs(queries),
            head_pairs(key_rows),
            head_pairs(val_rows),
            logsum,
            head_pairs(grad_out),
        ),
    )
    return (merge_pairs(results[0]), merge_pairs(results[1]), merge_pairs(results[2]))


def one_hot(ids, count):
    return (ids[:, None] == jnp.arange(count, dtype=jnp.int32)[None, :]).astype(BF)


def split_low(value):
    high = value.astype(BF)
    return (high, (value - high.astype(F32)).astype(BF))


def pick_weights(slot_ids, scores):
    slots = scores.shape[-1]
    count = jnp.sum(
        (slot_ids[..., None] == jnp.arange(slots, dtype=jnp.int32)).astype(F32), axis=2
    )
    named = count > 0.0
    top = jnp.max(jnp.where(named, scores, -jnp.inf), axis=-1, keepdims=True)
    raised = jnp.where(named, count * jnp.exp(scores - top), 0.0)
    return raised / jnp.sum(raised, axis=-1, keepdims=True)


def per_device(
    x_prompt,
    x_cont,
    cot_prompt,
    cot_cont,
    gain_attn,
    gain_mem,
    w_qkv,
    w_attn_out,
    w_mem_query,
    sub_keys,
    w_gate,
    w_mem_out,
    value_rows,
    request,
    slot_prompt,
    slot_cont,
):
    shard_rows, width = value_rows.shape
    owners, capacity = request.shape[2:]
    slots = owners * capacity
    rows = x_prompt.shape[1]
    cols = w_qkv.shape[2]
    asked = lax.all_to_all(request[:, 0], ALL, split_axis=1, concat_axis=1, tiled=True)
    serve_pick = one_hot(asked.transpose(1, 0, 2).reshape(-1), shard_rows)
    served = mm(serve_pick, value_rows).astype(BF).reshape(owners, 2 * capacity, width)
    table = lax.all_to_all(served, ALL, split_axis=0, concat_axis=0, tiled=True)
    table = table.reshape(owners, 2, capacity, width).transpose(1, 0, 2, 3).reshape(2, slots, width)

    qkv_full = lax.all_gather(w_qkv, "fsdp", axis=1, tiled=True)
    attn_out_full = lax.all_gather(w_attn_out, "fsdp", axis=0, tiled=True)
    query_full = lax.all_gather(w_mem_query, "fsdp", axis=0, tiled=True)
    keys_full = lax.all_gather(sub_keys, "fsdp", axis=0, tiled=True)
    gate_full = lax.all_gather(w_gate, "fsdp", axis=0, tiled=True)
    mem_out_full = lax.all_gather(w_mem_out, "fsdp", axis=0, tiled=True)

    x_rows = jnp.concatenate([x_prompt[0], x_cont[0]], axis=0).astype(F32)
    dy_low = jnp.concatenate([cot_prompt[0], cot_cont[0]], axis=0)
    normed, inverse = normalize(x_rows, gain_attn)
    normed = normed.astype(BF)
    queries = mm(normed, qkv_full[0]).astype(BF)
    keys = mm(normed, qkv_full[1]).astype(BF)
    vals = mm(normed, qkv_full[2]).astype(BF)
    all_keys = lax.all_gather(keys[:rows], "fsdp", axis=0, tiled=True)
    all_vals = lax.all_gather(vals[:rows], "fsdp", axis=0, tiled=True)
    start_row = lax.axis_index("fsdp") * rows
    visible_p = jnp.arange(PL)[None, :] <= start_row + jnp.arange(rows)[:, None]
    att_p, logsum_p = attend_forward(queries[:rows], all_keys, all_vals, visible_p)
    key_join = jnp.concatenate([all_keys, keys[rows:]], axis=0)
    val_join = jnp.concatenate([all_vals, vals[rows:]], axis=0)
    visible_c = jnp.concatenate(
        [
            jnp.ones((rows, PL), jnp.bool_),
            jnp.arange(rows)[None, :] <= jnp.arange(rows)[:, None],
        ],
        axis=1,
    )
    att_c, logsum_c = attend_forward(queries[rows:], key_join, val_join, visible_c)
    att = jnp.concatenate([att_p, att_c], axis=0)
    hidden = x_rows + mm(att, attn_out_full)
    normed2, inverse2 = normalize(hidden, gain_mem)
    normed2 = normed2.astype(BF)

    mquery = mm(normed2, query_full).astype(BF)
    gate_pre = mm(normed2, gate_full)
    key_heads = keys_full.reshape(MH, 2, SUB, HALF)
    offsets = jnp.maximum(request[:, 0].reshape(2, slots), 0)
    picked = (jnp.arange(slots, dtype=jnp.int32) // capacity)[None] * shard_rows + offsets
    slot_ids = (slot_prompt[0], slot_cont[0])
    first, second, weights, mixing, memory_out = [], [], [], [], []
    for part in range(2):
        first.append(one_hot(picked[part] // SUB, SUB))
        second.append(one_hot(picked[part] % SUB, SUB))
        section = slice(part * rows, (part + 1) * rows)
        heads = []
        for head in range(MH):
            slot_keys = jnp.concatenate(
                [
                    mm(first[part], key_heads[head, 0]).astype(BF),
                    mm(second[part], key_heads[head, 1]).astype(BF),
                ],
                axis=1,
            )
            span = slice(head * 2 * HALF, (head + 1) * 2 * HALF)
            heads.append(mm_t(mquery[section, span], slot_keys))
        weights.append(pick_weights(slot_ids[part], jnp.stack(heads, axis=1)))
        mixing.append(jnp.sum(weights[part], axis=1).astype(BF))
        memory_out.append(mm(mixing[part], table[part]))
    memory_out = jnp.concatenate(memory_out, axis=0)
    sigmoid_gate = jax.nn.sigmoid(gate_pre)
    blended = (memory_out * (gate_pre * sigmoid_gate)).astype(BF)
    out = (hidden + mm(blended, mem_out_full)).astype(BF)

    grad_blend = mm_t(dy_low, mem_out_full)
    grad_mem_out = mm_l(blended, dy_low)
    grad_memory = (grad_blend * gate_pre * sigmoid_gate).astype(BF)
    grad_gate = (
        grad_blend * memory_out * sigmoid_gate * (1.0 + gate_pre * (1.0 - sigmoid_gate))
    ).astype(BF)
    slot_grads, grad_query, sub_grads = [], [], []
    for part in range(2):
        section = slice(part * rows, (part + 1) * rows)
        slot_grads.append(mm_l(mixing[part], grad_memory[section]).astype(BF))
        grad_mixing = mm_t(grad_memory[section], table[part])[:, None, :]
        pulled = weights[part] * grad_mixing
        grad_scores = pulled - weights[part] * jnp.sum(pulled, axis=-1, keepdims=True)
        high, low = split_low(grad_scores.reshape(rows * MH, slots))
        halves = [
            (mm(high, picker) + mm(low, picker)).astype(BF).reshape(rows, MH, SUB)
            for picker in (first[part], second[part])
        ]
        sub_grads.append(jnp.stack(halves, axis=2))
    sub_grads = jnp.concatenate(sub_grads, axis=0)
    grad_query = jnp.concatenate(
        [
            mm(sub_grads[:, head, half], key_heads[head, half]).astype(BF)
            for head in range(MH)
            for half in range(2)
        ],
        axis=1,
    )
    grad_keys = jnp.concatenate(
        [
            mm_l(
                sub_grads[:, head, half],
                mquery[:, (2 * head + half) * HALF : (2 * head + half + 1) * HALF],
            )
            for head in range(MH)
            for half in range(2)
        ],
        axis=0,
    )
    arrived = lax.all_to_all(
        jnp.stack([piece.reshape(owners, capacity, width) for piece in slot_grads], axis=1),
        ALL,
        split_axis=0,
        concat_axis=0,
        tiled=True,
    )
    grad_rows = mm_l(serve_pick, arrived.reshape(owners * 2 * capacity, width))
    grad_normed2 = mm_t(grad_query, query_full) + mm_t(grad_gate, gate_full)
    grad_query_w = mm_l(normed2, grad_query)
    grad_gate_w = mm_l(normed2, grad_gate)
    back, gain_mem_part = norm_backward(hidden, inverse2, gain_mem, grad_normed2)
    grad_hidden = dy_low.astype(F32) + back
    hidden_low = grad_hidden.astype(BF)
    grad_attn_out = mm_l(att, hidden_low)
    grad_att = mm_t(hidden_low, attn_out_full).astype(BF)
    grad_q_p, grad_k_p, grad_v_p = attend_backward(
        queries[:rows], all_keys, all_vals, visible_p, logsum_p, grad_att[:rows]
    )
    grad_q_c, grad_k_c, grad_v_c = attend_backward(
        queries[rows:], key_join, val_join, visible_c, logsum_c, grad_att[rows:]
    )
    own_keys = lax.psum_scatter(
        (grad_k_c[:PL] + grad_k_p).astype(BF), "fsdp", scatter_dimension=0, tiled=True
    )
    own_vals = lax.psum_scatter(
        (grad_v_c[:PL] + grad_v_p).astype(BF), "fsdp", scatter_dimension=0, tiled=True
    )
    grad_q = jnp.concatenate([grad_q_p, grad_q_c], axis=0).astype(BF)
    grad_k = jnp.concatenate([own_keys, grad_k_c[PL:].astype(BF)], axis=0)
    grad_v = jnp.concatenate([own_vals, grad_v_c[PL:].astype(BF)], axis=0)
    grad_normed = (
        mm_t(grad_q, qkv_full[0]) + mm_t(grad_k, qkv_full[1]) + mm_t(grad_v, qkv_full[2])
    )
    grad_x, gain_attn_part = norm_backward(x_rows, inverse, gain_attn, grad_normed)
    grad_x = grad_hidden + grad_x
    grad_qkv = jnp.stack([mm_l(normed, piece) for piece in (grad_q, grad_k, grad_v)])

    def scatter(value, axis):
        return lax.psum_scatter(value, ALL, scatter_dimension=axis, tiled=True)

    return (
        out[None, :rows],
        out[None, rows:],
        grad_x[None, :rows],
        grad_x[None, rows:],
        scatter(gain_attn_part, 0),
        scatter(gain_mem_part, 0),
        scatter(grad_qkv.astype(BF), 1).astype(F32),
        scatter(grad_attn_out.astype(BF), 0).astype(F32),
        scatter(grad_query_w.astype(BF), 0).astype(F32),
        scatter(grad_keys.astype(BF), 0).astype(F32),
        scatter(grad_gate_w.astype(BF), 0).astype(F32),
        scatter(grad_mem_out.astype(BF), 0).astype(F32),
        grad_rows,
    )


def solution(mesh):
    in_specs = (
        P("dp", "fsdp", None),
        P("dp", "fsdp", None),
        P("dp", "fsdp", None),
        P("dp", "fsdp", None),
        P(),
        P(),
        P(None, "fsdp", None),
        P("fsdp", None),
        P("fsdp", None),
        P("fsdp", None),
        P("fsdp", None),
        P("fsdp", None),
        P(("dp", "fsdp"), None),
        P(None, ("dp", "fsdp"), None, None),
        P("dp", "fsdp", None, None),
        P("dp", "fsdp", None, None),
    )
    out_specs = (
        P("dp", "fsdp", None),
        P("dp", "fsdp", None),
        P("dp", "fsdp", None),
        P("dp", "fsdp", None),
        P(("dp", "fsdp")),
        P(("dp", "fsdp")),
        P(None, ("dp", "fsdp"), None),
        P(("dp", "fsdp"), None),
        P(("dp", "fsdp"), None),
        P(("dp", "fsdp"), None),
        P(("dp", "fsdp"), None),
        P(("dp", "fsdp"), None),
        P(("dp", "fsdp"), None),
    )
    return jax.shard_map(
        per_device, mesh=mesh, in_specs=in_specs, out_specs=out_specs, check_vma=False
    )
```

time: 5530 us -> 1880 us (0.34)
  local copies, waits for them, and re-layouts: 2330 us -> 106 us
  other arithmetic: 1470 us -> 113 us
  waiting for transfers between devices: 1270 us -> 1180 us
    gather x36 -> x0, local copies, waits for them, and re-layouts: 2230 us -> none  [the longest x10 632 us: memory_forward(): jnp.take_along_axis(sub_scores[:, :, 1], second_half, axis=2)]
    unnamed x14 -> x1, other arithmetic: 1360 us -> 0.01 us
    reduce_scatter x8, waiting for transfers between devices: 1080 us -> 789 us  [the longest x6 750 us: scatter(): return lax.psum_scatter(value, ALL, scatter_dimension=axis, tiled=True)]
    all_gather x8, waiting for transfers between devices: 118 us -> 288 us  [the longest x1 118 us: per_device(): qkv_full = lax.all_gather(w_qkv, 'fsdp', axis=1, tiled=True)]
    dot_general x54 -> x77, matrix products: 164 us -> 175 us  [the longest x42 79.5 us: mm(): return jnp.dot(left, right, preferred_element_type=F32)]
  transfers between devices with their start and end apart: 22 -> 19, of which waited for: 10 -> 13; matrix products, arithmetic and copies ran while one was open for 23% -> 18% of each run, Pallas kernels for 0% -> 0%
where the time goes in v1:
time: 1880 us; the launch traced here: 1870 us
  waiting for transfers between devices  1180 us (63%)
  matrix products  395 us (21%)
  other arithmetic  113 us (6%)
  local copies, waits for them, and re-layouts  106 us (6%)
  blocking collectives  43 us (2%)
    reduce_scatter x6, waiting for transfers between devices, scatter(): return lax.psum_scatter(value, ALL, scatter_dimension=axis, tiled=True)  750 us
    all_gather x1, waiting for transfers between devices, per_device(): qkv_full = lax.all_gather(w_qkv, 'fsdp', axis=1, tiled=True)  118 us
    all_gather x1, waiting for transfers between devices, per_device(): query_full = lax.all_gather(w_mem_query, 'fsdp', axis=0, tiled=True)  95.4 us
    dot_general x42, matrix products, mm(): return jnp.dot(left, right, preferred_element_type=F32)  79.5 us
    dot_general x32, matrix products, one_pair(): jnp.einsum('qhd,khd->hqk', q_pair, k_pair, preferred_element_type=jnp.flo...  60.4 us
    dot_general x18, matrix products, mm_l(): lax.dot_general(left, right, (((0,), (0,)), ((), ())), preferred_element_...  59.7 us
    all_to_all x1, waiting for transfers between devices, per_device(): lax.all_to_all(jnp.stack([piece.reshape(owners, capacity, width) for piec...  56.1 us
    unnamed x1, blocking collectives  43 us
  transfers between devices with their start and end apart: 19, of which 13 were waited for; matrix products, arithmetic and copies ran while one was open for 18% of the time, Pallas kernels for 0%

profile of v1, /device:TPU:0, one launch (start us, length us, event | category | flops | bytes accessed | tf_op | source)
XLA Modules:
  0.0 1866.8 jit_solution(4495922373010373773)
XLA Ops:
  9.6 118.1 %all-gather.9.cloned.1.call-done = bf16[3,1024,1024]{2,1,0:T(8,128)(2,1)} async-done(((bf16[3,256,1024]{2,1,0:T(8,128)(2,1)}), bf16[3,1024,1024]{2,1,0:T(8,128)(2,1)}) %all-gather.9.cloned.1.call-update) | async-done | bytes 6291472 | tf_op jit(solution)/shard_map/all_gather | solution.py:165
  142.3 17.4 convert_reduce_fusion
  160.0 18.7 %convert_reduce_fusion.1 = f32[256,4,512]{2,1,0:T(4,128)} fusion(s32[256,4,32]{2,1,0:T(4,128)S(1)} %copy.103), kind=kLoop, calls=%fused_computation.116 | loop fusion | flops 49807360 | bytes 2228224 | tf_op jit(solution)/shard_map/reduce_sum | solution.py:127
  178.8 8.1 fusion.106
  187.0 6.0 all-to-all-start.1
  221.5 41.9 %all-to-all-done.1 = bf16[32,32,1024]{2,1,0:T(8,128)(2,1)} async-done(((bf16[32,32,1024]{2,1,0:T(8,128)(2,1)}), bf16[32,32,1024]{2,1,0:T(8,128)(2,1)}, u32[]{:S(2)}, u32[]{:S(2)}) %all-to-all-start.1) | async-done | bytes 2097184 | tf_op jit(solution)/shard_map/all_to_all | solution.py:162
  282.2 18.7 %all-gather.11.cloned.1.call-done = bf16[1024,1024]{1,0:T(8,128)(2,1)} async-done(((bf16[256,1024]{1,0:T(8,128)(2,1)}), bf16[1024,1024]{1,0:T(8,128)(2,1)}) %all-gather.11.cloned.1.call-update) | async-done | bytes 2097168 | tf_op jit(solution)/shard_map/all_gather | solution.py:180
  309.7 37.6 %while.54 = (s32[]{:T(128)}, bf16[8,256,2,64]{1,3,2,0:T(8,128)(2,1)}, f32[8,2,256]{2,1,0:T(2,128)S(1)}, bf16[8,1280,2,64]{1,3,2,0:T(8,128)(2,1)}, pred[256,1280]...) while((s32[]{:T(128)}, ...), condition=%wide.region_8.9_spmd, body=%wide.region_5.8_spmd.sunk | while | flops 173047296 | bytes 8996953 | solution.py:70
  356.1 39.2 %while.56 = (s32[]{:T(128)}, bf16[8,256,2,64]{1,3,2,0:T(8,128)(2,1)}, f32[8,2,256]{2,1,0:T(2,128)S(1)}, bf16[8,1024,2,64]{1,3,2,0:T(8,128)(2,1)}, bf16[8,256,2,6...) while((s32[]{:T(128)}, ...), condition=%wide.region_4.5_spmd.clone, body=%wide.region_1.4_spmd.clone.sunk | while | flops 140803584 | bytes 8014937 | solution.py:70
  401.5 95.4 %all-gather.17.cloned.1.call-done = bf16[1024,4096]{1,0:T(8,128)(2,1)} async-done(((bf16[256,4096]{1,0:T(8,128)(2,1)}), bf16[1024,4096]{1,0:T(8,128)(2,1)}) %all-gather.17.cloned.1.call-update) | async-done | bytes 8388624 | tf_op jit(solution)/shard_map/all_gather | solution.py:167
  496.8 8.3 convolution_convert_fusion.2
  528.7 13.9 all-gather.21.cloned.1.call-done
  547.1 41.7 %all-gather.23.cloned.1.call-done = bf16[1024,1024]{1,0:T(8,128)(2,1)} async-done(((bf16[256,1024]{1,0:T(8,128)(2,1)}), bf16[1024,1024]{1,0:T(8,128)(2,1)}) %all-gather.23.cloned.1.call-update) | async-done | bytes 2097168 | tf_op jit(solution)/shard_map/all_gather | solution.py:170
  588.9 5.0 multiply_convert_fusion.3
  675.7 4.7 fusion.265
  689.2 79.1 %while.57 = (s32[]{:T(128)}, bf16[8,256,2,64]{1,3,2,0:T(8,128)(2,1)}, f32[8,1024,2,64]{1,3,2,0:T(8,128)}, f32[8,1024,2,64]{1,3,2,0:T(8,128)}, bf16[8,1024,2,64]{...) while((s32[]{:T(128)}, ...), condition=%wide.region_23.24_spmd.clone, body=%wide.region_21.23_spmd.clone.sunk | while | flops 340688384 | bytes 18497648 | solution.py:103
  771.1 81.6 %while.55 = (s32[]{:T(128)}, bf16[8,256,2,64]{1,3,2,0:T(8,128)(2,1)}, f32[8,1280,2,64]{1,3,2,0:T(8,128)}, f32[8,1280,2,64]{1,3,2,0:T(8,128)}, bf16[8,1280,2,64]{...) while((s32[]{:T(128)}, ...), condition=%wide.region_26.27_spmd, body=%wide.region_24.26_spmd.sunk | while | flops 425524736 | bytes 22690928 | solution.py:103
  852.8 5.5 fusion.94
  858.3 5.5 fusion.93
  881.1 4.5 convolution_convert_fusion.5
  907.2 39.3 %reduce-scatter.11.cloned.1.call-done = bf16[256,1024]{0,1:T(8,128)(2,1)} async-done(((bf16[1024,1024]{0,1:T(8,128)(2,1)}), bf16[256,1024]{0,1:T(8,128)(2,1)}) %reduce-scatter.11.cloned.1.call-update) | async-done | bytes 524304 | tf_op jit(solution)/shard_map/reduce_scatter | solution.py:293
  953.8 9.1 convolution_convert_fusion.1
  975.5 4.6 fusion.109
  980.1 56.1 %all-to-all-done.2 = bf16[32,2,16,1024]{3,2,1,0:T(8,128)(2,1)} async-done(((bf16[32,2,16,1024]{3,2,1,0:T(8,128)(2,1)}), bf16[32,2,16,1024]{3,2,1,0:T(8,128)(2,1)}, u32[]{:S(2)}, u32[]{:S(2)}) %all-to-all-start.2) | async-done | bytes 2097184 | tf_op jit(solution)/shard_map/all_to_all | solution.py:268
  1036.1 8.6 fusion.91
  1048.0 4.9 fusion.105
  1052.9 43.0 %all-reduce.3 = (f32[1024]{0:T(1024)S(1)}, f32[1024]{0:T(1024)S(1)}) all-reduce(f32[1024]{0:T(1024)S(1)} %get-tuple-element.249, f32[1024]{0:T(1024)S(1)} %get-tuple-element.247), channel_id=4, replica_groups=mesh['dp'=8,'fsdp'=4] {'dp','fsdp'}, use_global_device_ids=true, to_apply=%region_31.32.clone | all-reduce | flops 2048 | bytes 16384
  1098.5 137.2 %reduce-scatter.15.cloned.1.call-done = bf16[32,1024]{1,0:T(8,128)(2,1)} async-done(((bf16[1024,1024]{1,0:T(8,128)(2,1)}), bf16[32,1024]{1,0:T(8,128)(2,1)}) %reduce-scatter.15.cloned.1.call-update) | async-done | bytes 65552 | tf_op jit(solution)/shard_map/reduce_scatter | solution.py:307
  1237.2 136.9 %reduce-scatter.21.cloned.1.call-done = bf16[32,1024]{1,0:T(8,128)(2,1)} async-done(((bf16[1024,1024]{1,0:T(8,128)(2,1)}), bf16[32,1024]{1,0:T(8,128)(2,1)}) %reduce-scatter.21.cloned.1.call-update) | async-done | bytes 65552 | tf_op jit(solution)/shard_map/reduce_scatter | solution.py:307
  1375.7 137.0 %reduce-scatter.23.cloned.1.call-done = bf16[32,1024]{1,0:T(8,128)(2,1)} async-done(((bf16[1024,1024]{1,0:T(8,128)(2,1)}), bf16[32,1024]{1,0:T(8,128)(2,1)}) %reduce-scatter.23.cloned.1.call-update) | async-done | bytes 65552 | tf_op jit(solution)/shard_map/reduce_scatter | solution.py:307
  1517.8 154.1 %reduce-scatter.13.cloned.1.call-done = bf16[3,32,1024]{2,1,0:T(8,128)(2,1)} async-done(((bf16[3,1024,1024]{2,1,0:T(8,128)(2,1)}), bf16[3,32,1024]{2,1,0:T(8,128)(2,1)}) %reduce-scatter.13.cloned.1.call-update) | async-done | bytes 196624 | tf_op jit(solution)/shard_map/reduce_scatter | solution.py:307
  1673.5 184.5 %reduce-scatter.17.cloned.1.call-done = bf16[32,4096]{1,0:T(8,128)(2,1)} async-done(((bf16[1024,4096]{1,0:T(8,128)(2,1)}), bf16[32,4096]{1,0:T(8,128)(2,1)}) %reduce-scatter.17.cloned.1.call-update) | async-done | bytes 262160 | tf_op jit(solution)/shard_map/reduce_scatter | solution.py:307
  (582 shorter events, 521.8 us)
Async XLA Ops:
  7.2 120.5 %copy-start.78 = (f32[1024]{0:T(1024)S(1)}, f32[1024]{0:T(1024)}, u32[]{:S(2)}) copy-start(f32[1024]{0:T(1024)} %param.28) | copy-start | bytes 12292
  7.2 120.5 %all-gather.9.cloned.1.call-start = ((), (), s32[]{:S(2)}) async-start(), calls=%async_computation.11 | async-start | bytes 7864320 | tf_op jit(solution)/shard_map/all_gather | solution.py:165
  7.9 190.4 %all-gather.19.cloned.1.call-start = ((), (), s32[]{:S(2)}) async-start(), calls=%async_computation.16 | async-start | bytes 2621440 | tf_op jit(solution)/shard_map/all_gather | solution.py:168
  8.7 265.6 %all-gather.13.cloned.1.call-start = ((), (), s32[]{:S(2)}) async-start(), calls=%async_computation.13 | async-start | bytes 2621440 | tf_op jit(solution)/shard_map/all_gather | solution.py:179
  9.6 256.6 %copy-start.75 = (f32[512]{0:T(512)}, f32[512]{0:T(512)S(1)}, u32[]{:S(2)}) copy-start(f32[512]{0:T(512)S(1)} %get-tuple-element.360) | copy-start | bytes 6148
  131.7 169.2 %all-gather.11.cloned.1.call-start = ((), (), s32[]{:S(2)}) async-start(), calls=%async_computation.12 | async-start | bytes 2621440 | tf_op jit(solution)/shard_map/all_gather | solution.py:180
  135.7 259.7 %all-gather.15.cloned.1.call-start = ((), (), s32[]{:S(2)}) async-start(), calls=%async_computation.14 | async-start | bytes 2621440 | tf_op jit(solution)/shard_map/all_gather | solution.py:166
  136.3 360.5 %all-gather.17.cloned.1.call-start = ((), (), s32[]{:S(2)}) async-start(), calls=%async_computation.15 | async-start | bytes 10485760 | tf_op jit(solution)/shard_map/all_gather | solution.py:167
  136.9 405.7 %all-gather.21.cloned.1.call-start = ((), (), s32[]{:S(2)}) async-start(), calls=%async_computation.17 | async-start | bytes 2621440 | tf_op jit(solution)/shard_map/all_gather | solution.py:169
  137.6 22.1 %copy-start.71 = (s32[1,256,4,32]{1,3,2,0:T(8,128)S(1)}, s32[1,256,4,32]{1,3,2,0:T(8,128)}, u32[]{:S(2)}) copy-start(s32[1,256,4,32]{1,3,2,0:T(8,128)} %param.38) | copy-start | bytes 393220
  138.3 40.4 %all-to-all-start = ((s32[2,32,16]{2,0,1:T(2,128)}), s32[2,32,16]{2,0,1:T(2,128)S(1)}, u32[]{:S(2)}, u32[]{:S(2)}) async-start(s32[2,32,16]{2,0,1:T(2,128)} %bitcast.53), calls=%async_computation | async-start | bytes 65536 | tf_op jit(solution)/shard_map/all_to_all | solution.py:159
  141.1 447.7 %all-gather.23.cloned.1.call-start = ((), (), s32[]{:S(2)}) async-start(), calls=%async_computation.18 | async-start | bytes 2621440 | tf_op jit(solution)/shard_map/all_gather | solution.py:170
  187.0 76.3 %all-to-all-start.1 = ((bf16[32,32,1024]{2,1,0:T(8,128)(2,1)}), bf16[32,32,1024]{2,1,0:T(8,128)(2,1)}, u32[]{:S(2)}, u32[]{:S(2)}) async-start(bf16[32,32,1024]{2,1,0:T(8,128)(2,1)} %bitcast.492), calls=%async_computation.1 | async-start | bytes 4194304 | tf_op jit(solution)/shard_map/all_to_all | solution.py:162
  192.9 710.3 %reduce-scatter.9.cloned.1.call-start = ((), (), s32[]{:S(2)}) async-start(), calls=%async_computation.19 | async-start | bytes 2621440 | tf_op jit(solution)/shard_map/reduce_scatter | solution.py:290
  496.8 8.3 copy-start.64
  496.8 8.3 copy-start.66
  528.6 60.2 %copy-start.49 = (bf16[1,256,1024]{2,1,0:T(8,128)(2,1)S(1)}, bf16[1,256,1024]{2,1,0:T(8,128)(2,1)}, u32[]{:S(2)}) copy-start(bf16[1,256,1024]{2,1,0:T(8,128)(2,1)} %param.27) | copy-start | bytes 1572868
  528.6 60.2 %copy-start.51 = (bf16[1,256,1024]{2,1,0:T(8,128)(2,1)S(1)}, bf16[1,256,1024]{2,1,0:T(8,128)(2,1)}, u32[]{:S(2)}) copy-start(bf16[1,256,1024]{2,1,0:T(8,128)(2,1)} %param.26) | copy-start | bytes 1572868
  666.9 8.8 slice-start
  858.3 88.2 %reduce-scatter.11.cloned.1.call-start = ((), (), s32[]{:S(2)}) async-start(), calls=%async_computation.20 | async-start | bytes 2621440 | tf_op jit(solution)/shard_map/reduce_scatter | solution.py:293
  863.9 233.2 %reduce-scatter.19.cloned.1.call-start = ((), (), s32[]{:S(2)}) async-start(), calls=%async_computation.24 | async-start | bytes 2162688 | tf_op jit(solution)/shard_map/reduce_scatter | solution.py:307
  881.0 354.7 %reduce-scatter.15.cloned.1.call-start = ((), (), s32[]{:S(2)}) async-start(), calls=%async_computation.22 | async-start | bytes 2162688 | tf_op jit(solution)/shard_map/reduce_scatter | solution.py:307
  885.6 488.5 %reduce-scatter.21.cloned.1.call-start = ((), (), s32[]{:S(2)}) async-start(), calls=%async_computation.25 | async-start | bytes 2162688 | tf_op jit(solution)/shard_map/reduce_scatter | solution.py:307
  889.6 623.1 %reduce-scatter.23.cloned.1.call-start = ((), (), s32[]{:S(2)}) async-start(), calls=%async_computation.26 | async-start | bytes 2162688 | tf_op jit(solution)/shard_map/reduce_scatter | solution.py:307
  894.7 777.1 %reduce-scatter.13.cloned.1.call-start = ((), (), s32[]{:S(2)}) async-start(), calls=%async_computation.21 | async-start | bytes 6488064 | tf_op jit(solution)/shard_map/reduce_scatter | solution.py:307
  952.6 905.5 %reduce-scatter.17.cloned.1.call-start = ((), (), s32[]{:S(2)}) async-start(), calls=%async_computation.23 | async-start | bytes 8650752 | tf_op jit(solution)/shard_map/reduce_scatter | solution.py:307
  967.5 68.6 %all-to-all-start.2 = ((bf16[32,2,16,1024]{3,2,1,0:T(8,128)(2,1)}), bf16[32,2,16,1024]{3,2,1,0:T(8,128)(2,1)}, u32[]{:S(2)}, u32[]{:S(2)}) async-start(bf16[32,2,16,1024]{3,2,1,0:T(8,128)(2,1)} %pad_maximum_fusion.6), calls=%async_computation.10 | async-start | bytes 4194304 | tf_op jit(solution)/shard_map/all_to_all | solution.py:268
  975.5 60.7 %copy-start.81 = (s32[1024]{0:T(1024)S(1)}, s32[1024]{0:T(1024)}, u32[]{:S(2)}) copy-start(s32[1024]{0:T(1024)} %copy-done.80) | copy-start | bytes 12292
  1036.1 8.6 copy-start.68
  1036.1 8.6 copy-start.84
  1047.9 466.2 %copy-start.11 = (f32[512,1024]{1,0:T(8,128)S(1)}, f32[512,1024]{1,0:T(8,128)}, u32[]{:S(2)}) copy-start(f32[512,1024]{1,0:T(8,128)} %copy-done.10) | copy-start | bytes 6291460
  1047.9 466.2 %copy-start.74 = (f32[512]{0:T(512)S(1)}, f32[512]{0:T(512)}, u32[]{:S(2)}) copy-start(f32[512]{0:T(512)} %get-tuple-element.359) | copy-start | bytes 6148
  (77 other events, 217.2 us)
Sparse Core Ops, SparseCore 0:
  9.6 118.0 all-gather.8
  129.3 44.7 all-gather.18
  175.7 78.9 all-gather.12
  256.7 44.1 all-gather.10
  302.3 44.6 all-gather.14
  348.4 148.3 all-gather.16
  498.4 44.1 all-gather.20
  544.2 44.6 all-gather.22
  858.4 42.5 reduce-scatter.8
  903.2 43.1 reduce-scatter.10
  948.7 145.4 reduce-scatter.18
  1096.4 139.2 reduce-scatter.14
  1238.0 136.1 reduce-scatter.20
  1376.4 136.2 reduce-scatter.22
  1514.8 156.9 reduce-scatter.12
  1674.0 184.0 reduce-scatter.16

commit v2 on v1

--- a/solution.py
+++ b/solution.py
@@ -1,8 +1,17 @@
+import functools
 import jax
 import jax.numpy as jnp
 from jax import lax
+from jax.experimental import pallas as pl
+from jax.experimental.pallas import tpu as pltpu
 from jax.sharding import PartitionSpec as P
-
+BF = jnp.bfloat16
+F32 = jnp.float32
+ALL = ("dp", "fsdp")
+MESH = pl.DeviceIdType.MESH
+LAG = 2
+GATHER_LAG = 2
+PIECE = 1024
 HEADS = 16
 HDIM = 64
 MH = 4
@@ -11,11 +20,6 @@
 PL = 1024
 
 
-BF = jnp.bfloat16
-F32 = jnp.float32
-ALL = ("dp", "fsdp")
-
-
 def mm(left, right):
     return jnp.dot(left, right, preferred_element_type=F32)
 
@@ -40,6 +44,464 @@
         matrix * scaled, axis=-1, keepdims=True
     )
     return (grad_matrix, jnp.sum(grad_normed * matrix * inverse, axis=0))
+
+
+def grid_of(plane, depth):
+    side = 1
+    while 2 * side * side < plane:
+        side += 1
+    return side, depth
+
+
+def place(side):
+    dp = lax.axis_index("dp")
+    return (dp // (2 * side), (dp // 2) % side, dp % 2, lax.axis_index("fsdp"))
+
+
+def device_at(side, y, x, core, z):
+    return ((y * side + x) * 2 + core, z)
+
+
+def greet(side, depth):
+    y, x, core, z = place(side)
+    barrier = pltpu.get_barrier_semaphore()
+    peers = [device_at(side, y, x, 1 - core, z)]
+    for hop in range(1, side):
+        peers.append(device_at(side, y, (x + hop) % side, core, z))
+        peers.append(device_at(side, (y + hop) % side, x, core, z))
+    for hop in range(1, depth):
+        peers.append(device_at(side, y, x, core, (z + hop) % depth))
+    for peer in peers:
+        pl.semaphore_signal(barrier, inc=1, device_id=peer, device_id_type=MESH)
+    pl.semaphore_wait(barrier, len(peers))
+
+
+def remote(source, target, send_sem, recv_sem, peer):
+    return pltpu.make_async_remote_copy(
+        src_ref=source,
+        dst_ref=target,
+        send_sem=send_sem,
+        recv_sem=recv_sem,
+        device_id=peer,
+        device_id_type=MESH,
+    )
+
+
+def reduce_kernel(side, depth, layout, *refs):
+    count = sum(len(columns) for columns in layout)
+    n_in = len(layout)
+    sources = refs[:n_in]
+    gains = refs[n_in]
+    outs = refs[n_in + 1 : 2 * n_in + 1]
+    gains_out = refs[2 * n_in + 1]
+    (mine, got_core, got_one, got_two, got_deep, total, gain_sum, gain_got, local_sem, core_send,
+     core_recv, one_send, one_recv, two_send, two_recv, deep_send, deep_recv, gain_send,
+     gain_recv) = refs[2 * n_in + 2 :]
+    y, x, core, z = place(side)
+    block = total.shape[1:]
+    pieces = []
+    for number, columns in enumerate(layout):
+        for lead, start in columns:
+            def cut(half, number=number, lead=lead, start=start):
+                ref = sources[number] if lead is None else sources[number].at[lead]
+                return ref.at[:, :, half, :, :, pl.ds(start, block[1])]
+            pieces.append((cut, number, lead, start))
+    greet(side, depth)
+    partner = device_at(side, y, x, 1 - core, z)
+    for k, piece in enumerate(pieces):
+        remote(piece[0](1 - core), got_core.at[k], core_send.at[k], core_recv.at[k], partner).start()
+        pltpu.make_async_copy(piece[0](core), mine.at[k], local_sem.at[k]).start()
+
+    def one_copy(k, hop, x_first):
+        peer = device_at(side, y, (x + hop) % side, core, z) if x_first else device_at(
+            side, (y + hop) % side, x, core, z)
+        source = mine.at[k, :, (x + hop) % side] if x_first else mine.at[k, (y + hop) % side]
+        return remote(source, got_one.at[k, hop - 1], one_send.at[k, hop - 1],
+                      one_recv.at[k, hop - 1], peer)
+
+    def two_copy(k, hop, x_first):
+        peer = device_at(side, (y + hop) % side, x, core, z) if x_first else device_at(
+            side, y, (x + hop) % side, core, z)
+        source = mine.at[k, (y + hop) % side, x] if x_first else mine.at[k, y, (x + hop) % side]
+        return remote(source, got_two.at[k, hop - 1], two_send.at[k, hop - 1],
+                      two_recv.at[k, hop - 1], peer)
+
+    def deep_copy(k, hop):
+        there = (z + hop) % depth
+        return remote(mine.at[k, y, x, there], got_deep.at[k, hop - 1], deep_send.at[k, hop - 1],
+                      deep_recv.at[k, hop - 1], device_at(side, y, x, core, there))
+
+    def both_orders(k, action):
+        @pl.when(k % 2 == 0)
+        def _():
+            action(True)
+
+        @pl.when(k % 2 == 1)
+        def _():
+            action(False)
+
+    def added(base, others):
+        if len(others) == 1:
+            return base + others[0]
+        value = base.astype(F32)
+        for other in others:
+            value = value + other.astype(F32)
+        return value.astype(base.dtype)
+
+    def after_core(k):
+        remote(got_core.at[k], got_core.at[k], core_send.at[k], core_recv.at[k], partner).wait_recv()
+        pltpu.make_async_copy(got_core.at[k], mine.at[k], local_sem.at[k]).wait()
+
+        def add(index, carry):
+            a, b, c = index // (side * depth), (index // depth) % side, index % depth
+            mine[k, a, b, c] = mine[k, a, b, c] + got_core[k, a, b, c]
+            return carry
+
+        lax.fori_loop(0, side * side * depth, add, 0)
+
+        def send(x_first):
+            for hop in range(1, side):
+                one_copy(k, hop, x_first).start()
+
+        both_orders(k, send)
+
+    def after_one(k):
+        def finish(x_first):
+            for hop in range(1, side):
+                one_copy(k, hop, x_first).wait_recv()
+
+            def add(index, carry):
+                a, c = index // depth, index % depth
+                spot = (k, a, x, c) if x_first else (k, y, a, c)
+                mine[spot] = added(mine[spot], [got_one[k, hop, a, c] for hop in range(side - 1)])
+                return carry
+
+            lax.fori_loop(0, side * depth, add, 0)
+            for hop in range(1, side):
+                two_copy(k, hop, x_first).start()
+
+        both_orders(k, finish)
+
+    def after_two(k):
+        def finish(x_first):
+            for hop in range(1, side):
+                two_copy(k, hop, x_first).wait_recv()
+
+        both_orders(k, finish)
+
+        def add(c, carry):
+            mine[k, y, x, c] = added(mine[k, y, x, c], [got_two[k, hop, c] for hop in range(side - 1)])
+            return carry
+
+        lax.fori_loop(0, depth, add, 0)
+        for hop in range(1, depth):
+            deep_copy(k, hop).start()
+
+    def after_deep(k):
+        for hop in range(1, depth):
+            deep_copy(k, hop).wait_recv()
+        value = mine[k, y, x, z].astype(F32)
+        for hop in range(depth - 1):
+            value = value + got_deep[k, hop].astype(F32)
+        total[k] = value
+
+    gain_peers = [
+        [partner],
+        [device_at(side, y, (x + hop) % side, core, z) for hop in range(1, side)],
+        [device_at(side, (y + hop) % side, x, core, z) for hop in range(1, side)],
+        [device_at(side, y, x, core, (z + hop) % depth) for hop in range(1, depth)],
+    ]
+
+    def gain_copy(stage, number):
+        source = gains if stage == 0 else gain_sum.at[stage - 1]
+        return remote(source, gain_got.at[stage, number], gain_send.at[stage, number],
+                      gain_recv.at[stage, number], gain_peers[stage][number])
+
+    for number in range(len(gain_peers[0])):
+        gain_copy(0, number).start()
+
+    def run(i, carry):
+        for lag, action in ((0, after_core), (LAG, after_one), (2 * LAG, after_two), (3 * LAG, after_deep)):
+            @pl.when(jnp.logical_and(i >= lag, i < count + lag))
+            def _(lag=lag, action=action):
+                action(i - lag)
+
+        for stage in range(4):
+            @pl.when(i == stage + 1)
+            def _(stage=stage):
+                value = gains[...] if stage == 0 else gain_sum[stage - 1]
+                for number in range(len(gain_peers[stage])):
+                    gain_copy(stage, number).wait_recv()
+                    value = value + gain_got[stage, number]
+                gain_sum[stage] = value
+                if stage < 3:
+                    for number in range(len(gain_peers[stage + 1])):
+                        gain_copy(stage + 1, number).start()
+
+        return carry
+
+    lax.fori_loop(0, count + 3 * LAG, run, 0)
+    gains_out[...] = gain_sum[3]
+    for k, (cut, number, lead, start) in enumerate(pieces):
+        spot = (slice(None), pl.ds(start, block[1]))
+        if lead is None:
+            outs[number][spot] = total[k]
+        else:
+            outs[number][(lead,) + spot] = total[k]
+
+    def drain(k, carry):
+        remote(got_core.at[k], got_core.at[k], core_send.at[k], core_recv.at[k], partner).wait_send()
+
+        def finish(x_first):
+            for hop in range(1, side):
+                one_copy(k, hop, x_first).wait_send()
+                two_copy(k, hop, x_first).wait_send()
+
+        both_orders(k, finish)
+        for hop in range(1, depth):
+            deep_copy(k, hop).wait_send()
+        return carry
+
+    lax.fori_loop(0, count, drain, 0)
+    for stage in range(4):
+        for number in range(len(gain_peers[stage])):
+            gain_copy(stage, number).wait_send()
+
+
+def reduce_grads(side, depth, grads, gains, call_id):
+    devices = 2 * side * side * depth
+    layout, views, outs = [], [], []
+    width = 1024
+    for grad in grads:
+        rows, cols = grad.shape[-2:]
+        block = rows // devices
+        lead = grad.shape[:-2]
+        views.append(grad.reshape(lead + (side, side, 2, depth, block, cols)))
+        leads = range(lead[0]) if lead else (None,)
+        layout.append([(number, start) for number in leads for start in range(0, cols, width)])
+        outs.append(jax.ShapeDtypeStruct(lead + (block, cols), F32))
+    count = sum(len(columns) for columns in layout)
+    most = max(side, depth) - 1
+    dma = pltpu.SemaphoreType.DMA
+    return pl.pallas_call(
+        functools.partial(reduce_kernel, side, depth, layout),
+        out_shape=tuple(outs) + (jax.ShapeDtypeStruct(gains.shape, F32),),
+        in_specs=[pl.BlockSpec(memory_space=pl.ANY)] * len(views)
+        + [pl.BlockSpec(memory_space=pltpu.VMEM)],
+        out_specs=(pl.BlockSpec(memory_space=pltpu.VMEM),) * (len(views) + 1),
+        scratch_shapes=[
+            pltpu.VMEM((count, side, side, depth, block, width), BF),
+            pltpu.VMEM((count, side, side, depth, block, width), BF),
+            pltpu.VMEM((count, side - 1, side, depth, block, width), BF),
+            pltpu.VMEM((count, side - 1, depth, block, width), BF),
+            pltpu.VMEM((count, depth - 1, block, width), BF),
+            pltpu.VMEM((count, block, width), F32),
+            pltpu.VMEM((4,) + gains.shape, F32),
+            pltpu.VMEM((4, most) + gains.shape, F32),
+            dma((count,)),
+            dma((count,)),
+            dma((count,)),
+            dma((count, side - 1)),
+            dma((count, side - 1)),
+            dma((count, side - 1)),
+            dma((count, side - 1)),
+            dma((count, depth - 1)),
+            dma((count, depth - 1)),
+            dma((4, most)),
+            dma((4, most)),
+        ],
+        compiler_params=pltpu.CompilerParams(
+            collective_id=call_id, has_side_effects=True, vmem_limit_bytes=60 * 1024 * 1024
+        ),
+    )(*views, gains)
+
+
+def gather_kernel(side, depth, layout, *refs):
+    n_in = len(layout)
+    sources, outs = refs[:n_in], refs[n_in : 2 * n_in]
+    held = refs[2 * n_in : 3 * n_in]
+    (in_sem, out_sem, right_send, left_send, deep_recv, one_send, one_recv, two_send, two_recv,
+     core_send, core_recv) = refs[3 * n_in :]
+    y, x, core, z = place(side)
+    pieces = []
+    for number, columns in enumerate(layout):
+        for place_in, (lead, start) in enumerate(columns):
+            width = held[number].shape[-1]
+            width = width if sources[number].shape[-1] > width else None
+            pieces.append((number, lead, start, width, place_in))
+    count = len(pieces)
+
+    def cut(refs, k, *spot):
+        number, lead, start, width = pieces[k][:4]
+        ref = refs[number] if lead is None else refs[number].at[lead]
+        ref = ref.at[spot] if spot else ref
+        if width is None:
+            return ref
+        return ref.at[(slice(None),) * (len(ref.shape) - 1) + (pl.ds(start, width),)]
+
+    greet(side, depth)
+    partner = device_at(side, y, x, 1 - core, z)
+
+    def to_right(k, zp):
+        return remote(cut(outs, k, zp, y, x, core), cut(outs, k, zp, y, x, core),
+                      right_send.at[k, zp], deep_recv.at[k, zp],
+                      device_at(side, y, x, core, z + 1))
+
+    def to_left(k, zp):
+        return remote(cut(outs, k, zp, y, x, core), cut(outs, k, zp, y, x, core),
+                      left_send.at[k, zp], deep_recv.at[k, zp],
+                      device_at(side, y, x, core, z - 1))
+
+    def one_copy(k, zp, hop):
+        x_first = k % 2 == 0
+        peer = device_at(side, y, (x + hop) % side, core, z) if x_first else device_at(
+            side, (y + hop) % side, x, core, z)
+        ref = cut(outs, k, zp, y, x, core)
+        return remote(ref, ref, one_send.at[k, zp, hop - 1], one_recv.at[k, zp, hop - 1], peer)
+
+    def two_copy(k, zp, hop):
+        x_first = k % 2 == 0
+        peer = device_at(side, (y + hop) % side, x, core, z) if x_first else device_at(
+            side, y, (x + hop) % side, core, z)
+        ref = (cut(outs, k, zp, y, slice(None), core) if x_first
+               else cut(outs, k, zp, slice(None), x, core))
+        return remote(ref, ref, two_send.at[k, zp, hop - 1], two_recv.at[k, zp, hop - 1], peer)
+
+    def core_copy(k, zp):
+        ref = cut(outs, k, zp, slice(None), slice(None), core)
+        return remote(ref, ref, core_send.at[k, zp], core_recv.at[k, zp], partner)
+
+    def holder(k):
+        return held[pieces[k][0]].at[pieces[k][4]]
+
+    def take(k):
+        return pltpu.make_async_copy(cut(sources, k), holder(k), in_sem.at[k])
+
+    def put(k):
+        return pltpu.make_async_copy(holder(k), cut(outs, k, z), out_sem.at[k])
+
+    for k in range(count):
+        take(k).start()
+
+        @pl.when(z < depth - 1)
+        def _():
+            remote(cut(sources, k, y, x, core), cut(outs, k, z, y, x, core), right_send.at[k, z],
+                   deep_recv.at[k, z], device_at(side, y, x, core, z + 1)).start()
+
+        @pl.when(z > 0)
+        def _():
+            remote(cut(sources, k, y, x, core), cut(outs, k, z, y, x, core), left_send.at[k, z],
+                   deep_recv.at[k, z], device_at(side, y, x, core, z - 1)).start()
+
+    def arrivals(first):
+        for distance in range(1, depth):
+            for sign in (1, -1):
+                yield first + distance - 1, sign, distance
+
+    for i in range(count + depth - 2 + 3 * GATHER_LAG):
+        if i < count:
+            take(i).wait()
+            put(i).start()
+        for stage in range(4):
+            for lag, sign, distance in arrivals(stage * GATHER_LAG):
+                k = i - lag
+                if not 0 <= k < count:
+                    continue
+                zp = z + sign * distance
+
+                @pl.when(jnp.logical_and(zp >= 0, zp < depth))
+                def _(k=k, zp=zp, sign=sign, stage=stage):
+                    if stage == 0:
+                        to_right(k, zp).wait_recv()
+                        if sign < 0:
+                            @pl.when(z < depth - 1)
+                            def _():
+                                to_right(k, zp).start()
+                        else:
+                            @pl.when(z > 0)
+                            def _():
+                                to_left(k, zp).start()
+                        for hop in range(1, side):
+                            one_copy(k, zp, hop).start()
+                    elif stage == 1:
+                        for hop in range(1, side):
+                            one_copy(k, zp, hop).wait_recv()
+                        for hop in range(1, side):
+                            two_copy(k, zp, hop).start()
+                    elif stage == 2:
+                        for hop in range(1, side):
+                            two_copy(k, zp, hop).wait_recv()
+                        core_copy(k, zp).start()
+                    else:
+                        core_copy(k, zp).wait_recv()
+
+    for k in range(count):
+        put(k).wait()
+
+        @pl.when(z < depth - 1)
+        def _(k=k):
+            to_right(k, z).wait_send()
+
+        @pl.when(z > 0)
+        def _(k=k):
+            to_left(k, z).wait_send()
+
+        for zp in range(depth):
+            @pl.when(zp != z)
+            def _(k=k, zp=zp):
+                @pl.when(jnp.logical_and(zp < z, z < depth - 1))
+                def _():
+                    to_right(k, zp).wait_send()
+
+                @pl.when(jnp.logical_and(zp > z, z > 0))
+                def _():
+                    to_left(k, zp).wait_send()
+
+                for hop in range(1, side):
+                    one_copy(k, zp, hop).wait_send()
+                    two_copy(k, zp, hop).wait_send()
+                core_copy(k, zp).wait_send()
+
+
+def gather_weights(side, depth, shards, call_id):
+    plane = 2 * side * side
+    layout, views, outs, shapes, held = [], [], [], [], []
+    for shard in shards:
+        rows, cols = shard.shape[-2:]
+        block, width = rows // plane, min(cols, PIECE)
+        lead = shard.shape[:-2]
+        views.append(shard.reshape(lead + (side, side, 2, block, cols)))
+        leads = range(lead[0]) if lead else (None,)
+        layout.append([(number, start) for number in leads for start in range(0, cols, width)])
+        outs.append(jax.ShapeDtypeStruct(lead + (depth, side, side, 2, block, cols), BF))
+        shapes.append(lead + (depth * rows, cols))
+        held.append(pltpu.VMEM((len(layout[-1]), side, side, 2, block, width), BF))
+    count = sum(len(columns) for columns in layout)
+    dma = pltpu.SemaphoreType.DMA
+    full = pl.pallas_call(
+        functools.partial(gather_kernel, side, depth, layout),
+        out_shape=tuple(outs),
+        in_specs=[pl.BlockSpec(memory_space=pl.ANY)] * len(views),
+        out_specs=(pl.BlockSpec(memory_space=pl.ANY),) * len(views),
+        scratch_shapes=held
+        + [
+            dma((count,)),
+            dma((count,)),
+            dma((count, depth)),
+            dma((count, depth)),
+            dma((count, depth)),
+            dma((count, depth, side - 1)),
+            dma((count, depth, side - 1)),
+            dma((count, depth, side - 1)),
+            dma((count, depth, side - 1)),
+            dma((count, depth)),
+            dma((count, depth)),
+        ],
+        compiler_params=pltpu.CompilerParams(
+            collective_id=call_id, has_side_effects=True, vmem_limit_bytes=32 * 1024 * 1024
+        ),
+    )(*views)
+    return [one.reshape(shape) for one, shape in zip(full, shapes)]
 
 
 def head_pairs(matrix):
@@ -162,12 +624,13 @@
     table = lax.all_to_all(served, ALL, split_axis=0, concat_axis=0, tiled=True)
     table = table.reshape(owners, 2, capacity, width).transpose(1, 0, 2, 3).reshape(2, slots, width)
 
-    qkv_full = lax.all_gather(w_qkv, "fsdp", axis=1, tiled=True)
-    attn_out_full = lax.all_gather(w_attn_out, "fsdp", axis=0, tiled=True)
-    query_full = lax.all_gather(w_mem_query, "fsdp", axis=0, tiled=True)
-    keys_full = lax.all_gather(sub_keys, "fsdp", axis=0, tiled=True)
-    gate_full = lax.all_gather(w_gate, "fsdp", axis=0, tiled=True)
-    mem_out_full = lax.all_gather(w_mem_out, "fsdp", axis=0, tiled=True)
+    side, depth = grid_of(lax.axis_size("dp"), lax.axis_size("fsdp"))
+    qkv_full, attn_out_full, query_full, keys_full, gate_full, mem_out_full = gather_weights(
+        side,
+        depth,
+        (w_qkv, w_attn_out, w_mem_query, sub_keys, w_gate, w_mem_out),
+        0,
+    )
 
     x_rows = jnp.concatenate([x_prompt[0], x_cont[0]], axis=0).astype(F32)
     dy_low = jnp.concatenate([cot_prompt[0], cot_cont[0]], axis=0)
@@ -303,22 +766,42 @@
     grad_x = grad_hidden + grad_x
     grad_qkv = jnp.stack([mm_l(normed, piece) for piece in (grad_q, grad_k, grad_v)])
 
-    def scatter(value, axis):
-        return lax.psum_scatter(value, ALL, scatter_dimension=axis, tiled=True)
-
+    devices = owners
+    block = cols // devices
+    keys_low = grad_keys.astype(BF).reshape(devices, 2, block, HALF).transpose(0, 2, 1, 3)
+    gains = jnp.concatenate([gain_attn_part, gain_mem_part]).reshape(2 * cols // 128, 128)
+    sums = reduce_grads(
+        side,
+        depth,
+        (
+            grad_qkv.astype(BF),
+            grad_attn_out.astype(BF),
+            grad_query_w.astype(BF),
+            keys_low.reshape(cols, 2 * HALF),
+            grad_gate_w.astype(BF),
+            grad_mem_out.astype(BF),
+        ),
+        gains,
+        1,
+    )
+    own = lax.axis_index("dp") * depth + lax.axis_index("fsdp")
+    gain_shards = lax.dynamic_index_in_dim(
+        sums[6].reshape(2, devices, block), own, axis=1, keepdims=False
+    )
+    sub_shard = sums[3].reshape(block, 2, HALF).transpose(1, 0, 2).reshape(2 * block, HALF)
     return (
         out[None, :rows],
         out[None, rows:],
         grad_x[None, :rows],
         grad_x[None, rows:],
-        scatter(gain_attn_part, 0),
-        scatter(gain_mem_part, 0),
-        scatter(grad_qkv.astype(BF), 1).astype(F32),
-        scatter(grad_attn_out.astype(BF), 0).astype(F32),
-        scatter(grad_query_w.astype(BF), 0).astype(F32),
-        scatter(grad_keys.astype(BF), 0).astype(F32),
-        scatter(grad_gate_w.astype(BF), 0).astype(F32),
-        scatter(grad_mem_out.astype(BF), 0).astype(F32),
+        gain_shards[0],
+        gain_shards[1],
+        sums[0],
+        sums[1],
+        sums[2],
+        sub_shard,
+        sums[4],
+        sums[5],
         grad_rows,
     )
 

time: 1880 us -> 915 us (0.49)
  waiting for transfers between devices: 1180 us -> 54.7 us
  Pallas kernels: 0 us -> 221 us
  blocking collectives: 43 us -> 0 us
  matrix products: 395 us -> 362 us
  local copies, waits for them, and re-layouts: 106 us -> 129 us
    reduce_scatter x6 -> x0, waiting for transfers between devices: 750 us -> none  [scatter(): return lax.psum_scatter(value, ALL, scatter_dimension=axis, tiled=True)]
    all_gather x6 -> x0, waiting for transfers between devices: 269 us -> none  [the longest x1 118 us: per_device(): qkv_full = lax.all_gather(w_qkv, 'fsdp', axis=1, tiled=True)]
    pallas_call x0 -> x2, Pallas kernels: none -> 221 us  [the longest x1 119 us: reduce_grads(): pl.pallas_call(functools.partial(reduce_kernel, side, depth, layout), out...]
    unnamed x1 -> x0, blocking collectives: 43 us -> none
    all_to_all x1, waiting for transfers between devices: 41.9 us -> 0.01 us  [per_device(): table = lax.all_to_all(served, ALL, split_axis=0, concat_axis=0, tiled=True)]
    all_to_all x1, waiting for transfers between devices: 56.1 us -> 29.4 us  [per_device(): lax.all_to_all(jnp.stack([piece.reshape(owners, capacity, width) for piec...]
    dot_general x18, matrix products: 59.7 us -> 37.1 us  [mm_l(): lax.dot_general(left, right, (((0,), (0,)), ((), ())), preferred_element_...]
  transfers between devices with their start and end apart: 19 -> 7, of which waited for: 13 -> 2; matrix products, arithmetic and copies ran while one was open for 18% -> 33% of each run, Pallas kernels for 0% -> 0%
where the time goes in v2:
time: 915 us; the launch traced here: 904 us
  matrix products  362 us (40%)
  Pallas kernels  221 us (24%)
  local copies, waits for them, and re-layouts  129 us (14%)
  other arithmetic  105 us (11%)
  waiting for transfers between devices  54.7 us (6%)
  between operations  15.5 us (2%)
  starting transfers between devices  15.4 us (2%)
    pallas_call x1, Pallas kernels, reduce_grads(): pl.pallas_call(functools.partial(reduce_kernel, side, depth, layout), out...  119 us
    pallas_call x1, Pallas kernels, gather_weights(): pl.pallas_call(functools.partial(gather_kernel, side, depth, layout), out...  102 us
    dot_general x42, matrix products, mm(): return jnp.dot(left, right, preferred_element_type=F32)  76.4 us
    dot_general x32, matrix products, one_pair(): jnp.einsum('qhd,khd->hqk', q_pair, k_pair, preferred_element_type=jnp.flo...  59.7 us
    reduce_sum x2, other arithmetic, pick_weights(): jnp.sum((slot_ids[..., None] == jnp.arange(slots, dtype=jnp.int32)).astyp...  37.6 us
    dot_general x16, matrix products, one_pair(): jnp.einsum('hqk,khd->qhd', weights, v_pair, preferred_element_type=jnp.fl...  37.4 us
    dot_general x17, matrix products, mm_t(): lax.dot_general(left, right, (((1,), (1,)), ((), ())), preferred_element_...  37.3 us
    dot_general x18, matrix products, mm_l(): lax.dot_general(left, right, (((0,), (0,)), ((), ())), preferred_element_...  37.1 us
  transfers between devices with their start and end apart: 7, of which 2 were waited for; matrix products, arithmetic and copies ran while one was open for 33% of the time, Pallas kernels for 0%

profile of v2, /device:TPU:0, one launch (start us, length us, event | category | flops | bytes accessed | tf_op | source)
XLA Modules:
  0.0 903.8 jit_solution(2452472347334491757)
XLA Ops:
  14.4 101.7 %shard_map.255 = (bf16[3,4,2,2,2,32,1024]{6,5,4,3,2,1,0:T(8,128)(2,1)S(1)}, bf16[4,2,2,2,32,1024]{5,4,3,2,1,0:T(8,128)(2,1)S(1)}, bf16[4,2,2,2,32,4096]{5,4,3,2,...) custom-call(bf16[3,2,2,2,32,1024]{5,4,3,2,1,0:T(8,128)(2,1)S(1)} %bi, ...), custom_call_target="tpu_custom_call" | custom-call | tf_op jit(solution)/shard_map/pallas_call | solution.py:481
  155.7 18.9 %convert_reduce_fusion.1 = f32[256,4,512]{2,1,0:T(4,128)} fusion(s32[256,4,32]{2,1,0:T(4,128)S(1)} %copy.109), kind=kLoop, calls=%fused_computation.116 | loop fusion | flops 49807360 | bytes 2228224 | tf_op jit(solution)/shard_map/reduce_sum | solution.py:589
  174.6 18.7 %convert_reduce_fusion = f32[256,4,512]{2,1,0:T(4,128)} fusion(s32[256,4,32]{2,1,0:T(4,128)S(1)} %copy.114), kind=kLoop, calls=%fused_computation.114 | loop fusion | flops 49807360 | bytes 2228224 | tf_op jit(solution)/shard_map/reduce_sum | solution.py:589
  202.7 8.0 fusion.106
  210.8 5.9 all-to-all-start.1
  220.2 4.8 copy.106
  228.5 4.4 copy.108
  233.7 37.3 %while.54 = (s32[]{:T(128)}, bf16[8,256,2,64]{1,3,2,0:T(8,128)(2,1)}, f32[8,2,256]{2,1,0:T(2,128)S(1)}, bf16[8,1280,2,64]{1,3,2,0:T(8,128)(2,1)}, pred[256,1280]...) while((s32[]{:T(128)}, ...), condition=%wide.region_8.9_spmd, body=%wide.region_5.8_spmd.sunk | while | flops 173047296 | bytes 8996961 | solution.py:532
  271.0 4.1 copy.103
  275.2 3.9 copy.105
  280.0 38.6 %while.56 = (s32[]{:T(128)}, bf16[8,256,2,64]{1,3,2,0:T(8,128)(2,1)}, f32[8,2,256]{2,1,0:T(2,128)S(1)}, bf16[8,1024,2,64]{1,3,2,0:T(8,128)(2,1)}, bf16[8,256,2,6...) while((s32[]{:T(128)}, ...), condition=%wide.region_4.5_spmd.clone, body=%wide.region_1.4_spmd.clone.sunk | while | flops 140803584 | bytes 8014945 | solution.py:532
  318.6 3.5 multiply_reduce_fusion.6
  323.8 8.5 convolution_convert_fusion.2
  356.5 6.0 fusion.248
  363.8 4.2 copy.117
  393.4 3.6 multiply_subtract_fusion
  423.4 3.6 fusion.117
  429.0 4.0 fusion.116
  436.8 3.6 fusion.115
  445.9 9.3 %fusion.259 = f32[512,1024]{1,0:T(8,128)S(1)} fusion(bf16[512,4096]{0,1:T(8,128)(2,1)S(1)} %fusion.114, bf16[1024,4096]{1,0:T(8,128)(2,1)} %bitcast.557), kind=kOutput, calls=%fused_computation.445 | convolution fusion | flops 4294967296 | bytes 14680064 | tf_op jit(solution)/shard_map/dot_general | solution.py:28
  464.1 74.5 %while.55 = (s32[]{:T(128)}, bf16[8,256,2,64]{1,3,2,0:T(8,128)(2,1)}, f32[8,1280,2,64]{1,3,2,0:T(8,128)}, f32[8,1280,2,64]{1,3,2,0:T(8,128)}, bf16[8,1280,2,64]{...) while((s32[]{:T(128)}, ...), condition=%wide.region_26.27_spmd, body=%wide.region_24.26_spmd.sunk | while | flops 425524736 | bytes 22690936 | solution.py:565
  541.5 80.4 %while.57 = (s32[]{:T(128)}, bf16[8,256,2,64]{1,3,2,0:T(8,128)(2,1)}, f32[8,1024,2,64]{1,3,2,0:T(8,128)}, f32[8,1024,2,64]{1,3,2,0:T(8,128)}, bf16[8,1024,2,64]{...) while((s32[]{:T(128)}, ...), condition=%wide.region_23.24_spmd.clone, body=%wide.region_21.23_spmd.clone.sunk | while | flops 340688384 | bytes 18497656 | solution.py:565
  622.0 5.5 fusion.94
  632.2 5.9 all-to-all-start.2
  653.2 5.5 fusion.93
  678.8 6.8 convolution_convert_fusion.1
  685.6 29.4 %all-to-all-done.2 = bf16[32,2,16,1024]{3,2,1,0:T(8,128)(2,1)} async-done(((bf16[32,2,16,1024]{3,2,1,0:T(8,128)(2,1)}), bf16[32,2,16,1024]{3,2,1,0:T(8,128)(2,1)}, u32[]{:S(2)}, u32[]{:S(2)}) %all-to-all-start.2) | async-done | bytes 2097184 | tf_op jit(solution)/shard_map/all_to_all | solution.py:731
  715.0 9.0 %fusion.91 = f32[2048,1024]{1,0:T(8,128)} fusion(bf16[1024,1024]{1,0:T(8,128)(2,1)} %bitcast.132, s32[1024]{0:T(1024)S(1)} %copy-done.108), kind=kOutput, calls=%fused_computation.119 | convolution fusion | flops 4297064448 | bytes 10489856 | tf_op jit(solution)/shard_map/dot_general | solution.py:32
  724.1 4.6 fusion.153
  728.7 25.2 %reduce-scatter.5.cloned.1.call-done = bf16[256,1024]{0,1:T(8,128)(2,1)} async-done(((bf16[1024,1024]{0,1:T(8,128)(2,1)}), bf16[256,1024]{0,1:T(8,128)(2,1)}) %reduce-scatter.5.cloned.1.call-update) | async-done | bytes 524304 | tf_op jit(solution)/shard_map/reduce_scatter | solution.py:756
  753.9 5.1 fusion.105
  768.1 119.4 %shard_map.256 = (f32[3,32,1024]{2,1,0:T(8,128)}, f32[32,1024]{1,0:T(8,128)}, f32[32,4096]{1,0:T(8,128)}, f32[32,1024]{1,0:T(8,128)}, f32[32,1024]{1,0:T(8,128)}, /*index=5*/f32[32,1024]{1,0:T(8,128)}, f32[16,128]{1,0:T(8,128)}) custom-call(bf16[3,2,2,2,4,32,1024]{6,5,4,3,2,1,0:T(8,128)(2,1)} %pad_maximum_fusion.refs_0_, ...), custom_call_target="tpu_custom_call" | custom-call | tf_op jit(solution)/shard_map/pallas_call | solution.py:286
  (601 shorter events, 454.4 us)
Async XLA Ops:
  7.2 209.6 %all-gather.3.cloned.1.call-start = ((), (), s32[]{:S(2)}) async-start(), calls=%async_computation.5 | async-start | bytes 2621440 | tf_op jit(solution)/shard_map/all_gather | solution.py:643
  121.8 31.0 %copy-start.101 = (f32[512]{0:T(512)}, f32[512]{0:T(512)S(1)}, u32[]{:S(2)}) copy-start(f32[512]{0:T(512)S(1)} %get-tuple-element.389) | copy-start | bytes 6148
  124.9 76.9 %all-to-all-start = ((s32[2,32,16]{2,0,1:T(2,128)}), s32[2,32,16]{2,0,1:T(2,128)}, u32[]{:S(2)}, u32[]{:S(2)}) async-start(s32[2,32,16]{2,0,1:T(2,128)} %bitcast.61), calls=%async_computation | async-start | bytes 65536 | tf_op jit(solution)/shard_map/all_to_all | solution.py:621
  128.2 96.8 %all-gather.5.cloned.1.call-start = ((), (), s32[]{:S(2)}) async-start(), calls=%async_computation.6 | async-start | bytes 2621440 | tf_op jit(solution)/shard_map/all_gather | solution.py:642
  142.8 7.5 copy-start.96
  146.6 6.3 copy-start.49
  202.7 8.0 copy-start.107
  210.8 170.5 %all-to-all-start.1 = ((bf16[32,32,1024]{2,1,0:T(8,128)(2,1)}), bf16[32,32,1024]{2,1,0:T(8,128)(2,1)}, u32[]{:S(2)}, u32[]{:S(2)}) async-start(bf16[32,32,1024]{2,1,0:T(8,128)(2,1)} %bitcast.516), calls=%async_computation.1 | async-start | bytes 4194304 | tf_op jit(solution)/shard_map/all_to_all | solution.py:624
  216.7 507.4 %reduce-scatter.3.cloned.1.call-start = ((), (), s32[]{:S(2)}) async-start(), calls=%async_computation.7 | async-start | bytes 2621440 | tf_op jit(solution)/shard_map/reduce_scatter | solution.py:753
  280.0 38.6 %copy-start.40 = (bf16[1,256,1024]{2,1,0:T(8,128)(2,1)S(1)}, bf16[1,256,1024]{2,1,0:T(8,128)(2,1)}, u32[]{:S(2)}) copy-start(bf16[1,256,1024]{2,1,0:T(8,128)(2,1)} %param.25) | copy-start | bytes 1572868
  318.6 4.9 copy-start.99
  323.7 8.5 copy-start.62
  323.7 8.5 copy-start.83
  323.7 8.5 copy-start.85
  348.0 5.2 copy-start.57
  368.0 5.9 copy-start.63
  418.1 5.2 copy-start.31
  429.0 7.9 copy-start.33
  445.9 9.3 %copy-start.111 = (bf16[512,4096]{0,1:T(8,128)(2,1)}, bf16[512,4096]{0,1:T(8,128)(2,1)S(1)}, u32[]{:S(2)}) copy-start(bf16[512,4096]{0,1:T(8,128)(2,1)S(1)} %fusion.114) | copy-start | bytes 12582916
  445.9 9.3 %copy-start.34 = (f32[256,1024]{1,0:T(8,128)S(1)}, f32[256,1024]{1,0:T(8,128)}, u32[]{:S(2)}) copy-start(f32[256,1024]{1,0:T(8,128)} %fusion.260) | copy-start | bytes 3145732
  445.9 9.3 %copy-start.35 = (f32[256,1024]{1,0:T(8,128)S(1)}, f32[256,1024]{1,0:T(8,128)}, u32[]{:S(2)}) copy-start(f32[256,1024]{1,0:T(8,128)} %fusion.261) | copy-start | bytes 3145732
  445.9 9.3 %copy-start.52 = (f32[512,1024]{1,0:T(8,128)S(1)}, f32[512,1024]{1,0:T(8,128)}, u32[]{:S(2)}) copy-start(f32[512,1024]{1,0:T(8,128)} %copy-done.51) | copy-start | bytes 6291460
  445.9 9.3 %copy-start.53 = (f32[512,1024]{1,0:T(8,128)S(1)}, f32[512,1024]{1,0:T(8,128)}, u32[]{:S(2)}) copy-start(f32[512,1024]{1,0:T(8,128)} %get-tuple-element.399) | copy-start | bytes 6291460
  632.2 5.9 copy-start.47
  632.2 82.8 %all-to-all-start.2 = ((bf16[32,2,16,1024]{3,2,1,0:T(8,128)(2,1)}), bf16[32,2,16,1024]{3,2,1,0:T(8,128)(2,1)}, u32[]{:S(2)}, u32[]{:S(2)}) async-start(bf16[32,2,16,1024]{3,2,1,0:T(8,128)(2,1)} %pad_maximum_fusion.6), calls=%async_computation.4 | async-start | bytes 4194304 | tf_op jit(solution)/shard_map/all_to_all | solution.py:731
  638.1 115.8 %reduce-scatter.5.cloned.1.call-start = ((), (), s32[]{:S(2)}) async-start(), calls=%async_computation.8 | async-start | bytes 2621440 | tf_op jit(solution)/shard_map/reduce_scatter | solution.py:756
  678.8 36.2 %copy-start.108 = (s32[1024]{0:T(1024)S(1)}, s32[1024]{0:T(1024)}, u32[]{:S(2)}) copy-start(s32[1024]{0:T(1024)} %copy-done.107) | copy-start | bytes 12292
  724.1 29.9 %copy-start.42 = (bf16[1,256,1024]{2,1,0:T(8,128)(2,1)S(1)}, bf16[1,256,1024]{2,1,0:T(8,128)(2,1)}, u32[]{:S(2)}) copy-start(bf16[1,256,1024]{2,1,0:T(8,128)(2,1)} %param.25) | copy-start | bytes 1572868
  724.1 29.9 %copy-start.45 = (bf16[1,256,1024]{2,1,0:T(8,128)(2,1)S(1)}, bf16[1,256,1024]{2,1,0:T(8,128)(2,1)}, u32[]{:S(2)}) copy-start(bf16[1,256,1024]{2,1,0:T(8,128)(2,1)} %param.24) | copy-start | bytes 1572868
  753.9 5.1 copy-start.103
  887.5 8.3 copy-start.95
  887.5 8.9 copy-start.94
  (90 other events, 200.5 us)
Sparse Core Ops, SparseCore 0:
  124.3 44.3 all-gather.2
  170.8 44.5 all-gather.4
  627.6 73.0 reduce-scatter.2
  703.0 50.9 reduce-scatter.4

commit v3 on v1

--- a/solution.py
+++ b/solution.py
@@ -1,19 +1,25 @@
+import functools
 import jax
 import jax.numpy as jnp
 from jax import lax
+from jax.experimental import pallas as pl
+from jax.experimental.pallas import tpu as pltpu
 from jax.sharding import PartitionSpec as P
-
-HEADS = 16
+BF = jnp.bfloat16
+F32 = jnp.float32
+ALL = ("dp", "fsdp")
+MESH = pl.DeviceIdType.MESH
+LAG = 2
+GATHER_LAG = 2
+COLLECT_LAG = 2
+AHEAD = 3
+PIECE = 1024
+PAIR = 128
 HDIM = 64
 MH = 4
 HALF = 512
 SUB = 256
-PL = 1024
-
-
-BF = jnp.bfloat16
-F32 = jnp.float32
-ALL = ("dp", "fsdp")
+NEVER = -1e30
 
 
 def mm(left, right):
@@ -42,75 +48,939 @@
     return (grad_matrix, jnp.sum(grad_normed * matrix * inverse, axis=0))
 
 
-def head_pairs(matrix):
-    row_count = matrix.shape[0]
-    return matrix.reshape(row_count, HEADS // 2, 2, HDIM).transpose(1, 0, 2, 3)
-
-
-def merge_pairs(matrix):
-    row_count = matrix.shape[1]
-    return matrix.transpose(1, 0, 2, 3).reshape(row_count, HEADS * HDIM)
-
-
-def attend_forward(queries, key_rows, val_rows, visible):
-
-    def one_pair(pieces):
-        q_pair, k_pair, v_pair = pieces
-        scores = (
-            jnp.einsum("qhd,khd->hqk", q_pair, k_pair, preferred_element_type=jnp.float32) * 0.125
+def grid_of(plane, depth):
+    side = 1
+    while 2 * side * side < plane:
+        side += 1
+    return side, depth
+
+
+def place(side):
+    dp = lax.axis_index("dp")
+    return (dp // (2 * side), (dp // 2) % side, dp % 2, lax.axis_index("fsdp"))
+
+
+def device_at(side, y, x, core, z):
+    return ((y * side + x) * 2 + core, z)
+
+
+def greet(side, depth):
+    y, x, core, z = place(side)
+    barrier = pltpu.get_barrier_semaphore()
+    peers = [device_at(side, y, x, 1 - core, z)]
+    for hop in range(1, side):
+        peers.append(device_at(side, y, (x + hop) % side, core, z))
+        peers.append(device_at(side, (y + hop) % side, x, core, z))
+    for hop in range(1, depth):
+        peers.append(device_at(side, y, x, core, (z + hop) % depth))
+    for peer in peers:
+        pl.semaphore_signal(barrier, inc=1, device_id=peer, device_id_type=MESH)
+    pl.semaphore_wait(barrier, len(peers))
+
+
+def remote(source, target, send_sem, recv_sem, peer):
+    return pltpu.make_async_remote_copy(
+        src_ref=source,
+        dst_ref=target,
+        send_sem=send_sem,
+        recv_sem=recv_sem,
+        device_id=peer,
+        device_id_type=MESH,
+    )
+
+
+class Gather:
+    def __init__(self, side, depth, shards):
+        self.side, self.depth = side, depth
+        self.views, self.outs, self.shapes, self.held, self.layout = [], [], [], [], []
+        plane = 2 * side * side
+        for shard in shards:
+            rows, cols = shard.shape[-2:]
+            block, width = rows // plane, min(cols, PIECE)
+            lead = shard.shape[:-2]
+            self.views.append(shard.reshape(lead + (side, side, 2, block, cols)))
+            leads = range(lead[0]) if lead else (None,)
+            self.layout.append(
+                [(number, start) for number in leads for start in range(0, cols, width)]
+            )
+            self.outs.append(
+                jax.ShapeDtypeStruct(lead + (depth, side, side, 2, block, cols), BF)
+            )
+            self.shapes.append(lead + (depth * rows, cols))
+            self.held.append(
+                pltpu.VMEM((len(self.layout[-1]), side, side, 2, block, width), BF)
+            )
+        self.count = count = sum(len(columns) for columns in self.layout)
+        self.steps = count + depth - 2 + 3 * GATHER_LAG
+        dma = pltpu.SemaphoreType.DMA
+        self.scratch = self.held + [
+            dma((count,)),
+            dma((count,)),
+            dma((count, depth)),
+            dma((count, depth)),
+            dma((count, depth)),
+            dma((count, depth, side - 1)),
+            dma((count, depth, side - 1)),
+            dma((count, depth, side - 1)),
+            dma((count, depth, side - 1)),
+            dma((count, depth)),
+            dma((count, depth)),
+        ]
+
+    def restore(self, full):
+        return [one.reshape(shape) for one, shape in zip(full, self.shapes)]
+
+    def bind(self, sources, outs, scratch):
+        self.sources, self.results = sources, outs
+        n_in = len(self.layout)
+        self.holders = scratch[:n_in]
+        (self.in_sem, self.out_sem, self.right_send, self.left_send, self.deep_recv,
+         self.one_send, self.one_recv, self.two_send, self.two_recv, self.core_send,
+         self.core_recv) = scratch[n_in:]
+        self.pieces = []
+        for number, columns in enumerate(self.layout):
+            width = self.holders[number].shape[-1]
+            width = width if sources[number].shape[-1] > width else None
+            for inner, (lead, start) in enumerate(columns):
+                self.pieces.append((number, lead, start, width, inner))
+
+    def cut(self, refs, k, *spot):
+        number, lead, start, width = self.pieces[k][:4]
+        ref = refs[number] if lead is None else refs[number].at[lead]
+        ref = ref.at[spot] if spot else ref
+        if width is None:
+            return ref
+        return ref.at[(slice(None),) * (len(ref.shape) - 1) + (pl.ds(start, width),)]
+
+    def along_z(self, k, zp, move, source=None):
+        y, x, core, z = place(self.side)
+        target = self.cut(self.results, k, zp, y, x, core)
+        send = self.right_send if move > 0 else self.left_send
+        return remote(target if source is None else source, target, send.at[k, zp],
+                      self.deep_recv.at[k, zp], device_at(self.side, y, x, core, z + move))
+
+    def one_copy(self, k, zp, hop):
+        side = self.side
+        y, x, core, z = place(side)
+        peer = device_at(side, y, (x + hop) % side, core, z) if k % 2 == 0 else device_at(
+            side, (y + hop) % side, x, core, z)
+        ref = self.cut(self.results, k, zp, y, x, core)
+        return remote(ref, ref, self.one_send.at[k, zp, hop - 1],
+                      self.one_recv.at[k, zp, hop - 1], peer)
+
+    def two_copy(self, k, zp, hop):
+        side = self.side
+        y, x, core, z = place(side)
+        x_first = k % 2 == 0
+        peer = device_at(side, (y + hop) % side, x, core, z) if x_first else device_at(
+            side, y, (x + hop) % side, core, z)
+        ref = (self.cut(self.results, k, zp, y, slice(None), core) if x_first
+               else self.cut(self.results, k, zp, slice(None), x, core))
+        return remote(ref, ref, self.two_send.at[k, zp, hop - 1],
+                      self.two_recv.at[k, zp, hop - 1], peer)
+
+    def core_copy(self, k, zp):
+        y, x, core, z = place(self.side)
+        ref = self.cut(self.results, k, zp, slice(None), slice(None), core)
+        return remote(ref, ref, self.core_send.at[k, zp], self.core_recv.at[k, zp],
+                      device_at(self.side, y, x, 1 - core, z))
+
+    def take(self, k):
+        number, inner = self.pieces[k][0], self.pieces[k][4]
+        return pltpu.make_async_copy(self.cut(self.sources, k), self.holders[number].at[inner],
+                                     self.in_sem.at[k])
+
+    def put(self, k):
+        z = place(self.side)[3]
+        number, inner = self.pieces[k][0], self.pieces[k][4]
+        return pltpu.make_async_copy(self.holders[number].at[inner],
+                                     self.cut(self.results, k, z), self.out_sem.at[k])
+
+    def start(self):
+        y, x, core, z = place(self.side)
+        for k in range(self.count):
+            self.take(k).start()
+            own = self.cut(self.sources, k, y, x, core)
+
+            @pl.when(z < self.depth - 1)
+            def _(k=k, own=own):
+                self.along_z(k, z, 1, own).start()
+
+            @pl.when(z > 0)
+            def _(k=k, own=own):
+                self.along_z(k, z, -1, own).start()
+
+    def step(self, i):
+        side, depth = self.side, self.depth
+        z = place(side)[3]
+        if i < self.count:
+            self.take(i).wait()
+            self.put(i).start()
+        for stage in range(4):
+            for distance in range(1, depth):
+                k = i - stage * GATHER_LAG - (distance - 1)
+                if not 0 <= k < self.count:
+                    continue
+                for sign in (1, -1):
+                    zp = z + sign * distance
+
+                    @pl.when(jnp.logical_and(zp >= 0, zp < depth))
+                    def _(k=k, zp=zp, sign=sign, stage=stage):
+                        self.arrival(stage, k, zp, sign)
+
+    def arrival(self, stage, k, zp, sign):
+        side, depth = self.side, self.depth
+        z = place(side)[3]
+        if stage == 0:
+            self.along_z(k, zp, 1).wait_recv()
+
+            @pl.when(z < depth - 1 if sign < 0 else z > 0)
+            def _():
+                self.along_z(k, zp, -sign).start()
+
+            for hop in range(1, side):
+                self.one_copy(k, zp, hop).start()
+        elif stage == 1:
+            for hop in range(1, side):
+                self.one_copy(k, zp, hop).wait_recv()
+            for hop in range(1, side):
+                self.two_copy(k, zp, hop).start()
+        elif stage == 2:
+            for hop in range(1, side):
+                self.two_copy(k, zp, hop).wait_recv()
+            self.core_copy(k, zp).start()
+        else:
+            self.core_copy(k, zp).wait_recv()
+
+    def finish(self):
+        side, depth = self.side, self.depth
+        z = place(side)[3]
+        for k in range(self.count):
+            self.put(k).wait()
+            for zp in range(depth):
+                @pl.when(jnp.logical_and(zp <= z, z < depth - 1))
+                def _(k=k, zp=zp):
+                    self.along_z(k, zp, 1).wait_send()
+
+                @pl.when(jnp.logical_and(zp >= z, z > 0))
+                def _(k=k, zp=zp):
+                    self.along_z(k, zp, -1).wait_send()
+
+                @pl.when(zp != z)
+                def _(k=k, zp=zp):
+                    for hop in range(1, side):
+                        self.one_copy(k, zp, hop).wait_send()
+                        self.two_copy(k, zp, hop).wait_send()
+                    self.core_copy(k, zp).wait_send()
+
+
+class Reduce:
+    def __init__(self, side, depth, grads, gains=None):
+        self.side, self.depth = side, depth
+        self.layout, self.views, self.outs = [], [], []
+        self.width = width = 1024
+        devices = 2 * side * side * depth
+        for grad in grads:
+            rows, cols = grad.shape[-2:]
+            self.block = block = rows // devices
+            lead = grad.shape[:-2]
+            self.views.append(grad.reshape(lead + (side, side, 2, depth, block, cols)))
+            leads = range(lead[0]) if lead else (None,)
+            self.layout.append(
+                [(number, start) for number in leads for start in range(0, cols, width)]
+            )
+            self.outs.append(jax.ShapeDtypeStruct(lead + (block, cols), F32))
+        self.count = count = sum(len(columns) for columns in self.layout)
+        self.steps = count + 3 * LAG
+        self.gains = gains is not None
+        most = max(side, depth) - 1
+        dma = pltpu.SemaphoreType.DMA
+        self.scratch = [
+            pltpu.VMEM((count, side, side, depth, block, width), BF),
+            pltpu.VMEM((count, side, side, depth, block, width), BF),
+            pltpu.VMEM((count, side - 1, side, depth, block, width), BF),
+            pltpu.VMEM((count, side - 1, depth, block, width), BF),
+            pltpu.VMEM((count, depth - 1, block, width), BF),
+            pltpu.VMEM((count, block, width), F32),
+            dma((count,)),
+            dma((count,)),
+            dma((count,)),
+            dma((count, side - 1)),
+            dma((count, side - 1)),
+            dma((count, side - 1)),
+            dma((count, side - 1)),
+            dma((count, depth - 1)),
+            dma((count, depth - 1)),
+        ]
+        if self.gains:
+            self.views.append(gains)
+            self.outs.append(jax.ShapeDtypeStruct(gains.shape, F32))
+            self.scratch += [
+                pltpu.VMEM((4,) + gains.shape, F32),
+                pltpu.VMEM((4, most) + gains.shape, F32),
+                dma((4, most)),
+                dma((4, most)),
+            ]
+        any_space, vmem = pl.BlockSpec(memory_space=pl.ANY), pl.BlockSpec(memory_space=pltpu.VMEM)
+        self.in_specs = [any_space] * len(self.layout) + [vmem] * self.gains
+        self.out_specs = [vmem] * len(self.views)
+
+    def bind(self, sources, outs, scratch):
+        (self.mine, self.got_core, self.got_one, self.got_two, self.got_deep, self.total,
+         self.local_sem, self.core_send, self.core_recv, self.one_send, self.one_recv,
+         self.two_send, self.two_recv, self.deep_send, self.deep_recv) = scratch[:15]
+        self.results = outs
+        if self.gains:
+            self.gain_in, self.gain_out = sources[-1], outs[-1]
+            self.gain_sum, self.gain_got, self.gain_send, self.gain_recv = scratch[15:]
+        self.pieces = []
+        for number, columns in enumerate(self.layout):
+            for lead, start in columns:
+                ref = sources[number] if lead is None else sources[number].at[lead]
+                self.pieces.append((ref, number, lead, start))
+
+    def core_wait(self, k):
+        y, x, core, z = place(self.side)
+        return remote(self.got_core.at[k], self.got_core.at[k], self.core_send.at[k],
+                      self.core_recv.at[k], device_at(self.side, y, x, 1 - core, z))
+
+    def start(self):
+        y, x, core, z = place(self.side)
+        for k, (ref, _, _, start) in enumerate(self.pieces):
+            spot = pl.ds(start, self.width)
+            remote(ref.at[:, :, 1 - core, :, :, spot], self.got_core.at[k], self.core_send.at[k],
+                   self.core_recv.at[k], device_at(self.side, y, x, 1 - core, z)).start()
+            pltpu.make_async_copy(ref.at[:, :, core, :, :, spot], self.mine.at[k],
+                                  self.local_sem.at[k]).start()
+        if self.gains:
+            self.gain_copy(0, 0).start()
+
+    def one_copy(self, k, hop, x_first):
+        side = self.side
+        y, x, core, z = place(side)
+        peer = device_at(side, y, (x + hop) % side, core, z) if x_first else device_at(
+            side, (y + hop) % side, x, core, z)
+        source = (self.mine.at[k, :, (x + hop) % side] if x_first
+                  else self.mine.at[k, (y + hop) % side])
+        return remote(source, self.got_one.at[k, hop - 1], self.one_send.at[k, hop - 1],
+                      self.one_recv.at[k, hop - 1], peer)
+
+    def two_copy(self, k, hop, x_first):
+        side = self.side
+        y, x, core, z = place(side)
+        peer = device_at(side, (y + hop) % side, x, core, z) if x_first else device_at(
+            side, y, (x + hop) % side, core, z)
+        source = (self.mine.at[k, (y + hop) % side, x] if x_first
+                  else self.mine.at[k, y, (x + hop) % side])
+        return remote(source, self.got_two.at[k, hop - 1], self.two_send.at[k, hop - 1],
+                      self.two_recv.at[k, hop - 1], peer)
+
+    def deep_copy(self, k, hop):
+        y, x, core, z = place(self.side)
+        there = (z + hop) % self.depth
+        return remote(self.mine.at[k, y, x, there], self.got_deep.at[k, hop - 1],
+                      self.deep_send.at[k, hop - 1], self.deep_recv.at[k, hop - 1],
+                      device_at(self.side, y, x, core, there))
+
+    def gain_count(self, stage):
+        return (1, self.side - 1, self.side - 1, self.depth - 1)[stage]
+
+    def gain_copy(self, stage, number):
+        side, depth, hop = self.side, self.depth, number + 1
+        y, x, core, z = place(side)
+        peer = (
+            device_at(side, y, x, 1 - core, z),
+            device_at(side, y, (x + hop) % side, core, z),
+            device_at(side, (y + hop) % side, x, core, z),
+            device_at(side, y, x, core, (z + hop) % depth),
+        )[stage]
+        source = self.gain_in if stage == 0 else self.gain_sum.at[stage - 1]
+        return remote(source, self.gain_got.at[stage, number], self.gain_send.at[stage, number],
+                      self.gain_recv.at[stage, number], peer)
+
+    def both_orders(self, k, action):
+        @pl.when(k % 2 == 0)
+        def _():
+            action(True)
+
+        @pl.when(k % 2 == 1)
+        def _():
+            action(False)
+
+    def added(self, base, others):
+        if len(others) == 1:
+            return base + others[0]
+        value = base.astype(F32)
+        for other in others:
+            value = value + other.astype(F32)
+        return value.astype(base.dtype)
+
+    def after_core(self, k):
+        side, depth, mine, got = self.side, self.depth, self.mine, self.got_core
+        self.core_wait(k).wait_recv()
+        pltpu.make_async_copy(got.at[k], mine.at[k], self.local_sem.at[k]).wait()
+
+        def add(index, carry):
+            spot = (k, index // (side * depth), (index // depth) % side, index % depth)
+            mine[spot] = mine[spot] + got[spot]
+            return carry
+
+        lax.fori_loop(0, side * side * depth, add, 0)
+
+        def send(x_first):
+            for hop in range(1, side):
+                self.one_copy(k, hop, x_first).start()
+
+        self.both_orders(k, send)
+
+    def after_one(self, k):
+        side, depth, mine = self.side, self.depth, self.mine
+        y, x, core, z = place(side)
+
+        def finish(x_first):
+            for hop in range(1, side):
+                self.one_copy(k, hop, x_first).wait_recv()
+
+            def add(index, carry):
+                a, c = index // depth, index % depth
+                spot = (k, a, x, c) if x_first else (k, y, a, c)
+                mine[spot] = self.added(
+                    mine[spot], [self.got_one[k, hop, a, c] for hop in range(side - 1)]
+                )
+                return carry
+
+            lax.fori_loop(0, side * depth, add, 0)
+            for hop in range(1, side):
+                self.two_copy(k, hop, x_first).start()
+
+        self.both_orders(k, finish)
+
+    def after_two(self, k):
+        side, depth, mine = self.side, self.depth, self.mine
+        y, x, core, z = place(side)
+
+        def finish(x_first):
+            for hop in range(1, side):
+                self.two_copy(k, hop, x_first).wait_recv()
+
+        self.both_orders(k, finish)
+
+        def add(c, carry):
+            mine[k, y, x, c] = self.added(
+                mine[k, y, x, c], [self.got_two[k, hop, c] for hop in range(side - 1)]
+            )
+            return carry
+
+        lax.fori_loop(0, depth, add, 0)
+        for hop in range(1, depth):
+            self.deep_copy(k, hop).start()
+
+    def after_deep(self, k):
+        y, x, core, z = place(self.side)
+        for hop in range(1, self.depth):
+            self.deep_copy(k, hop).wait_recv()
+        value = self.mine[k, y, x, z].astype(F32)
+        for hop in range(self.depth - 1):
+            value = value + self.got_deep[k, hop].astype(F32)
+        self.total[k] = value
+
+    def step(self, i):
+        stages = (self.after_core, self.after_one, self.after_two, self.after_deep)
+        for number, action in enumerate(stages):
+            lag = number * LAG
+
+            @pl.when(jnp.logical_and(i >= lag, i < self.count + lag))
+            def _(lag=lag, action=action):
+                action(i - lag)
+
+        for stage in range(4 if self.gains else 0):
+            @pl.when(i == stage + 1)
+            def _(stage=stage):
+                value = self.gain_in[...] if stage == 0 else self.gain_sum[stage - 1]
+                for number in range(self.gain_count(stage)):
+                    self.gain_copy(stage, number).wait_recv()
+                    value = value + self.gain_got[stage, number]
+                self.gain_sum[stage] = value
+                if stage < 3:
+                    for number in range(self.gain_count(stage + 1)):
+                        self.gain_copy(stage + 1, number).start()
+
+    def finish(self):
+        if self.gains:
+            self.gain_out[...] = self.gain_sum[3]
+        for k, (_, number, lead, start) in enumerate(self.pieces):
+            spot = (slice(None), pl.ds(start, self.width))
+            if lead is None:
+                self.results[number][spot] = self.total[k]
+            else:
+                self.results[number][(lead,) + spot] = self.total[k]
+
+        def drain(k, carry):
+            self.core_wait(k).wait_send()
+
+            def sent(x_first):
+                for hop in range(1, self.side):
+                    self.one_copy(k, hop, x_first).wait_send()
+                    self.two_copy(k, hop, x_first).wait_send()
+
+            self.both_orders(k, sent)
+            for hop in range(1, self.depth):
+                self.deep_copy(k, hop).wait_send()
+            return carry
+
+        lax.fori_loop(0, self.count, drain, 0)
+        for stage in range(4 if self.gains else 0):
+            for number in range(self.gain_count(stage)):
+                self.gain_copy(stage, number).wait_send()
+
+
+def split_refs(refs, *counts):
+    groups, at = [], 0
+    for count in counts:
+        groups.append(refs[at : at + count])
+        at += count
+    return groups + [refs[at:]]
+
+
+def params(call_id, mib):
+    return pltpu.CompilerParams(
+        collective_id=call_id, has_side_effects=True, vmem_limit_bytes=mib * 1024 * 1024
+    )
+
+
+def gather_kernel(plan, *refs):
+    n = len(plan.views)
+    sources, outs, scratch = split_refs(refs, n, n)
+    plan.bind(sources, outs, scratch)
+    greet(plan.side, plan.depth)
+    plan.start()
+    for i in range(plan.steps):
+        plan.step(i)
+    plan.finish()
+
+
+def gather_weights(side, depth, shards, call_id):
+    plan = Gather(side, depth, shards)
+    any_space = pl.BlockSpec(memory_space=pl.ANY)
+    full = pl.pallas_call(
+        functools.partial(gather_kernel, plan),
+        out_shape=tuple(plan.outs),
+        in_specs=[any_space] * len(plan.views),
+        out_specs=(any_space,) * len(plan.views),
+        scratch_shapes=plan.scratch,
+        compiler_params=params(call_id, 32),
+    )(*plan.views)
+    return plan.restore(full)
+
+
+def reduce_kernel(plan, *refs):
+    n = len(plan.views)
+    sources, outs, scratch = split_refs(refs, n, n)
+    plan.bind(sources, outs, scratch)
+    greet(plan.side, plan.depth)
+    plan.start()
+
+    def run(i, carry):
+        plan.step(i)
+        return carry
+
+    lax.fori_loop(0, max(plan.steps, 5), run, 0)
+    plan.finish()
+
+
+def reduce_grads(side, depth, grads, gains, call_id):
+    plan = Reduce(side, depth, grads, gains)
+    return pl.pallas_call(
+        functools.partial(reduce_kernel, plan),
+        out_shape=tuple(plan.outs),
+        in_specs=plan.in_specs,
+        out_specs=tuple(plan.out_specs),
+        scratch_shapes=plan.scratch,
+        compiler_params=params(call_id, 60),
+    )(*plan.views)
+
+
+def half_masks(width):
+    lane = lax.broadcasted_iota(jnp.int32, (1, width), 1)
+    return (lane < width // 2, lane >= width // 2)
+
+
+def dot_rows(left, right):
+    return lax.dot_general(left, right, (((1,), (1,)), ((), ())), preferred_element_type=F32)
+
+
+def dot_first(left, right):
+    return lax.dot_general(left, right, (((0,), (0,)), ((), ())), preferred_element_type=F32)
+
+
+def dot_plain(left, right):
+    return lax.dot_general(left, right, (((1,), (0,)), ((), ())), preferred_element_type=F32)
+
+
+def prompt_mask(scores, chunk, z, rows):
+    key = lax.broadcasted_iota(jnp.int32, scores.shape, 0) + chunk * rows
+    query = lax.broadcasted_iota(jnp.int32, scores.shape, 1)
+    seen = jnp.logical_or(query >= rows, key <= query + z * rows)
+    return jnp.where(seen, scores, NEVER)
+
+
+def own_mask(scores):
+    key = lax.broadcasted_iota(jnp.int32, scores.shape, 0)
+    query = lax.broadcasted_iota(jnp.int32, scores.shape, 1)
+    return jnp.where(key <= query, scores, NEVER)
+
+
+def forward_pair(p, z, rows, depth, q_ref, k_ref, v_ref, keys, vals, att_ref, lse_ref):
+    cols = pl.ds(pl.multiple_of(p * PAIR, PAIR), PAIR)
+    q_pair = q_ref[:, cols] * jnp.asarray(0.125, BF)
+    k_own, v_own = k_ref[pl.ds(rows, rows), cols], v_ref[pl.ds(rows, rows), cols]
+    outs = []
+    for head, mask in enumerate(half_masks(PAIR)):
+        q_head = jnp.where(mask, q_pair, jnp.zeros_like(q_pair))
+        scores = [
+            prompt_mask(dot_rows(keys[p, chunk], q_head), chunk, z, rows) for chunk in range(depth)
+        ]
+        own = own_mask(dot_rows(k_own, q_head[rows:]))
+        top = jnp.max(scores[0], axis=0, keepdims=True)
+        for piece in scores[1:]:
+            top = jnp.maximum(top, jnp.max(piece, axis=0, keepdims=True))
+        top_c = jnp.maximum(top[:, rows:], jnp.max(own, axis=0, keepdims=True))
+        top = jnp.concatenate([top[:, :rows], top_c], axis=1)
+        total = jnp.zeros_like(top)
+        out = jnp.zeros((PAIR, 2 * rows), F32)
+        for chunk in range(depth):
+            expo = jnp.exp(scores[chunk] - top)
+            total = total + jnp.sum(expo, axis=0, keepdims=True)
+            out = out + dot_first(vals[p, chunk], expo.astype(BF))
+        expo = jnp.exp(own - top_c)
+        total_c = total[:, rows:] + jnp.sum(expo, axis=0, keepdims=True)
+        out_c = out[:, rows:] + dot_first(v_own, expo.astype(BF))
+        total = jnp.concatenate([total[:, :rows], total_c], axis=1)
+        out = jnp.concatenate([out[:, :rows], out_c], axis=1) / total
+        lse_ref[pl.ds(2 * p + head, 1), :] = top + jnp.log(total)
+        outs.append(out[head * HDIM : (head + 1) * HDIM])
+    att_ref[:, cols] = jnp.concatenate(outs, axis=0).T.astype(BF)
+
+
+def backward_pair(p, z, rows, depth, q_ref, k_ref, v_ref, keys, vals, lse_ref, att_ref, g_ref,
+                  dq_ref, dk_ref, dv_ref, part):
+    cols = pl.ds(pl.multiple_of(p * PAIR, PAIR), PAIR)
+    own_rows = pl.ds(rows, rows)
+    q_pair = q_ref[:, cols] * jnp.asarray(0.125, BF)
+    g_pair = g_ref[:, cols]
+    k_own, v_own = k_ref[own_rows, cols], v_ref[own_rows, cols]
+    pulled = (g_pair.astype(F32) * att_ref[:, cols].astype(F32)).T
+    masks = half_masks(PAIR)
+    q_heads = [jnp.where(mask, q_pair, jnp.zeros_like(q_pair)) for mask in masks]
+    g_heads = [jnp.where(mask, g_pair, jnp.zeros_like(g_pair)) for mask in masks]
+    lses = [lse_ref[pl.ds(2 * p + head, 1), :] for head in range(2)]
+    deltas = [
+        jnp.sum(pulled[head * HDIM : (head + 1) * HDIM], axis=0, keepdims=True)
+        for head in range(2)
+    ]
+    dq = [jnp.zeros((PAIR, 2 * rows), F32) for _ in range(2)]
+    for chunk in range(depth):
+        dk = jnp.zeros((rows, PAIR), F32)
+        dv = jnp.zeros((rows, PAIR), F32)
+        k_chunk, v_chunk = keys[p, chunk], vals[p, chunk]
+        for head in range(2):
+            scores = prompt_mask(dot_rows(k_chunk, q_heads[head]), chunk, z, rows)
+            prob = jnp.exp(scores - lses[head])
+            d_prob = dot_rows(v_chunk, g_heads[head])
+            d_score = (prob * (d_prob - deltas[head])).astype(BF)
+            dv = dv + dot_plain(prob.astype(BF), g_heads[head])
+            dk = dk + dot_plain(d_score, q_heads[head])
+            dq[head] = dq[head] + dot_first(k_chunk, d_score)
+        part[p, chunk, 0] = dk.astype(BF)
+        part[p, chunk, 1] = dv.astype(BF)
+    dk = jnp.zeros((rows, PAIR), F32)
+    dv = jnp.zeros((rows, PAIR), F32)
+    for head in range(2):
+        q_head, g_head = q_heads[head][rows:], g_heads[head][rows:]
+        scores = own_mask(dot_rows(k_own, q_head))
+        prob = jnp.exp(scores - lses[head][:, rows:])
+        d_prob = dot_rows(v_own, g_head)
+        d_score = (prob * (d_prob - deltas[head][:, rows:])).astype(BF)
+        dv = dv + dot_plain(prob.astype(BF), g_head)
+        dk = dk + dot_plain(d_score, q_head)
+        more = dot_first(k_own, d_score)
+        dq[head] = jnp.concatenate([dq[head][:, :rows], dq[head][:, rows:] + more], axis=1)
+    dk_ref[own_rows, cols] = dk.astype(BF)
+    dv_ref[own_rows, cols] = dv.astype(BF)
+    both = jnp.concatenate([dq[0][:HDIM], dq[1][HDIM:]], axis=0) * 0.125
+    dq_ref[:, cols] = both.T.astype(BF)
+
+
+class Exchange:
+    def __init__(self, depth, rows, pairs):
+        self.depth, self.rows, self.pairs = depth, rows, pairs
+        dma = pltpu.SemaphoreType.DMA
+        self.scratch = [dma((2, 2, pairs, depth)), dma((2, pairs, depth))]
+
+    def bind(self, owned, gathered, scratch):
+        self.owned, self.gathered = owned, gathered
+        self.send_sem, self.recv_sem = scratch
+
+    def hop(self, kind, p, zp, move, own=False):
+        target = self.gathered[kind].at[p, zp]
+        cols = pl.ds(pl.multiple_of(p * PAIR, PAIR), PAIR)
+        source = self.owned[kind].at[pl.ds(0, self.rows), cols] if own else target
+        z = lax.axis_index("fsdp")
+        return remote(source, target, self.send_sem.at[kind, (move + 1) // 2, p, zp],
+                      self.recv_sem.at[kind, p, zp], (lax.axis_index("dp"), z + move))
+
+    def offer(self, p):
+        z = lax.axis_index("fsdp")
+        for move in (1, -1):
+            @pl.when(z < self.depth - 1 if move > 0 else z > 0)
+            def _(move=move):
+                for kind in range(2):
+                    self.hop(kind, p, z, move, own=True).start()
+        cols = pl.ds(pl.multiple_of(p * PAIR, PAIR), PAIR)
+        for kind in range(2):
+            self.gathered[kind][p, z] = self.owned[kind][pl.ds(0, self.rows), cols]
+
+    def step(self, i):
+        z = lax.axis_index("fsdp")
+        for distance in range(1, self.depth):
+            p = i - (distance - 1)
+            for sign in (1, -1):
+                zp = z + sign * distance
+                seen = jnp.logical_and(zp >= 0, zp < self.depth)
+
+                @pl.when(jnp.logical_and(seen, jnp.logical_and(p >= 0, p < self.pairs)))
+                def _(p=p, zp=zp, sign=sign):
+                    for kind in range(2):
+                        self.hop(kind, p, zp, 1).wait_recv()
+
+                    @pl.when(z < self.depth - 1 if sign < 0 else z > 0)
+                    def _():
+                        for kind in range(2):
+                            self.hop(kind, p, zp, -sign).start()
+
+    def finish(self):
+        z = lax.axis_index("fsdp")
+
+        def drain(p, carry):
+            for zp in range(self.depth):
+                for move in (1, -1):
+                    far = zp <= z if move > 0 else zp >= z
+                    inner = z < self.depth - 1 if move > 0 else z > 0
+
+                    @pl.when(jnp.logical_and(far, inner))
+                    def _(zp=zp, move=move):
+                        for kind in range(2):
+                            self.hop(kind, p, zp, move).wait_send()
+            return carry
+
+        lax.fori_loop(0, self.pairs, drain, 0)
+
+
+def forward_kernel(gather, exchange, *refs):
+    depth, rows, pairs = exchange.depth, exchange.rows, exchange.pairs
+    n = len(gather.views)
+    (q_ref, k_ref, v_ref), shards, (att_ref, lse_ref, keys, vals), full, swap, rest = split_refs(
+        refs, 3, n, 4, n, len(exchange.scratch))
+    gather.bind(shards, full, rest)
+    exchange.bind((k_ref, v_ref), (keys, vals), swap)
+    z = lax.axis_index("fsdp")
+    greet(gather.side, depth)
+    ahead = min(AHEAD, pairs)
+    for p in range(ahead):
+        exchange.offer(p)
+    gather.start()
+    turns = pairs + depth - 1
+
+    def run(i, carry):
+        @pl.when(i + ahead < pairs)
+        def _():
+            exchange.offer(i + ahead)
+
+        exchange.step(i)
+        for number in range(min(turns, gather.steps)):
+            @pl.when(i == number)
+            def _(number=number):
+                gather.step(number)
+
+        @pl.when(i >= depth - 1)
+        def _():
+            forward_pair(i - (depth - 1), z, rows, depth, q_ref, k_ref, v_ref, keys, vals, att_ref,
+                         lse_ref)
+
+        return carry
+
+    lax.fori_loop(0, turns, run, 0)
+    for number in range(turns, gather.steps):
+        gather.step(number)
+    exchange.finish()
+    gather.finish()
+
+
+def attention_forward(side, depth, q, k, v, shards, call_id):
+    rows, width = q.shape[0] // 2, q.shape[1]
+    pairs = width // PAIR
+    gather, exchange = Gather(side, depth, shards), Exchange(depth, rows, pairs)
+    any_space, vmem = pl.BlockSpec(memory_space=pl.ANY), pl.BlockSpec(memory_space=pltpu.VMEM)
+    spread = jax.ShapeDtypeStruct((pairs, depth, rows, PAIR), BF)
+    results = pl.pallas_call(
+        functools.partial(forward_kernel, gather, exchange),
+        out_shape=(
+            jax.ShapeDtypeStruct(q.shape, BF),
+            jax.ShapeDtypeStruct((2 * pairs, 2 * rows), F32),
+            spread,
+            spread,
         )
-        scores = jnp.where(visible[None], scores, -1e30)
-        row_max = jnp.max(scores, axis=-1, keepdims=True)
-        expo_rows = jnp.exp(scores - row_max)
-        row_total = jnp.sum(expo_rows, axis=-1, keepdims=True)
-        weights = (expo_rows / row_total).astype(jnp.bfloat16)
-        blended = jnp.einsum("hqk,khd->qhd", weights, v_pair, preferred_element_type=jnp.float32)
-        return (blended.astype(jnp.bfloat16), (row_max + jnp.log(row_total))[..., 0])
-
-    blended, logsum = lax.map(
-        one_pair, (head_pairs(queries), head_pairs(key_rows), head_pairs(val_rows))
-    )
-    return (merge_pairs(blended), logsum)
-
-
-def attend_backward(queries, key_rows, val_rows, visible, logsum, grad_out):
-
-    def one_pair(pieces):
-        q_pair, k_pair, v_pair, lse_pair, g_pair = pieces
-        scores = (
-            jnp.einsum("qhd,khd->hqk", q_pair, k_pair, preferred_element_type=jnp.float32) * 0.125
-        )
-        scores = jnp.where(visible[None], scores, -1e30)
-        weights = jnp.exp(scores - lse_pair[..., None])
-        grad_weights = jnp.einsum(
-            "qhd,khd->hqk", g_pair, v_pair, preferred_element_type=jnp.float32
-        )
-        row_dot = jnp.sum(weights * grad_weights, axis=-1, keepdims=True)
-        grad_scores = (weights * (grad_weights - row_dot)).astype(jnp.bfloat16)
-        grad_q = (
-            jnp.einsum("hqk,khd->qhd", grad_scores, k_pair, preferred_element_type=jnp.float32)
-            * 0.125
-        )
-        grad_k = (
-            jnp.einsum("hqk,qhd->khd", grad_scores, q_pair, preferred_element_type=jnp.float32)
-            * 0.125
-        )
-        grad_v = jnp.einsum(
-            "hqk,qhd->khd", weights.astype(jnp.bfloat16), g_pair, preferred_element_type=jnp.float32
-        )
-        return (grad_q, grad_k, grad_v)
-
-    results = lax.map(
-        one_pair,
-        (
-            head_pairs(queries),
-            head_pairs(key_rows),
-            head_pairs(val_rows),
-            logsum,
-            head_pairs(grad_out),
-        ),
-    )
-    return (merge_pairs(results[0]), merge_pairs(results[1]), merge_pairs(results[2]))
+        + tuple(gather.outs),
+        in_specs=[vmem] * 3 + [any_space] * len(gather.views),
+        out_specs=(vmem,) * 4 + (any_space,) * len(gather.views),
+        scratch_shapes=exchange.scratch + gather.scratch,
+        compiler_params=params(call_id, 56),
+    )(q, k, v, *gather.views)
+    return results[:4], gather.restore(results[4:])
+
+
+class Collect:
+    def __init__(self, depth, rows, pairs):
+        self.depth, self.rows, self.pairs = depth, rows, pairs
+        dma = pltpu.SemaphoreType.DMA
+        shape = (pairs, depth, 2, rows, PAIR)
+        self.scratch = [
+            pltpu.VMEM(shape, BF),
+            pltpu.VMEM(shape, BF),
+            pltpu.VMEM(shape, BF),
+            pltpu.VMEM((2, rows, PAIR), F32),
+            dma((2, pairs, depth)),
+            dma((2, pairs, depth)),
+        ]
+        self.steps = pairs + (depth - 1) * COLLECT_LAG + 1
+
+    def bind(self, scratch):
+        (self.part, self.from_left, self.from_right, self.whole, self.send_sem,
+         self.recv_sem) = scratch
+
+    def hop(self, p, zd, move):
+        z = lax.axis_index("fsdp")
+        target = self.from_left if move > 0 else self.from_right
+        way = (move + 1) // 2
+        return remote(self.part.at[p, zd], target.at[p, zd], self.send_sem.at[way, p, zd],
+                      self.recv_sem.at[way, p, zd], (lax.axis_index("dp"), z + move))
+
+    def flow(self, p, move):
+        depth = self.depth
+        z = lax.axis_index("fsdp")
+        first = z == 0 if move > 0 else z == depth - 1
+        arrived = self.from_left if move > 0 else self.from_right
+        for zd in range(depth - 1, -1, -1) if move > 0 else range(depth):
+            beyond = zd > z if move > 0 else zd < z
+
+            @pl.when(jnp.logical_and(jnp.logical_not(first), jnp.logical_or(beyond, zd == z)))
+            def _(zd=zd):
+                self.hop(p, zd, move).wait_recv()
+
+                def add(part, carry):
+                    self.part[p, zd, part] = self.part[p, zd, part] + arrived[p, zd, part]
+                    return carry
+
+                @pl.when(zd != z)
+                def _():
+                    lax.fori_loop(0, 2, add, 0)
+
+            @pl.when(beyond)
+            def _(zd=zd):
+                self.hop(p, zd, move).start()
+
+    def step(self, i):
+        depth = self.depth
+        z = lax.axis_index("fsdp")
+        for move in (1, -1):
+            stage = z if move > 0 else depth - 1 - z
+            p = i - stage * COLLECT_LAG
+
+            @pl.when(jnp.logical_and(p >= 0, p < self.pairs))
+            def _(p=p, move=move):
+                self.flow(p, move)
+
+    def result(self, p):
+        z = lax.axis_index("fsdp")
+        depth = self.depth
+        whole = self.whole
+        whole[...] = self.part[p, z].astype(F32)
+
+        @pl.when(z > 0)
+        def _():
+            whole[...] = whole[...] + self.from_left[p, z].astype(F32)
+
+        @pl.when(z < depth - 1)
+        def _():
+            whole[...] = whole[...] + self.from_right[p, z].astype(F32)
+
+        return whole[...]
+
+    def finish(self):
+        depth = self.depth
+        z = lax.axis_index("fsdp")
+
+        def drain(p, carry):
+            for zd in range(depth):
+                for move in (1, -1):
+                    @pl.when(zd > z if move > 0 else zd < z)
+                    def _(zd=zd, move=move):
+                        self.hop(p, zd, move).wait_send()
+            return carry
+
+        lax.fori_loop(0, self.pairs, drain, 0)
+
+
+def backward_kernel(plan, collect, *refs):
+    depth, rows, pairs = collect.depth, collect.rows, collect.pairs
+    n = len(plan.views)
+    ins, sources, (dq_ref, dk_ref, dv_ref), sums, swap, rest = split_refs(
+        refs, 8, n, 3, n, len(collect.scratch))
+    q_ref, k_ref, v_ref, keys, vals, lse_ref, att_ref, g_ref = ins
+    plan.bind(sources, sums, rest)
+    collect.bind(swap)
+    z = lax.axis_index("fsdp")
+    greet(plan.side, depth)
+    plan.start()
+    last = (depth - 1) * COLLECT_LAG
+
+    def run(i, carry):
+        @pl.when(i < pairs)
+        def _():
+            backward_pair(i, z, rows, depth, q_ref, k_ref, v_ref, keys, vals, lse_ref, att_ref,
+                          g_ref, dq_ref, dk_ref, dv_ref, collect.part)
+
+        collect.step(i)
+        plan.step(i)
+
+        @pl.when(jnp.logical_and(i >= last, i < last + pairs))
+        def _():
+            p = i - last
+            cols = pl.ds(pl.multiple_of(p * PAIR, PAIR), PAIR)
+            value = collect.result(p)
+            dk_ref[pl.ds(0, rows), cols] = value[0].astype(BF)
+            dv_ref[pl.ds(0, rows), cols] = value[1].astype(BF)
+
+        return carry
+
+    lax.fori_loop(0, max(pairs + last, plan.steps), run, 0)
+    collect.finish()
+    plan.finish()
+
+
+def attention_backward(side, depth, q, k, v, keys, vals, lse, att, grad_att, grads, call_id):
+    rows, width = q.shape[0] // 2, q.shape[1]
+    plan, collect = Reduce(side, depth, grads), Collect(depth, rows, width // PAIR)
+    vmem = pl.BlockSpec(memory_space=pltpu.VMEM)
+    results = pl.pallas_call(
+        functools.partial(backward_kernel, plan, collect),
+        out_shape=(jax.ShapeDtypeStruct(q.shape, BF),) * 3 + tuple(plan.outs),
+        in_specs=[vmem] * 8 + plan.in_specs,
+        out_specs=(vmem,) * 3 + tuple(plan.out_specs),
+        scratch_shapes=collect.scratch + plan.scratch,
+        compiler_params=params(call_id, 62),
+    )(q, k, v, keys, vals, lse, att, grad_att, *plan.views)
+    return results[:3], results[3:]
 
 
 def one_hot(ids, count):
@@ -162,12 +1032,8 @@
     table = lax.all_to_all(served, ALL, split_axis=0, concat_axis=0, tiled=True)
     table = table.reshape(owners, 2, capacity, width).transpose(1, 0, 2, 3).reshape(2, slots, width)
 
-    qkv_full = lax.all_gather(w_qkv, "fsdp", axis=1, tiled=True)
-    attn_out_full = lax.all_gather(w_attn_out, "fsdp", axis=0, tiled=True)
-    query_full = lax.all_gather(w_mem_query, "fsdp", axis=0, tiled=True)
-    keys_full = lax.all_gather(sub_keys, "fsdp", axis=0, tiled=True)
-    gate_full = lax.all_gather(w_gate, "fsdp", axis=0, tiled=True)
-    mem_out_full = lax.all_gather(w_mem_out, "fsdp", axis=0, tiled=True)
+    side, depth = grid_of(lax.axis_size("dp"), lax.axis_size("fsdp"))
+    (qkv_full,) = gather_weights(side, depth, (w_qkv,), 0)
 
     x_rows = jnp.concatenate([x_prompt[0], x_cont[0]], axis=0).astype(F32)
     dy_low = jnp.concatenate([cot_prompt[0], cot_cont[0]], axis=0)
@@ -176,22 +1042,16 @@
     queries = mm(normed, qkv_full[0]).astype(BF)
     keys = mm(normed, qkv_full[1]).astype(BF)
     vals = mm(normed, qkv_full[2]).astype(BF)
-    all_keys = lax.all_gather(keys[:rows], "fsdp", axis=0, tiled=True)
-    all_vals = lax.all_gather(vals[:rows], "fsdp", axis=0, tiled=True)
-    start_row = lax.axis_index("fsdp") * rows
-    visible_p = jnp.arange(PL)[None, :] <= start_row + jnp.arange(rows)[:, None]
-    att_p, logsum_p = attend_forward(queries[:rows], all_keys, all_vals, visible_p)
-    key_join = jnp.concatenate([all_keys, keys[rows:]], axis=0)
-    val_join = jnp.concatenate([all_vals, vals[rows:]], axis=0)
-    visible_c = jnp.concatenate(
-        [
-            jnp.ones((rows, PL), jnp.bool_),
-            jnp.arange(rows)[None, :] <= jnp.arange(rows)[:, None],
-        ],
-        axis=1,
-    )
-    att_c, logsum_c = attend_forward(queries[rows:], key_join, val_join, visible_c)
-    att = jnp.concatenate([att_p, att_c], axis=0)
+    (att, lse, all_keys, all_vals), full = attention_forward(
+        side,
+        depth,
+        queries,
+        keys,
+        vals,
+        (w_attn_out, w_mem_query, sub_keys, w_gate, w_mem_out),
+        1,
+    )
+    attn_out_full, query_full, keys_full, gate_full, mem_out_full = full
     hidden = x_rows + mm(att, attn_out_full)
     normed2, inverse2 = normalize(hidden, gain_mem)
     normed2 = normed2.astype(BF)
@@ -281,21 +1141,28 @@
     hidden_low = grad_hidden.astype(BF)
     grad_attn_out = mm_l(att, hidden_low)
     grad_att = mm_t(hidden_low, attn_out_full).astype(BF)
-    grad_q_p, grad_k_p, grad_v_p = attend_backward(
-        queries[:rows], all_keys, all_vals, visible_p, logsum_p, grad_att[:rows]
-    )
-    grad_q_c, grad_k_c, grad_v_c = attend_backward(
-        queries[rows:], key_join, val_join, visible_c, logsum_c, grad_att[rows:]
-    )
-    own_keys = lax.psum_scatter(
-        (grad_k_c[:PL] + grad_k_p).astype(BF), "fsdp", scatter_dimension=0, tiled=True
-    )
-    own_vals = lax.psum_scatter(
-        (grad_v_c[:PL] + grad_v_p).astype(BF), "fsdp", scatter_dimension=0, tiled=True
-    )
-    grad_q = jnp.concatenate([grad_q_p, grad_q_c], axis=0).astype(BF)
-    grad_k = jnp.concatenate([own_keys, grad_k_c[PL:].astype(BF)], axis=0)
-    grad_v = jnp.concatenate([own_vals, grad_v_c[PL:].astype(BF)], axis=0)
+    block = cols // owners
+    keys_low = grad_keys.astype(BF).reshape(owners, 2, block, HALF).transpose(0, 2, 1, 3)
+    (grad_q, grad_k, grad_v), early = attention_backward(
+        side,
+        depth,
+        queries,
+        keys,
+        vals,
+        all_keys,
+        all_vals,
+        lse,
+        att,
+        grad_att,
+        (
+            grad_query_w.astype(BF),
+            keys_low.reshape(cols, 2 * HALF),
+            grad_gate_w.astype(BF),
+            grad_mem_out.astype(BF),
+            grad_attn_out.astype(BF),
+        ),
+        2,
+    )
     grad_normed = (
         mm_t(grad_q, qkv_full[0]) + mm_t(grad_k, qkv_full[1]) + mm_t(grad_v, qkv_full[2])
     )
@@ -303,22 +1170,26 @@
     grad_x = grad_hidden + grad_x
     grad_qkv = jnp.stack([mm_l(normed, piece) for piece in (grad_q, grad_k, grad_v)])
 
-    def scatter(value, axis):
-        return lax.psum_scatter(value, ALL, scatter_dimension=axis, tiled=True)
-
+    gains = jnp.concatenate([gain_attn_part, gain_mem_part]).reshape(2 * cols // 128, 128)
+    qkv_shard, gain_sums = reduce_grads(side, depth, (grad_qkv.astype(BF),), gains, 3)
+    own = lax.axis_index("dp") * depth + lax.axis_index("fsdp")
+    gain_shards = lax.dynamic_index_in_dim(
+        gain_sums.reshape(2, owners, block), own, axis=1, keepdims=False
+    )
+    sub_shard = early[1].reshape(block, 2, HALF).transpose(1, 0, 2).reshape(2 * block, HALF)
     return (
         out[None, :rows],
         out[None, rows:],
         grad_x[None, :rows],
         grad_x[None, rows:],
-        scatter(gain_attn_part, 0),
-        scatter(gain_mem_part, 0),
-        scatter(grad_qkv.astype(BF), 1).astype(F32),
-        scatter(grad_attn_out.astype(BF), 0).astype(F32),
-        scatter(grad_query_w.astype(BF), 0).astype(F32),
-        scatter(grad_keys.astype(BF), 0).astype(F32),
-        scatter(grad_gate_w.astype(BF), 0).astype(F32),
-        scatter(grad_mem_out.astype(BF), 0).astype(F32),
+        gain_shards[0],
+        gain_shards[1],
+        qkv_shard,
+        early[4],
+        early[0],
+        sub_shard,
+        early[2],
+        early[3],
         grad_rows,
     )
 

time: 1880 us -> 660 us (0.35)
  waiting for transfers between devices: 1180 us -> 1.82 us
  Pallas kernels: 0 us -> 344 us
  matrix products: 395 us -> 153 us
  other arithmetic: 113 us -> 65.3 us
  blocking collectives: 43 us -> 0 us
  local copies, waits for them, and re-layouts: 106 us -> 70 us
    reduce_scatter x8 -> x0, waiting for transfers between devices: 789 us -> none  [the longest x6 750 us: scatter(): return lax.psum_scatter(value, ALL, scatter_dimension=axis, tiled=True)]
    pallas_call x0 -> x4, Pallas kernels: none -> 344 us  [the longest x1 128 us: attention_forward(): pl.pallas_call(functools.partial(forward_kernel, gather, exchange), out_s...]
    all_gather x8 -> x0, waiting for transfers between devices: 288 us -> none  [the longest x1 118 us: per_device(): qkv_full = lax.all_gather(w_qkv, 'fsdp', axis=1, tiled=True)]
    dot_general x112 -> x0, matrix products: 219 us -> none  [the longest x32 60.4 us: one_pair(): jnp.einsum('qhd,khd->hqk', q_pair, k_pair, preferred_element_type=jnp.flo...]
    all_to_all x1, waiting for transfers between devices: 56.1 us -> 0.01 us  [per_device(): lax.all_to_all(jnp.stack([piece.reshape(owners, capacity, width) for piec...]
    unnamed x1 -> x0, blocking collectives: 43 us -> none
    all_to_all x1, waiting for transfers between devices: 41.9 us -> 1.82 us  [per_device(): table = lax.all_to_all(served, ALL, split_axis=0, concat_axis=0, tiled=True)]
    convert_element_type x24 -> x0, other arithmetic: 24.9 us -> none  [the longest x1 5.5 us: per_device(): (grad_v_c[:PL] + grad_v_p).astype(BF)]
  transfers between devices with their start and end apart: 19 -> 3, of which waited for: 13 -> 1; matrix products, arithmetic and copies ran while one was open for 18% -> 24% of each run, Pallas kernels for 0% -> 34%
where the time goes in v3:
time: 660 us; the launch traced here: 651 us
  Pallas kernels  344 us (52%)
  matrix products  153 us (23%)
  local copies, waits for them, and re-layouts  70 us (11%)
  other arithmetic  65.3 us (10%)
  starting transfers between devices  15 us (2%)
    pallas_call x1, Pallas kernels, attention_forward(): pl.pallas_call(functools.partial(forward_kernel, gather, exchange), out_s...  128 us
    pallas_call x1, Pallas kernels, attention_backward(): pl.pallas_call(functools.partial(backward_kernel, plan, collect), out_sha...  121 us
    dot_general x42, matrix products, mm(): return jnp.dot(left, right, preferred_element_type=F32)  83.7 us
    pallas_call x1, Pallas kernels, reduce_grads(): pl.pallas_call(functools.partial(reduce_kernel, plan), out_shape=tuple(pl...  58.3 us
    pallas_call x1, Pallas kernels, gather_weights(): pl.pallas_call(functools.partial(gather_kernel, plan), out_shape=tuple(pl...  36.2 us
    dot_general x18, matrix products, mm_l(): lax.dot_general(left, right, (((0,), (0,)), ((), ())), preferred_element_...  34.9 us
    reduce_sum x2, other arithmetic, pick_weights(): jnp.sum((slot_ids[..., None] == jnp.arange(slots, dtype=jnp.int32)).astyp...  34.8 us
    dot_general x17, matrix products, mm_t(): lax.dot_general(left, right, (((1,), (1,)), ((), ())), preferred_element_...  33.9 us
  transfers between devices with their start and end apart: 3, of which 1 were waited for; matrix products, arithmetic and copies ran while one was open for 24% of the time, Pallas kernels for 34%

profile of v3, /device:TPU:0, one launch (start us, length us, event | category | flops | bytes accessed | tf_op | source)
XLA Modules:
  0.0 650.9 jit_solution(14849293848550329316)
XLA Ops:
  2.1 7.3 %all-to-all-start = ((s32[2,32,16]{2,0,1:T(2,128)}), s32[2,32,16]{2,0,1:T(2,128)S(1)}, u32[]{:S(2)}, u32[]{:S(2)}) async-start(s32[2,32,16]{2,0,1:T(2,128)} %bitcast.28), calls=%async_computation | async-start | bytes 65536 | tf_op jit(solution)/shard_map/all_to_all | solution.py:1029
  11.5 36.2 %shard_map.255 = bf16[3,4,2,2,2,32,1024]{6,5,4,3,2,1,0:T(8,128)(2,1)S(1)} custom-call(bf16[3,2,2,2,32,1024]{5,4,3,2,1,0:T(8,128)(2,1)S(1)} %bitcast.198), custom_call_target="tpu_custom_call" | custom-call | tf_op jit(solution)/shard_map/pallas_call | solution.py:565
  57.4 128.1 %shard_map.256 = (bf16[512,1024]{1,0:T(8,128)(2,1)}, f32[16,512]{1,0:T(8,128)}, bf16[8,4,256,128]{3,2,1,0:T(8,128)(2,1)}, bf16[8,4,256,128]{3,2,1,0:T(8,128)(2,1...) custom-call(bf16[512,1024]{1,0:T(8,128)(2,1)} %convolution_convert_f, ...), custom_call_target="tpu_custom_call" | custom-call | tf_op jit(solution)/shard_map/pallas_call | solution.py:825
  202.4 17.4 %convert_reduce_fusion.1 = f32[256,4,512]{2,1,0:T(4,128)S(1)} fusion(s32[256,4,32]{2,1,0:T(4,128)S(1)} %copy.79), kind=kLoop, calls=%fused_computation.2 | loop fusion | flops 49807360 | bytes 2228224 | tf_op jit(solution)/shard_map/reduce_sum | solution.py:997
  220.1 17.4 %convert_reduce_fusion = f32[256,4,512]{2,1,0:T(4,128)S(1)} fusion(s32[256,4,32]{2,1,0:T(4,128)S(1)} %copy.84), kind=kLoop, calls=%fused_computation | loop fusion | flops 49807360 | bytes 2228224 | tf_op jit(solution)/shard_map/reduce_sum | solution.py:997
  237.8 19.2 %convolution_convert_fusion.1 = bf16[512,4096]{1,0:T(8,128)(2,1)S(1)} fusion(bf16[512,1024]{1,0:T(8,128)(2,1)S(1)} %multiply_convert_fusion.3, bf16[1024,4096]{1,0:T(8,128)(2,1)} %bitcast.287), kind=kOutput, calls=%fused_computation.9 | convolution fusion | flops 4297064448 | bytes 13631488 | tf_op jit(solution)/shard_map/dot_general | solution.py:26
  266.3 8.0 %fusion.13 = bf16[1024,1024]{1,0:T(8,128)(2,1)} fusion(bf16[2048,1024]{1,0:T(8,128)(2,1)} %param.28, s32[1024]{0:T(1024)S(1)} %eq.110), kind=kOutput, calls=%fused_computation.56 | convolution fusion | flops 4298113024 | bytes 6295552 | tf_op jit(solution)/shard_map/dot_general | solution.py:26
  274.3 3.5 all-to-all-start.1
  280.4 2.9 reduce_sum.140
  283.3 4.2 copy.94
  287.6 2.9 stack.67
  304.2 5.4 fusion.145
  310.0 2.9 copy.87
  316.4 3.0 fusion.150
  320.7 2.8 multiply_convert_fusion.1
  331.9 3.3 multiply_subtract_fusion
  342.1 2.9 mul.268
  346.6 3.7 multiply_subtract_fusion.1
  363.3 4.0 fusion.23
  379.6 7.1 %fusion.151 = f32[512,1024]{1,0:T(8,128)S(1)} fusion(bf16[512,4096]{0,1:T(8,128)(2,1)S(1)} %fusion.21, bf16[1024,4096]{1,0:T(8,128)(2,1)} %bitcast.288), kind=kOutput, calls=%fused_computation.302 | convolution fusion | flops 4294967296 | bytes 14680064 | tf_op jit(solution)/shard_map/dot_general | solution.py:30
  386.8 7.0 %convolution_convert_fusion = bf16[1024,4096]{1,0:T(8,128)(2,1)} fusion(bf16[512,1024]{1,0:T(8,128)(2,1)S(1)} %copy-done.49, bf16[512,4096]{0,1:T(8,128)(2,1)S(1)} %fusion.21), kind=kOutput, calls=%fused_computation.7 | convolution fusion | flops 4299161600 | bytes 13631488 | tf_op jit(solution)/shard_map/dot_general | solution.py:34
  399.8 2.7 convolution_convert_fusion.7
  417.2 3.0 reshape_reshape.7.refs_9_
  420.2 4.1 convolution_convert_fusion.6
  424.3 121.2 %shard_map.257 = (bf16[512,1024]{1,0:T(8,128)(2,1)}, bf16[512,1024]{1,0:T(8,128)(2,1)}, bf16[512,1024]{1,0:T(8,128)(2,1)}, f32[32,4096]{1,0:T(8,128)}, f32[32,10...) custom-call(bf16[512,1024]{1,0:T(8,128)(2,1)} %convolution_convert_fusion.13.refs_0_, ...), custom_call_target="tpu_custom_call" | custom-call | tf_op jit(solution)/shard_map/pallas_call | solution.py:975
  545.5 4.6 fusion.152
  551.7 4.3 all-to-all-start.2
  559.2 3.1 fusion.12
  567.2 3.4 pad_maximum_fusion.refs_0_
  570.6 58.3 %shard_map.258 = (f32[3,32,1024]{2,1,0:T(8,128)}, f32[16,128]{1,0:T(8,128)}) custom-call(bf16[3,2,2,2,4,32,1024]{6,5,4,3,2,1,0:T(8,128)(2,1)} %pad_maximum_fusion.refs_0_, f32[16,128]{1,0:T(8,128)} %pad_maximum_fusion.9.refs_1_), custom_call_target="tpu_custom_call" | custom-call | tf_op jit(solution)/shard_map/pallas_call | solution.py:593
  631.0 3.3 add_convert_fusion
  638.3 8.6 %fusion = f32[2048,1024]{1,0:T(8,128)} fusion(bf16[1024,1024]{1,0:T(8,128)(2,1)} %bitcast.77, s32[1024]{0:T(1024)S(1)} %copy-done.80), kind=kOutput, calls=%fused_computation.5 | convolution fusion | flops 4297064448 | bytes 10489856 | tf_op jit(solution)/shard_map/dot_general | solution.py:34
  (314 shorter events, 142.5 us)
Async XLA Ops:
  2.1 264.1 %all-to-all-start = ((s32[2,32,16]{2,0,1:T(2,128)}), s32[2,32,16]{2,0,1:T(2,128)S(1)}, u32[]{:S(2)}, u32[]{:S(2)}) async-start(s32[2,32,16]{2,0,1:T(2,128)} %bitcast.28), calls=%async_computation | async-start | bytes 65536 | tf_op jit(solution)/shard_map/all_to_all | solution.py:1029
  49.1 5.7 copy-start.28
  50.3 4.6 copy-start.74
  185.4 5.9 copy-start.9
  191.4 6.3 copy-start.45
  191.4 6.3 copy-start.82
  197.7 4.5 copy-start.63
  200.3 19.5 %copy-start.64 = (s32[1,256,4,32]{1,3,2,0:T(8,128)S(1)}, s32[1,256,4,32]{1,3,2,0:T(8,128)}, u32[]{:S(2)}) copy-start(s32[1,256,4,32]{1,3,2,0:T(8,128)} %param.31) | copy-start | bytes 393220
  200.9 36.6 %copy-start.71 = (f32[512]{0:T(512)}, f32[512]{0:T(512)S(1)}, u32[]{:S(2)}) copy-start(f32[512]{0:T(512)S(1)} %get-tuple-element.85) | copy-start | bytes 6148
  219.8 17.7 %copy-start.69 = (f32[1024]{0:T(1024)S(1)}, f32[1024]{0:T(1024)}, u32[]{:S(2)}) copy-start(f32[1024]{0:T(1024)} %param.21) | copy-start | bytes 12292
  220.1 17.4 %copy-start.4 = (f32[512,1024]{1,0:T(8,128)S(1)}, f32[512,1024]{1,0:T(8,128)}, u32[]{:S(2)}) copy-start(f32[512,1024]{1,0:T(8,128)} %get-tuple-element.91) | copy-start | bytes 6291460
  237.5 24.4 %copy-start.3 = (f32[256,4,512]{2,1,0:T(4,128)}, f32[256,4,512]{2,1,0:T(4,128)S(1)}, u32[]{:S(2)}) copy-start(f32[256,4,512]{2,1,0:T(4,128)S(1)} %convert_reduce_fusion) | copy-start | bytes 6291460
  237.7 19.2 %copy-start.47 = (bf16[512,1024]{1,0:T(8,128)(2,1)}, bf16[512,1024]{1,0:T(8,128)(2,1)S(1)}, u32[]{:S(2)}) copy-start(bf16[512,1024]{1,0:T(8,128)(2,1)S(1)} %multiply_convert_fusion.3) | copy-start | bytes 3145732
  237.8 19.2 %copy-start.60 = (bf16[512,512]{0,1:T(8,128)(2,1)S(1)}, bf16[512,512]{0,1:T(8,128)(2,1)}, u32[]{:S(2)}) copy-start(bf16[512,512]{0,1:T(8,128)(2,1)} %convolution_convert_fusion.23) | copy-start | bytes 1572868
  266.3 8.1 %copy-start.79 = (s32[1024]{0:T(1024)}, s32[1024]{0:T(1024)S(1)}, u32[]{:S(2)}) copy-start(s32[1024]{0:T(1024)S(1)} %eq.110) | copy-start | bytes 12292
  274.3 51.0 %all-to-all-start.1 = ((bf16[32,32,1024]{2,1,0:T(8,128)(2,1)}), bf16[32,32,1024]{2,1,0:T(8,128)(2,1)}, u32[]{:S(2)}, u32[]{:S(2)}) async-start(bf16[32,32,1024]{2,1,0:T(8,128)(2,1)} %bitcast.257), calls=%async_computation.1 | async-start | bytes 4194304 | tf_op jit(solution)/shard_map/all_to_all | solution.py:1032
  292.4 4.4 copy-start.10
  296.8 4.8 copy-start.39
  316.4 4.3 copy-start.50
  316.4 4.3 copy-start.52
  316.4 4.3 copy-start.81
  363.3 7.9 %copy-start.2 = (f32[1024,512]{1,0:T(8,128)S(1)}, f32[1024,512]{1,0:T(8,128)}, u32[]{:S(2)}) copy-start(f32[1024,512]{1,0:T(8,128)} %copy-done.1) | copy-start | bytes 6291460
  379.6 7.2 %copy-start.49 = (bf16[512,1024]{1,0:T(8,128)(2,1)S(1)}, bf16[512,1024]{1,0:T(8,128)(2,1)}, u32[]{:S(2)}) copy-start(bf16[512,1024]{1,0:T(8,128)(2,1)} %copy-done.47) | copy-start | bytes 3145732
  408.1 4.6 copy-start.89
  545.5 4.6 copy-start.20
  551.7 86.6 %all-to-all-start.2 = ((bf16[32,2,16,1024]{3,2,1,0:T(8,128)(2,1)}), bf16[32,2,16,1024]{3,2,1,0:T(8,128)(2,1)}, u32[]{:S(2)}, u32[]{:S(2)}) async-start(bf16[32,2,16,1024]{3,2,1,0:T(8,128)(2,1)} %pad_maximum_fusion.4), calls=%async_computation.2 | async-start | bytes 4194304 | tf_op jit(solution)/shard_map/all_to_all | solution.py:1128
  570.6 59.1 %copy-start.68 = (f32[32,1024]{1,0:T(8,128)S(1)}, f32[32,1024]{1,0:T(8,128)}, u32[]{:S(2)}) copy-start(f32[32,1024]{1,0:T(8,128)} %get-tuple-element.48) | copy-start | bytes 393220
  570.6 60.4 %copy-start.6 = (f32[512,1024]{1,0:T(8,128)S(1)}, f32[512,1024]{1,0:T(8,128)}, u32[]{:S(2)}) copy-start(f32[512,1024]{1,0:T(8,128)} %get-tuple-element.91) | copy-start | bytes 6291460
  631.0 4.4 copy-start.23
  638.3 8.7 %copy-start.62 = (f32[3,32,1024]{2,1,0:T(8,128)S(1)}, f32[3,32,1024]{2,1,0:T(8,128)}, u32[]{:S(2)}) copy-start(f32[3,32,1024]{2,1,0:T(8,128)} %get-tuple-element.117) | copy-start | bytes 1179652
  638.3 9.4 %copy-start.67 = (f32[32,1024]{1,0:T(8,128)S(1)}, f32[32,1024]{1,0:T(8,128)}, u32[]{:S(2)}) copy-start(f32[32,1024]{1,0:T(8,128)} %get-tuple-element.118) | copy-start | bytes 393220
  638.3 10.1 %copy-start.61 = (f32[32,4096]{1,0:T(8,128)S(1)}, f32[32,4096]{1,0:T(8,128)}, u32[]{:S(2)}) copy-start(f32[32,4096]{1,0:T(8,128)} %get-tuple-element.119) | copy-start | bytes 1572868
  (61 other events, 132.0 us)

commit v4 on v3

--- a/solution.py
+++ b/solution.py
@@ -11,8 +11,10 @@
 MESH = pl.DeviceIdType.MESH
 LAG = 2
 GATHER_LAG = 2
+GATHER_RATE = 1
 COLLECT_LAG = 2
 AHEAD = 3
+HOP_LAG = 1
 PIECE = 1024
 PAIR = 128
 HDIM = 64
@@ -548,29 +550,43 @@
     )
 
 
-def gather_kernel(plan, *refs):
+def gather_kernel(plan, slots, rows, *refs):
     n = len(plan.views)
-    sources, outs, scratch = split_refs(refs, n, n)
+    (picks_ref,), sources, (counts_ref,), outs, scratch = split_refs(refs, 1, n, 1, n)
     plan.bind(sources, outs, scratch)
+    blocks = picks_ref.shape[1] // 128
+    turns = max(plan.steps, blocks)
     greet(plan.side, plan.depth)
     plan.start()
-    for i in range(plan.steps):
-        plan.step(i)
+
+    def run(i, carry):
+        for number in range(plan.steps):
+            @pl.when(i == number)
+            def _(number=number):
+                plan.step(number)
+
+        @pl.when(i < blocks)
+        def _():
+            count_block(i, rows, slots, picks_ref, counts_ref)
+
+        return carry
+
+    lax.fori_loop(0, turns, run, 0)
     plan.finish()
 
 
-def gather_weights(side, depth, shards, call_id):
+def gather_and_count(side, depth, shards, picks, slots, rows, call_id):
     plan = Gather(side, depth, shards)
-    any_space = pl.BlockSpec(memory_space=pl.ANY)
-    full = pl.pallas_call(
-        functools.partial(gather_kernel, plan),
-        out_shape=tuple(plan.outs),
-        in_specs=[any_space] * len(plan.views),
-        out_specs=(any_space,) * len(plan.views),
+    any_space, vmem = pl.BlockSpec(memory_space=pl.ANY), pl.BlockSpec(memory_space=pltpu.VMEM)
+    results = pl.pallas_call(
+        functools.partial(gather_kernel, plan, slots, rows),
+        out_shape=(jax.ShapeDtypeStruct((2, MH, slots, rows), BF),) + tuple(plan.outs),
+        in_specs=[vmem] + [any_space] * len(plan.views),
+        out_specs=(vmem,) + (any_space,) * len(plan.views),
         scratch_shapes=plan.scratch,
         compiler_params=params(call_id, 32),
-    )(*plan.views)
-    return plan.restore(full)
+    )(picks, *plan.views)
+    return results[0], plan.restore(results[1:])
 
 
 def reduce_kernel(plan, *refs):
@@ -743,7 +759,7 @@
     def step(self, i):
         z = lax.axis_index("fsdp")
         for distance in range(1, self.depth):
-            p = i - (distance - 1)
+            p = i - (distance - 1) * HOP_LAG
             for sign in (1, -1):
                 zp = z + sign * distance
                 seen = jnp.logical_and(zp >= 0, zp < self.depth)
@@ -789,7 +805,8 @@
     for p in range(ahead):
         exchange.offer(p)
     gather.start()
-    turns = pairs + depth - 1
+    delay = (depth - 2) * HOP_LAG + 1
+    turns = pairs + delay
 
     def run(i, carry):
         @pl.when(i + ahead < pairs)
@@ -797,20 +814,21 @@
             exchange.offer(i + ahead)
 
         exchange.step(i)
-        for number in range(min(turns, gather.steps)):
-            @pl.when(i == number)
-            def _(number=number):
-                gather.step(number)
-
-        @pl.when(i >= depth - 1)
+        for turn in range(turns):
+            @pl.when(i == turn)
+            def _(turn=turn):
+                for number in range(turn * GATHER_RATE, min((turn + 1) * GATHER_RATE, gather.steps)):
+                    gather.step(number)
+
+        @pl.when(i >= delay)
         def _():
-            forward_pair(i - (depth - 1), z, rows, depth, q_ref, k_ref, v_ref, keys, vals, att_ref,
+            forward_pair(i - delay, z, rows, depth, q_ref, k_ref, v_ref, keys, vals, att_ref,
                          lse_ref)
 
         return carry
 
     lax.fori_loop(0, turns, run, 0)
-    for number in range(turns, gather.steps):
+    for number in range(turns * GATHER_RATE, gather.steps):
         gather.step(number)
     exchange.finish()
     gather.finish()
@@ -983,24 +1001,162 @@
     return results[:3], results[3:]
 
 
+def count_block(b, rows, slots, picks_ref, counts_ref):
+    low, per_word, bits = 16, 5, 6
+    groups = -(-(slots // low) // per_word)
+    per_head = rows // 128
+    cols = pl.ds(pl.multiple_of(b * 128, 128), 128)
+    picks = picks_ref[:, cols]
+    high = jnp.right_shift(picks, 4)
+    group = jnp.right_shift(high * 13, 6)
+    word = group * low + jnp.bitwise_and(picks, low - 1)
+    unit = jnp.left_shift(jnp.ones_like(picks), bits * (high - per_word * group))
+    spot = lax.broadcasted_iota(jnp.int32, (groups * low, 128), 0)
+    words = jnp.zeros((groups * low, 128), jnp.int32)
+    for pick in range(picks.shape[0]):
+        words = words + jnp.where(spot == word[pick : pick + 1], unit[pick : pick + 1], 0)
+    part, head = b // (per_head * MH), (b // per_head) % MH
+    lanes = pl.ds(pl.multiple_of((b % per_head) * 128, 128), 128)
+    for tile in range(slots // low):
+        piece = words[(tile // per_word) * low : (tile // per_word + 1) * low]
+        count = jnp.bitwise_and(jnp.right_shift(piece, bits * (tile % per_word)), 2**bits - 1)
+        counts_ref[part, head, pl.ds(tile * low, low), lanes] = count.astype(F32).astype(BF)
+
+
+def selector(ids_ref, index, count):
+    ids = ids_ref[pl.ds(index, 1), :]
+    spot = lax.broadcasted_iota(jnp.int32, (count, ids.shape[1]), 0)
+    return jnp.where(spot == ids, 1.0, 0.0).astype(BF)
+
+
+def picks_kernel(ids_ref, counts_ref, query_ref, keys_ref, weight_ref, mixing_ref, total):
+    part, head = pl.program_id(0), pl.program_id(1)
+    scores = None
+    for half in range(2):
+        pick = selector(ids_ref, 2 * part + half, SUB)
+        slot_keys = dot_first(pick, keys_ref[half * SUB : (half + 1) * SUB]).astype(BF)
+        piece = dot_rows(slot_keys, query_ref[:, half * HALF : (half + 1) * HALF])
+        scores = piece if scores is None else scores + piece
+    count = counts_ref[0, 0].astype(F32)
+    named = count > 0.0
+    top = jnp.max(jnp.where(named, scores, -jnp.inf), axis=0, keepdims=True)
+    raised = jnp.where(named, count * jnp.exp(scores - top), 0.0)
+    weight = raised / jnp.sum(raised, axis=0, keepdims=True)
+    weight_ref[0, 0] = weight
+
+    @pl.when(head == 0)
+    def _():
+        total[...] = weight
+
+    @pl.when(head > 0)
+    def _():
+        total[...] = total[...] + weight
+
+    @pl.when(head == MH - 1)
+    def _():
+        mixing_ref[0] = total[...].astype(BF)
+
+
+def slot_weights(ids, counts, mquery, keys_full):
+    slots, rows = counts.shape[2:]
+    return pl.pallas_call(
+        picks_kernel,
+        grid=(2, MH),
+        out_shape=(
+            jax.ShapeDtypeStruct(counts.shape, F32),
+            jax.ShapeDtypeStruct((2, slots, rows), BF),
+        ),
+        in_specs=[
+            pl.BlockSpec(ids.shape, lambda u, m: (0, 0)),
+            pl.BlockSpec((1, 1, slots, rows), lambda u, m: (u, m, 0, 0)),
+            pl.BlockSpec((rows, 2 * HALF), lambda u, m: (u, m)),
+            pl.BlockSpec((2 * SUB, HALF), lambda u, m: (m, 0)),
+        ],
+        out_specs=(
+            pl.BlockSpec((1, 1, slots, rows), lambda u, m: (u, m, 0, 0)),
+            pl.BlockSpec((1, slots, rows), lambda u, m: (u, 0, 0)),
+        ),
+        scratch_shapes=[pltpu.VMEM((slots, rows), F32)],
+        cost_estimate=pl.CostEstimate(
+            flops=2 * 2 * MH * slots * 2 * HALF * (SUB + rows),
+            bytes_accessed=24 * 2**20,
+            transcendentals=2 * MH * slots * rows,
+        ),
+    )(ids, counts, mquery, keys_full)
+
+
+def picks_back_kernel(block, ids_ref, weight_ref, table_ref, memory_ref, query_ref, keys_ref,
+                      grad_query_ref, grad_keys_ref, grad_mixing, total):
+    head, part = pl.program_id(0), pl.program_id(1)
+
+    @pl.when(head == 0)
+    def _():
+        grad_mixing[part] = dot_rows(table_ref[0], memory_ref[...])
+
+    weight = weight_ref[0, 0]
+    pulled = weight * grad_mixing[part]
+    grad = pulled - weight * jnp.sum(pulled, axis=0, keepdims=True)
+    high = grad.astype(BF)
+    low = (grad - high.astype(F32)).astype(BF)
+    for half in range(2):
+        pick = selector(ids_ref, 2 * part + half, SUB)
+        sub = (dot_plain(pick, high) + dot_plain(pick, low)).astype(BF)
+        span = slice(half * HALF, (half + 1) * HALF)
+        keys = keys_ref[half * SUB : (half + 1) * SUB]
+        grad_query_ref[:, span] = dot_first(sub, keys).astype(BF)
+        piece = dot_plain(sub, query_ref[:, span])
+        rows = slice(half * SUB, (half + 1) * SUB)
+
+        @pl.when(part == 0)
+        def _(piece=piece, rows=rows):
+            total[rows] = piece
+
+        @pl.when(part == 1)
+        def _(piece=piece, rows=rows):
+            total[rows] = total[rows] + piece
+
+    @pl.when(part == 1)
+    def _():
+        for shard in range(SUB // block):
+            for side in range(2):
+                start = (2 * shard + side) * block
+                grad_keys_ref[shard * block : (shard + 1) * block, side * HALF : (side + 1) * HALF] = (
+                    total[start : start + block].astype(BF))
+
+
+def slot_weights_back(ids, weights, table, grad_memory, mquery, keys_full, block):
+    slots, rows = weights.shape[2:]
+    width = table.shape[2]
+    return pl.pallas_call(
+        functools.partial(picks_back_kernel, block),
+        grid=(MH, 2),
+        out_shape=(
+            jax.ShapeDtypeStruct(mquery.shape, BF),
+            jax.ShapeDtypeStruct((MH * SUB, 2 * HALF), BF),
+        ),
+        in_specs=[
+            pl.BlockSpec(ids.shape, lambda m, u: (0, 0)),
+            pl.BlockSpec((1, 1, slots, rows), lambda m, u: (u, m, 0, 0)),
+            pl.BlockSpec((1, slots, width), lambda m, u: (jnp.where(m == 0, u, 1), 0, 0)),
+            pl.BlockSpec((rows, width), lambda m, u: (jnp.where(m == 0, u, 1), 0)),
+            pl.BlockSpec((rows, 2 * HALF), lambda m, u: (u, m)),
+            pl.BlockSpec((2 * SUB, HALF), lambda m, u: (m, 0)),
+        ],
+        out_specs=(
+            pl.BlockSpec((rows, 2 * HALF), lambda m, u: (u, m)),
+            pl.BlockSpec((SUB, 2 * HALF), lambda m, u: (m, 0)),
+        ),
+        scratch_shapes=[pltpu.VMEM((2, slots, rows), F32), pltpu.VMEM((2 * SUB, HALF), F32)],
+        cost_estimate=pl.CostEstimate(
+            flops=2 * 2 * MH * slots * rows * (4 * SUB + 4 * HALF),
+            bytes_accessed=24 * 2**20,
+            transcendentals=0,
+        ),
+    )(ids, weights, table, grad_memory, mquery, keys_full)
+
+
 def one_hot(ids, count):
     return (ids[:, None] == jnp.arange(count, dtype=jnp.int32)[None, :]).astype(BF)
-
-
-def split_low(value):
-    high = value.astype(BF)
-    return (high, (value - high.astype(F32)).astype(BF))
-
-
-def pick_weights(slot_ids, scores):
-    slots = scores.shape[-1]
-    count = jnp.sum(
-        (slot_ids[..., None] == jnp.arange(slots, dtype=jnp.int32)).astype(F32), axis=2
-    )
-    named = count > 0.0
-    top = jnp.max(jnp.where(named, scores, -jnp.inf), axis=-1, keepdims=True)
-    raised = jnp.where(named, count * jnp.exp(scores - top), 0.0)
-    return raised / jnp.sum(raised, axis=-1, keepdims=True)
 
 
 def per_device(
@@ -1026,14 +1182,21 @@
     slots = owners * capacity
     rows = x_prompt.shape[1]
     cols = w_qkv.shape[2]
+    block = cols // owners
+    side, depth = grid_of(lax.axis_size("dp"), lax.axis_size("fsdp"))
+
     asked = lax.all_to_all(request[:, 0], ALL, split_axis=1, concat_axis=1, tiled=True)
     serve_pick = one_hot(asked.transpose(1, 0, 2).reshape(-1), shard_rows)
     served = mm(serve_pick, value_rows).astype(BF).reshape(owners, 2 * capacity, width)
     table = lax.all_to_all(served, ALL, split_axis=0, concat_axis=0, tiled=True)
     table = table.reshape(owners, 2, capacity, width).transpose(1, 0, 2, 3).reshape(2, slots, width)
-
-    side, depth = grid_of(lax.axis_size("dp"), lax.axis_size("fsdp"))
-    (qkv_full,) = gather_weights(side, depth, (w_qkv,), 0)
+    offsets = jnp.maximum(request[:, 0].reshape(2, slots), 0)
+    picked = (jnp.arange(slots, dtype=jnp.int32) // capacity)[None] * shard_rows + offsets
+    ids = jnp.stack([picked // SUB, picked % SUB], axis=1).reshape(4, slots)
+    picks = jnp.stack([slot_prompt[0], slot_cont[0]]).transpose(3, 0, 2, 1)
+    counts, (qkv_full,) = gather_and_count(
+        side, depth, (w_qkv,), picks.reshape(picks.shape[0], -1), slots, rows, 0
+    )
 
     x_rows = jnp.concatenate([x_prompt[0], x_cont[0]], axis=0).astype(F32)
     dy_low = jnp.concatenate([cot_prompt[0], cot_cont[0]], axis=0)
@@ -1058,30 +1221,8 @@
 
     mquery = mm(normed2, query_full).astype(BF)
     gate_pre = mm(normed2, gate_full)
-    key_heads = keys_full.reshape(MH, 2, SUB, HALF)
-    offsets = jnp.maximum(request[:, 0].reshape(2, slots), 0)
-    picked = (jnp.arange(slots, dtype=jnp.int32) // capacity)[None] * shard_rows + offsets
-    slot_ids = (slot_prompt[0], slot_cont[0])
-    first, second, weights, mixing, memory_out = [], [], [], [], []
-    for part in range(2):
-        first.append(one_hot(picked[part] // SUB, SUB))
-        second.append(one_hot(picked[part] % SUB, SUB))
-        section = slice(part * rows, (part + 1) * rows)
-        heads = []
-        for head in range(MH):
-            slot_keys = jnp.concatenate(
-                [
-                    mm(first[part], key_heads[head, 0]).astype(BF),
-                    mm(second[part], key_heads[head, 1]).astype(BF),
-                ],
-                axis=1,
-            )
-            span = slice(head * 2 * HALF, (head + 1) * 2 * HALF)
-            heads.append(mm_t(mquery[section, span], slot_keys))
-        weights.append(pick_weights(slot_ids[part], jnp.stack(heads, axis=1)))
-        mixing.append(jnp.sum(weights[part], axis=1).astype(BF))
-        memory_out.append(mm(mixing[part], table[part]))
-    memory_out = jnp.concatenate(memory_out, axis=0)
+    weights, mixing = slot_weights(ids, counts, mquery, keys_full)
+    memory_out = jnp.concatenate([mm_l(mixing[part], table[part]) for part in range(2)], axis=0)
     sigmoid_gate = jax.nn.sigmoid(gate_pre)
     blended = (memory_out * (gate_pre * sigmoid_gate)).astype(BF)
     out = (hidden + mm(blended, mem_out_full)).astype(BF)
@@ -1092,39 +1233,10 @@
     grad_gate = (
         grad_blend * memory_out * sigmoid_gate * (1.0 + gate_pre * (1.0 - sigmoid_gate))
     ).astype(BF)
-    slot_grads, grad_query, sub_grads = [], [], []
-    for part in range(2):
-        section = slice(part * rows, (part + 1) * rows)
-        slot_grads.append(mm_l(mixing[part], grad_memory[section]).astype(BF))
-        grad_mixing = mm_t(grad_memory[section], table[part])[:, None, :]
-        pulled = weights[part] * grad_mixing
-        grad_scores = pulled - weights[part] * jnp.sum(pulled, axis=-1, keepdims=True)
-        high, low = split_low(grad_scores.reshape(rows * MH, slots))
-        halves = [
-            (mm(high, picker) + mm(low, picker)).astype(BF).reshape(rows, MH, SUB)
-            for picker in (first[part], second[part])
-        ]
-        sub_grads.append(jnp.stack(halves, axis=2))
-    sub_grads = jnp.concatenate(sub_grads, axis=0)
-    grad_query = jnp.concatenate(
-        [
-            mm(sub_grads[:, head, half], key_heads[head, half]).astype(BF)
-            for head in range(MH)
-            for half in range(2)
-        ],
-        axis=1,
-    )
-    grad_keys = jnp.concatenate(
-        [
-            mm_l(
-                sub_grads[:, head, half],
-                mquery[:, (2 * head + half) * HALF : (2 * head + half + 1) * HALF],
-            )
-            for head in range(MH)
-            for half in range(2)
-        ],
-        axis=0,
-    )
+    slot_grads = [
+        mm(mixing[part], grad_memory[part * rows : (part + 1) * rows]).astype(BF)
+        for part in range(2)
+    ]
     arrived = lax.all_to_all(
         jnp.stack([piece.reshape(owners, capacity, width) for piece in slot_grads], axis=1),
         ALL,
@@ -1132,17 +1244,19 @@
         concat_axis=0,
         tiled=True,
     )
-    grad_rows = mm_l(serve_pick, arrived.reshape(owners * 2 * capacity, width))
+    grad_query, grad_keys = slot_weights_back(
+        ids, weights, table, grad_memory, mquery, keys_full, block
+    )
     grad_normed2 = mm_t(grad_query, query_full) + mm_t(grad_gate, gate_full)
-    grad_query_w = mm_l(normed2, grad_query)
-    grad_gate_w = mm_l(normed2, grad_gate)
+    grad_query_w = mm_l(normed2, grad_query).astype(BF)
+    grad_gate_w = mm_l(normed2, grad_gate).astype(BF)
     back, gain_mem_part = norm_backward(hidden, inverse2, gain_mem, grad_normed2)
     grad_hidden = dy_low.astype(F32) + back
     hidden_low = grad_hidden.astype(BF)
-    grad_attn_out = mm_l(att, hidden_low)
+    grad_attn_out = mm_l(att, hidden_low).astype(BF)
     grad_att = mm_t(hidden_low, attn_out_full).astype(BF)
-    block = cols // owners
-    keys_low = grad_keys.astype(BF).reshape(owners, 2, block, HALF).transpose(0, 2, 1, 3)
+    grad_att, arrived = lax.optimization_barrier((grad_att, arrived))
+    grad_rows = mm_l(serve_pick, arrived.reshape(owners * 2 * capacity, width))
     (grad_q, grad_k, grad_v), early = attention_backward(
         side,
         depth,
@@ -1154,13 +1268,7 @@
         lse,
         att,
         grad_att,
-        (
-            grad_query_w.astype(BF),
-            keys_low.reshape(cols, 2 * HALF),
-            grad_gate_w.astype(BF),
-            grad_mem_out.astype(BF),
-            grad_attn_out.astype(BF),
-        ),
+        (grad_query_w, grad_keys, grad_gate_w, grad_mem_out.astype(BF), grad_attn_out),
         2,
     )
     grad_normed = (
@@ -1168,10 +1276,9 @@
     )
     grad_x, gain_attn_part = norm_backward(x_rows, inverse, gain_attn, grad_normed)
     grad_x = grad_hidden + grad_x
-    grad_qkv = jnp.stack([mm_l(normed, piece) for piece in (grad_q, grad_k, grad_v)])
-
+    grad_qkv = jnp.stack([mm_l(normed, piece).astype(BF) for piece in (grad_q, grad_k, grad_v)])
     gains = jnp.concatenate([gain_attn_part, gain_mem_part]).reshape(2 * cols // 128, 128)
-    qkv_shard, gain_sums = reduce_grads(side, depth, (grad_qkv.astype(BF),), gains, 3)
+    qkv_shard, gain_sums = reduce_grads(side, depth, (grad_qkv,), gains, 3)
     own = lax.axis_index("dp") * depth + lax.axis_index("fsdp")
     gain_shards = lax.dynamic_index_in_dim(
         gain_sums.reshape(2, owners, block), own, axis=1, keepdims=False

time: 660 us -> 568 us (0.86)
  matrix products: 153 us -> 87.7 us
  Pallas kernels: 344 us -> 401 us
  other arithmetic: 65.3 us -> 8.93 us
  local copies, waits for them, and re-layouts: 70 us -> 25.6 us
  waiting for transfers between devices: 1.82 us -> 22.3 us
    dot_general x42 -> x10, matrix products: 83.7 us -> 33 us  [mm(): return jnp.dot(left, right, preferred_element_type=F32)]
    reduce_sum x5 -> x0, other arithmetic: 42.1 us -> none  [the longest x2 34.8 us: pick_weights(): jnp.sum((slot_ids[..., None] == jnp.arange(slots, dtype=jnp.int32)).astyp...]
    pallas_call x1 -> x3, Pallas kernels: 36.2 us -> 71.5 us  [the longest x1 38.2 us: gather_and_count(): pl.pallas_call(functools.partial(gather_kernel, plan, slots, rows), out_s...]
    pallas_call x1, Pallas kernels: 128 us -> 158 us  [attention_forward(): pl.pallas_call(functools.partial(forward_kernel, gather, exchange), out_s...]
    another operation x13 -> x1, local copies, waits for them, and re-layouts: 26.2 us -> 0.01 us  [per_device(): ids = jnp.stack([picked // SUB, picked % SUB], axis=1).reshape(4, slots)]
    all_to_all x1, waiting for transfers between devices: 0.01 us -> 22.3 us  [per_device(): lax.all_to_all(jnp.stack([piece.reshape(owners, capacity, width) for piec...]
    dot_general x17 -> x7, matrix products: 33.9 us -> 26 us  [mm_t(): lax.dot_general(left, right, (((1,), (1,)), ((), ())), preferred_element_...]
    mul x6 -> x0, local copies, waits for them, and re-layouts: 7.52 us -> none  [the longest x4 6.69 us: per_device(): pulled = weights[part] * grad_mixing]
  transfers between devices with their start and end apart: 3 -> 3, of which waited for: 1 -> 1; matrix products, arithmetic and copies ran while one was open for 24% -> 9% of each run, Pallas kernels for 34% -> 37%
where the time goes in v4:
time: 568 us; the launch traced here: 563 us
  Pallas kernels  401 us (71%)
  matrix products  87.7 us (15%)
  local copies, waits for them, and re-layouts  25.6 us (5%)
  waiting for transfers between devices  22.3 us (4%)
  starting transfers between devices  15.4 us (3%)
  other arithmetic  8.93 us (2%)
    pallas_call x1, Pallas kernels, attention_forward(): pl.pallas_call(functools.partial(forward_kernel, gather, exchange), out_s...  158 us
    pallas_call x1, Pallas kernels, attention_backward(): pl.pallas_call(functools.partial(backward_kernel, plan, collect), out_sha...  121 us
    pallas_call x1, Pallas kernels, reduce_grads(): pl.pallas_call(functools.partial(reduce_kernel, plan), out_shape=tuple(pl...  50.8 us
    pallas_call x1, Pallas kernels, gather_and_count(): pl.pallas_call(functools.partial(gather_kernel, plan, slots, rows), out_s...  38.2 us
    dot_general x10, matrix products, mm(): return jnp.dot(left, right, preferred_element_type=F32)  33 us
    dot_general x10, matrix products, mm_l(): lax.dot_general(left, right, (((0,), (0,)), ((), ())), preferred_element_...  28.7 us
    dot_general x7, matrix products, mm_t(): lax.dot_general(left, right, (((1,), (1,)), ((), ())), preferred_element_...  26 us
    all_to_all x1, waiting for transfers between devices, per_device(): lax.all_to_all(jnp.stack([piece.reshape(owners, capacity, width) for piec...  22.3 us
  transfers between devices with their start and end apart: 3, of which 1 were waited for; matrix products, arithmetic and copies ran while one was open for 9% of the time, Pallas kernels for 37%

profile of v4, /device:TPU:0, one launch (start us, length us, event | category | flops | bytes accessed | tf_op | source)
XLA Modules:
  0.0 562.5 jit_solution(3703334126358685658)
XLA Ops:
  2.2 7.3 %all-to-all-start = ((s32[2,32,16]{2,0,1:T(2,128)}), s32[2,32,16]{2,0,1:T(2,128)S(1)}, u32[]{:S(2)}, u32[]{:S(2)}) async-start(s32[2,32,16]{2,0,1:T(2,128)} %bitcast.16), calls=%async_computation | async-start | bytes 65536 | tf_op jit(solution)/shard_map/all_to_all | solution.py:1188
  11.5 38.2 %shard_map.255 = (bf16[2,4,512,256]{3,2,1,0:T(8,128)(2,1)S(1)}, bf16[3,4,2,2,2,32,1024]{6,5,4,3,2,1,0:T(8,128)(2,1)S(1)}) custom-call(s32[32,2048]{1,0:T(8,128)S(1)} %reshape.299.refs_0_, bf16[3,2,2,2,32,1024]{5,4,3,2,1,0:T(8,128)(2,1)S(1)} %bitcast.110), custom_call_target="tpu_custom_call" | custom-call | tf_op jit(solution)/shard_map/pallas_call | solution.py:581
  51.1 3.2 fusion.41
  55.6 8.1 %fusion.13 = bf16[1024,1024]{1,0:T(8,128)(2,1)} fusion(bf16[2048,1024]{1,0:T(8,128)(2,1)} %param.28, s32[1024]{0:T(1024)S(1)} %eq.17), kind=kOutput, calls=%fused_computation.36 | convolution fusion | flops 4298113024 | bytes 6295552 | tf_op jit(solution)/shard_map/dot_general | solution.py:28
  63.7 4.1 all-to-all-start.1
  67.9 4.0 convolution_convert_fusion.13.refs_0_
  71.9 2.3 convolution_convert_fusion.12.refs_1_
  74.2 2.3 convolution_convert_fusion.11.refs_2_
  76.5 157.6 %shard_map.256 = (bf16[512,1024]{1,0:T(8,128)(2,1)}, f32[16,512]{1,0:T(8,128)}, bf16[8,4,256,128]{3,2,1,0:T(8,128)(2,1)}, bf16[8,4,256,128]{3,2,1,0:T(8,128)(2,1...) custom-call(bf16[512,1024]{1,0:T(8,128)(2,1)} %convolution_convert_f, ...), custom_call_target="tpu_custom_call" | custom-call | tf_op jit(solution)/shard_map/pallas_call | solution.py:843
  234.1 3.4 multiply_reduce_fusion.2
  239.9 2.7 fusion.18
  242.5 6.2 %convolution_convert_fusion.1.query_ref = bf16[512,4096]{1,0:T(8,128)(2,1)} fusion(bf16[512,1024]{1,0:T(8,128)(2,1)S(1)} %multiply_convert_fusion.3, bf16[1024,4096]{1,0:T(8,128)(2,1)S(1)} %bitcast.171), kind=kOutput, calls=%fused_computation.5 | convolution fusion | flops 4297064448 | bytes 13631488 | tf_op jit(solution)/shard_map/dot_general | solution.py:28
  248.8 13.5 %shard_map.257 = (f32[2,4,512,256]{3,2,1,0:T(8,128)}, bf16[2,512,256]{2,1,0:T(8,128)(2,1)}) custom-call(s32[4,512]{1,0:T(4,128)} %reshape.307.ids_ref, bf16[2,4,512,256]{3,2,1,0:T(8,128)(2,1)} %copy-done.1, bf16[512,4096]{1,0:T(8,128)(2,1)} %convolution_convert_fusion.1.query_ref, bf16[2048,512]{1,0:T(8,128)(2,1)} %bitcast.176), custom_call_target="tpu_custom_call" | custom-call | flops 4294967296 | bytes 25165824 | tf_op jit(solution)/shard_map/pallas_call | solution.py:1062
  262.2 1.7 fusion.42
  264.0 3.3 copy.43
  269.5 3.5 multiply_convert_fusion
  274.9 19.8 %shard_map.258 = (bf16[512,4096]{1,0:T(8,128)(2,1)}, bf16[1024,1024]{1,0:T(8,128)(2,1)}) custom-call(s32[4,512]{1,0:T(4,128)} %reshape.307.ids_ref, f32[2,4,512,256]{3,2,1,0:T(8,128)} %get-tuple-element.49.weight_ref, bf16[2,512,1024]{2,1,0:T(8,128)(2,1)} %bitcast.143, bf16[512,1024]{1,0:T(8,128)(2,1)} %copy-done.17, ...), custom_call_target="tpu_custom_call" | custom-call | flops 6442450944 | bytes 25165824 | tf_op jit(solution)/shard_map/pallas_call | solution.py:1130
  294.7 10.6 %fusion.43 = f32[512,1024]{1,0:T(8,128)} fusion(bf16[512,4096]{1,0:T(8,128)(2,1)} %get-tuple-element.50, bf16[1024,4096]{1,0:T(8,128)(2,1)} %bitcast.168), kind=kOutput, calls=%fused_computation.102 | convolution fusion | flops 4294967296 | bytes 14680064 | tf_op jit(solution)/shard_map/dot_general | solution.py:32
  306.9 4.0 all-to-all-start.2
  310.9 4.0 multiply_reduce_fusion
  317.8 2.7 convolution_convert_fusion.6
  320.5 2.6 convolution_convert_fusion.7
  324.4 2.7 convolution_convert_fusion.5
  327.0 2.3 convolution_convert_fusion.10.refs_7_
  329.3 6.8 %convolution_convert_fusion = bf16[1024,4096]{1,0:T(8,128)(2,1)} fusion(bf16[512,1024]{1,0:T(8,128)(2,1)S(1)} %copy-done.19, bf16[512,4096]{1,0:T(8,128)(2,1)S(1)} %copy-done.40), kind=kOutput, calls=%fused_computation.3 | convolution fusion | flops 4299161600 | bytes 13631488 | tf_op jit(solution)/shard_map/dot_general | solution.py:36
  336.1 22.3 %all-to-all-done.2 = bf16[32,2,16,1024]{3,2,1,0:T(8,128)(2,1)} async-done(((bf16[32,2,16,1024]{3,2,1,0:T(8,128)(2,1)}), bf16[32,2,16,1024]{3,2,1,0:T(8,128)(2,1)}, u32[]{:S(2)}, u32[]{:S(2)}) %all-to-all-start.2) | async-done | bytes 2097184 | tf_op jit(solution)/shard_map/all_to_all | solution.py:1240
  358.4 121.1 %shard_map.259 = (bf16[512,1024]{1,0:T(8,128)(2,1)}, bf16[512,1024]{1,0:T(8,128)(2,1)}, bf16[512,1024]{1,0:T(8,128)(2,1)}, f32[32,4096]{1,0:T(8,128)}, f32[32,10...) custom-call(bf16[512,1024]{1,0:T(8,128)(2,1)} %convolution_convert_fusion.13.refs_0_, ...), custom_call_target="tpu_custom_call" | custom-call | tf_op jit(solution)/shard_map/pallas_call | solution.py:993
  479.5 3.3 fusion.45
  489.1 1.9 fusion.12
  493.6 3.4 pad_maximum_fusion.refs_0_
  497.0 50.8 %shard_map.260 = (f32[3,32,1024]{2,1,0:T(8,128)}, f32[16,128]{1,0:T(8,128)}) custom-call(bf16[3,2,2,2,4,32,1024]{6,5,4,3,2,1,0:T(8,128)(2,1)} %pad_maximum_fusion.refs_0_, f32[16,128]{1,0:T(8,128)} %pad_maximum_fusion.7.refs_1_), custom_call_target="tpu_custom_call" | custom-call | tf_op jit(solution)/shard_map/pallas_call | solution.py:609
  549.4 8.9 %fusion = f32[2048,1024]{1,0:T(8,128)} fusion(bf16[1024,1024]{1,0:T(8,128)(2,1)} %bitcast.52, s32[1024]{0:T(1024)S(1)} %eq.17), kind=kOutput, calls=%fused_computation.1 | convolution fusion | flops 4297064448 | bytes 10489856 | tf_op jit(solution)/shard_map/dot_general | solution.py:36
  (132 shorter events, 32.6 us)
Async XLA Ops:
  0.6 10.9 %copy-start = (bf16[3,256,1024]{2,1,0:T(8,128)(2,1)S(1)}, bf16[3,256,1024]{2,1,0:T(8,128)(2,1)}, u32[]{:S(2)}) copy-start(bf16[3,256,1024]{2,1,0:T(8,128)(2,1)} %param.22) | copy-start | bytes 4718596
  2.2 53.3 %all-to-all-start = ((s32[2,32,16]{2,0,1:T(2,128)}), s32[2,32,16]{2,0,1:T(2,128)S(1)}, u32[]{:S(2)}, u32[]{:S(2)}) async-start(s32[2,32,16]{2,0,1:T(2,128)} %bitcast.16), calls=%async_computation | async-start | bytes 65536 | tf_op jit(solution)/shard_map/all_to_all | solution.py:1188
  51.1 3.2 copy-start.7
  51.1 3.2 copy-start.9
  54.2 20.0 %copy-start.11 = (bf16[1,4,2,2,2,32,1024]{6,5,4,3,2,1,0:T(8,128)(2,1)}, bf16[1,4,2,2,2,32,1024]{6,5,4,3,2,1,0:T(8,128)(2,1)S(1)}, u32[]{:S(2)}) copy-start(bf16[1,4,2,2,2,32,1024]{6,5,4,3,2,1,0:T(8,128)(2,1)S(1)} %get-tuple-element.71) | copy-start | bytes 6291460
  63.7 4.1 copy-start.31
  63.7 198.5 %all-to-all-start.1 = ((bf16[32,32,1024]{2,1,0:T(8,128)(2,1)}), bf16[32,32,1024]{2,1,0:T(8,128)(2,1)}, u32[]{:S(2)}, u32[]{:S(2)}) async-start(bf16[32,32,1024]{2,1,0:T(8,128)(2,1)} %bitcast.18), calls=%async_computation.1 | async-start | bytes 4194304 | tf_op jit(solution)/shard_map/all_to_all | solution.py:1191
  67.9 4.0 copy-start.14
  234.1 3.5 copy-start.30
  234.1 8.4 %slice-start = ((s8[8388608]{0:T(1024)(128)(4,1)}), s8[4194304]{0:T(1024)(128)(4,1)S(1)}, s32[]{:S(2)}) async-start(s8[8388608]{0:T(1024)(128)(4,1)} %bitcast.169), calls=%async_computation.3 | async-start | bytes 8388608
  237.6 2.3 copy-start.33
  237.6 4.9 slice-start.1
  237.9 30.3 %copy-start.18 = (bf16[512,1024]{1,0:T(8,128)(2,1)}, bf16[512,1024]{1,0:T(8,128)(2,1)S(1)}, u32[]{:S(2)}) copy-start(bf16[512,1024]{1,0:T(8,128)(2,1)S(1)} %multiply_convert_fusion.3) | copy-start | bytes 3145732
  263.9 3.3 copy-start.6
  294.7 10.6 %copy-start.4 = (bf16[512,1024]{1,0:T(8,128)(2,1)S(1)}, bf16[512,1024]{1,0:T(8,128)(2,1)}, u32[]{:S(2)}) copy-start(bf16[512,1024]{1,0:T(8,128)(2,1)} %convolution_convert_fusion.9) | copy-start | bytes 3145732
  306.9 4.0 copy-start.16
  306.9 51.5 %all-to-all-start.2 = ((bf16[32,2,16,1024]{3,2,1,0:T(8,128)(2,1)}), bf16[32,2,16,1024]{3,2,1,0:T(8,128)(2,1)}, u32[]{:S(2)}, u32[]{:S(2)}) async-start(bf16[32,2,16,1024]{3,2,1,0:T(8,128)(2,1)} %pad_maximum_fusion.2), calls=%async_computation.2 | async-start | bytes 4194304 | tf_op jit(solution)/shard_map/all_to_all | solution.py:1240
  310.9 4.1 copy-start.34
  310.9 4.1 copy-start.38
  317.8 2.7 copy-start.19
  324.4 2.7 copy-start.2
  324.4 2.7 copy-start.32
  327.0 2.3 copy-start.40
  479.5 3.4 copy-start.8
  479.5 3.4 copy-start.10
  479.5 3.4 copy-start.37
  497.0 51.6 %copy-start.29 = (f32[32,1024]{1,0:T(8,128)S(1)}, f32[32,1024]{1,0:T(8,128)}, u32[]{:S(2)}) copy-start(f32[32,1024]{1,0:T(8,128)} %get-tuple-element.63) | copy-start | bytes 393220
  549.4 9.4 %copy-start.25 = (f32[3,32,1024]{2,1,0:T(8,128)S(1)}, f32[3,32,1024]{2,1,0:T(8,128)}, u32[]{:S(2)}) copy-start(f32[3,32,1024]{2,1,0:T(8,128)} %get-tuple-element.114) | copy-start | bytes 1179652
  549.4 10.1 %copy-start.28 = (f32[32,1024]{1,0:T(8,128)S(1)}, f32[32,1024]{1,0:T(8,128)}, u32[]{:S(2)}) copy-start(f32[32,1024]{1,0:T(8,128)} %get-tuple-element.115) | copy-start | bytes 393220
  549.4 10.8 %copy-start.24 = (f32[32,4096]{1,0:T(8,128)S(1)}, f32[32,4096]{1,0:T(8,128)}, u32[]{:S(2)}) copy-start(f32[32,4096]{1,0:T(8,128)} %get-tuple-element.116) | copy-start | bytes 1572868
  558.2 2.7 copy-start.27
  558.2 3.4 copy-start.26
  (14 other events, 21.6 us)

commit v5 on v4

--- a/solution.py
+++ b/solution.py
@@ -15,7 +15,8 @@
 COLLECT_LAG = 2
 AHEAD = 3
 HOP_LAG = 1
-PIECE = 1024
+FIRST_PIECE = 512
+LAST_PIECE = 512
 PAIR = 128
 HDIM = 64
 MH = 4
@@ -92,13 +93,13 @@
 
 
 class Gather:
-    def __init__(self, side, depth, shards):
+    def __init__(self, side, depth, shards, piece=1024):
         self.side, self.depth = side, depth
         self.views, self.outs, self.shapes, self.held, self.layout = [], [], [], [], []
         plane = 2 * side * side
         for shard in shards:
             rows, cols = shard.shape[-2:]
-            block, width = rows // plane, min(cols, PIECE)
+            block, width = rows // plane, min(cols, piece)
             lead = shard.shape[:-2]
             self.views.append(shard.reshape(lead + (side, side, 2, block, cols)))
             leads = range(lead[0]) if lead else (None,)
@@ -277,10 +278,10 @@
 
 
 class Reduce:
-    def __init__(self, side, depth, grads, gains=None):
+    def __init__(self, side, depth, grads, gains=None, piece=1024):
         self.side, self.depth = side, depth
         self.layout, self.views, self.outs = [], [], []
-        self.width = width = 1024
+        self.width = width = piece
         devices = 2 * side * side * depth
         for grad in grads:
             rows, cols = grad.shape[-2:]
@@ -576,7 +577,7 @@
 
 
 def gather_and_count(side, depth, shards, picks, slots, rows, call_id):
-    plan = Gather(side, depth, shards)
+    plan = Gather(side, depth, shards, FIRST_PIECE)
     any_space, vmem = pl.BlockSpec(memory_space=pl.ANY), pl.BlockSpec(memory_space=pltpu.VMEM)
     results = pl.pallas_call(
         functools.partial(gather_kernel, plan, slots, rows),
@@ -605,7 +606,7 @@
 
 
 def reduce_grads(side, depth, grads, gains, call_id):
-    plan = Reduce(side, depth, grads, gains)
+    plan = Reduce(side, depth, grads, gains, LAST_PIECE)
     return pl.pallas_call(
         functools.partial(reduce_kernel, plan),
         out_shape=tuple(plan.outs),
@@ -1186,14 +1187,20 @@
     side, depth = grid_of(lax.axis_size("dp"), lax.axis_size("fsdp"))
 
     asked = lax.all_to_all(request[:, 0], ALL, split_axis=1, concat_axis=1, tiled=True)
-    serve_pick = one_hot(asked.transpose(1, 0, 2).reshape(-1), shard_rows)
-    served = mm(serve_pick, value_rows).astype(BF).reshape(owners, 2 * capacity, width)
-    table = lax.all_to_all(served, ALL, split_axis=0, concat_axis=0, tiled=True)
-    table = table.reshape(owners, 2, capacity, width).transpose(1, 0, 2, 3).reshape(2, slots, width)
+    serve_picks = [one_hot(asked[part].reshape(-1), shard_rows) for part in range(2)]
+
+    def swap(values):
+        values = values.reshape(owners, capacity, width)
+        swapped = lax.all_to_all(values, ALL, split_axis=0, concat_axis=0, tiled=True)
+        return swapped.reshape(slots, width)
+
+    served = [mm(pick, value_rows).astype(BF) for pick in serve_picks]
     offsets = jnp.maximum(request[:, 0].reshape(2, slots), 0)
     picked = (jnp.arange(slots, dtype=jnp.int32) // capacity)[None] * shard_rows + offsets
     ids = jnp.stack([picked // SUB, picked % SUB], axis=1).reshape(4, slots)
     picks = jnp.stack([slot_prompt[0], slot_cont[0]]).transpose(3, 0, 2, 1)
+    picks, served = lax.optimization_barrier((picks, served))
+    tables = [swap(served[0])]
     counts, (qkv_full,) = gather_and_count(
         side, depth, (w_qkv,), picks.reshape(picks.shape[0], -1), slots, rows, 0
     )
@@ -1205,6 +1212,7 @@
     queries = mm(normed, qkv_full[0]).astype(BF)
     keys = mm(normed, qkv_full[1]).astype(BF)
     vals = mm(normed, qkv_full[2]).astype(BF)
+    queries, tables[0] = lax.optimization_barrier((queries, tables[0]))
     (att, lse, all_keys, all_vals), full = attention_forward(
         side,
         depth,
@@ -1215,6 +1223,8 @@
         1,
     )
     attn_out_full, query_full, keys_full, gate_full, mem_out_full = full
+    att, late = lax.optimization_barrier((att, served[1]))
+    tables.append(swap(late))
     hidden = x_rows + mm(att, attn_out_full)
     normed2, inverse2 = normalize(hidden, gain_mem)
     normed2 = normed2.astype(BF)
@@ -1222,7 +1232,7 @@
     mquery = mm(normed2, query_full).astype(BF)
     gate_pre = mm(normed2, gate_full)
     weights, mixing = slot_weights(ids, counts, mquery, keys_full)
-    memory_out = jnp.concatenate([mm_l(mixing[part], table[part]) for part in range(2)], axis=0)
+    memory_out = jnp.concatenate([mm_l(mixing[part], tables[part]) for part in range(2)], axis=0)
     sigmoid_gate = jax.nn.sigmoid(gate_pre)
     blended = (memory_out * (gate_pre * sigmoid_gate)).astype(BF)
     out = (hidden + mm(blended, mem_out_full)).astype(BF)
@@ -1237,15 +1247,9 @@
         mm(mixing[part], grad_memory[part * rows : (part + 1) * rows]).astype(BF)
         for part in range(2)
     ]
-    arrived = lax.all_to_all(
-        jnp.stack([piece.reshape(owners, capacity, width) for piece in slot_grads], axis=1),
-        ALL,
-        split_axis=0,
-        concat_axis=0,
-        tiled=True,
-    )
+    arrived = swap(slot_grads[1])
     grad_query, grad_keys = slot_weights_back(
-        ids, weights, table, grad_memory, mquery, keys_full, block
+        ids, weights, jnp.stack(tables), grad_memory, mquery, keys_full, block
     )
     grad_normed2 = mm_t(grad_query, query_full) + mm_t(grad_gate, gate_full)
     grad_query_w = mm_l(normed2, grad_query).astype(BF)
@@ -1256,7 +1260,6 @@
     grad_attn_out = mm_l(att, hidden_low).astype(BF)
     grad_att = mm_t(hidden_low, attn_out_full).astype(BF)
     grad_att, arrived = lax.optimization_barrier((grad_att, arrived))
-    grad_rows = mm_l(serve_pick, arrived.reshape(owners * 2 * capacity, width))
     (grad_q, grad_k, grad_v), early = attention_backward(
         side,
         depth,
@@ -1270,6 +1273,10 @@
         grad_att,
         (grad_query_w, grad_keys, grad_gate_w, grad_mem_out.astype(BF), grad_attn_out),
         2,
+    )
+    grad_q, late = lax.optimization_barrier((grad_q, slot_grads[0]))
+    grad_rows = mm_l(
+        jnp.concatenate(serve_picks, axis=0), jnp.concatenate([swap(late), arrived], axis=0)
     )
     grad_normed = (
         mm_t(grad_q, qkv_full[0]) + mm_t(grad_k, qkv_full[1]) + mm_t(grad_v, qkv_full[2])

time: 568 us -> 566 us (level)
  matrix products: 87.7 us -> 101 us
  Pallas kernels: 401 us -> 388 us
  waiting for transfers between devices: 22.3 us -> 12 us
  starting transfers between devices: 15.4 us -> 24.9 us
  local copies, waits for them, and re-layouts: 25.6 us -> 16.4 us
  other arithmetic: 8.93 us -> 17.3 us
    pallas_call x1, Pallas kernels: 158 us -> 127 us  [attention_forward(): pl.pallas_call(functools.partial(forward_kernel, gather, exchange), out_s...]
    pallas_call x1, Pallas kernels: 38.2 us -> 59 us  [gather_and_count(): pl.pallas_call(functools.partial(gather_kernel, plan, slots, rows), out_s...]
    all_to_all x2 -> x4, waiting for transfers between devices: 22.3 us -> 8.79 us  [swap(): lax.all_to_all(values, ALL, split_axis=0, concat_axis=0, tiled=True)]
    all_to_all x2 -> x4, starting transfers between devices: 8.15 us -> 17.6 us  [swap(): lax.all_to_all(values, ALL, split_axis=0, concat_axis=0, tiled=True)]
    dot_general x10 -> x11, matrix products: 33 us -> 36.8 us  [mm(): return jnp.dot(left, right, preferred_element_type=F32)]
    unnamed x92 -> x98, local copies, waits for them, and re-layouts: 11.6 us -> 9.14 us
  transfers between devices with their start and end apart: 3 -> 5, of which waited for: 1 -> 2; matrix products, arithmetic and copies ran while one was open for 9% -> 12% of each run, Pallas kernels for 37% -> 21%
where the time goes in v5:
time: 566 us; the launch traced here: 561 us
  Pallas kernels  388 us (69%)
  matrix products  101 us (18%)
  starting transfers between devices  24.9 us (4%)
  other arithmetic  17.3 us (3%)
  local copies, waits for them, and re-layouts  16.4 us (3%)
  waiting for transfers between devices  12 us (2%)
    pallas_call x1, Pallas kernels, attention_forward(): pl.pallas_call(functools.partial(forward_kernel, gather, exchange), out_s...  127 us
    pallas_call x1, Pallas kernels, attention_backward(): pl.pallas_call(functools.partial(backward_kernel, plan, collect), out_sha...  122 us
    pallas_call x1, Pallas kernels, gather_and_count(): pl.pallas_call(functools.partial(gather_kernel, plan, slots, rows), out_s...  59 us
    pallas_call x1, Pallas kernels, reduce_grads(): pl.pallas_call(functools.partial(reduce_kernel, plan), out_shape=tuple(pl...  46.9 us
    dot_general x11, matrix products, mm(): return jnp.dot(left, right, preferred_element_type=F32)  36.8 us
    dot_general x10, matrix products, mm_l(): lax.dot_general(left, right, (((0,), (0,)), ((), ())), preferred_element_...  33.1 us
    dot_general x7, matrix products, mm_t(): lax.dot_general(left, right, (((1,), (1,)), ((), ())), preferred_element_...  30.8 us
    pallas_call x1, Pallas kernels, slot_weights_back(): pl.pallas_call(functools.partial(picks_back_kernel, block), grid=(MH, 2),...  20.2 us
  transfers between devices with their start and end apart: 5, of which 2 were waited for; matrix products, arithmetic and copies ran while one was open for 12% of the time, Pallas kernels for 21%

profile of v5, /device:TPU:0, one launch (start us, length us, event | category | flops | bytes accessed | tf_op | source)
XLA Modules:
  0.0 561.1 jit_solution(11085595208263504970)
XLA Ops:
  2.1 7.3 %all-to-all-start = ((s32[2,32,16]{2,0,1:T(2,128)}), s32[2,32,16]{2,0,1:T(2,128)S(1)}, u32[]{:S(2)}, u32[]{:S(2)}) async-start(s32[2,32,16]{2,0,1:T(2,128)} %bitcast.3), calls=%async_computation | async-start | bytes 65536 | tf_op jit(solution)/shard_map/all_to_all | solution.py:1189
  13.4 3.2 all-to-all-done
  16.9 5.7 %convolution_convert_fusion.15 = bf16[512,1024]{1,0:T(8,128)(2,1)} fusion(bf16[2048,1024]{1,0:T(8,128)(2,1)} %param.28, s32[512]{0:T(512)S(1)} %eq.32), kind=kOutput, calls=%fused_computation.54 | convolution fusion | flops 2149056512 | bytes 5244928 | tf_op jit(solution)/shard_map/dot_general | solution.py:29
  22.6 3.4 convolution_convert_fusion.14
  26.3 3.3 all-to-all-start.1
  29.7 59.0 %shard_map.255 = (bf16[2,4,512,256]{3,2,1,0:T(8,128)(2,1)S(1)}, bf16[3,4,2,2,2,32,1024]{6,5,4,3,2,1,0:T(8,128)(2,1)S(1)}) custom-call(s32[32,2048]{1,0:T(8,128)S(1)} %reshape.308.refs_0_, bf16[3,2,2,2,32,1024]{5,4,3,2,1,0:T(8,128)(2,1)S(1)} %bitcast.105), custom_call_target="tpu_custom_call" | custom-call | tf_op jit(solution)/shard_map/pallas_call | solution.py:582
  91.3 2.8 convolution_convert_fusion.13.refs_0_
  101.2 127.4 %shard_map.256 = (bf16[512,1024]{1,0:T(8,128)(2,1)}, f32[16,512]{1,0:T(8,128)}, bf16[8,4,256,128]{3,2,1,0:T(8,128)(2,1)}, bf16[8,4,256,128]{3,2,1,0:T(8,128)(2,1...) custom-call(bf16[512,1024]{1,0:T(8,128)(2,1)} %convolution_convert_f, ...), custom_call_target="tpu_custom_call" | custom-call | tf_op jit(solution)/shard_map/pallas_call | solution.py:844
  228.6 4.2 all-to-all-start.2
  232.8 3.6 multiply_reduce_fusion.2
  237.4 6.1 %convolution_convert_fusion.1.query_ref = bf16[512,4096]{1,0:T(8,128)(2,1)} fusion(bf16[512,1024]{1,0:T(8,128)(2,1)S(1)} %multiply_convert_fusion.3, bf16[1024,4096]{1,0:T(8,128)(2,1)S(1)} %bitcast.161), kind=kOutput, calls=%fused_computation.6 | convolution fusion | flops 4297064448 | bytes 13631488 | tf_op jit(solution)/shard_map/dot_general | solution.py:29
  243.5 13.4 %shard_map.257 = (f32[2,4,512,256]{3,2,1,0:T(8,128)}, bf16[2,512,256]{2,1,0:T(8,128)(2,1)}) custom-call(s32[4,512]{1,0:T(4,128)} %reshape.318.ids_ref, bf16[2,4,512,256]{3,2,1,0:T(8,128)(2,1)} %copy-done.1, bf16[512,4096]{1,0:T(8,128)(2,1)} %convolution_convert_fusion.1.query_ref, bf16[2048,512]{1,0:T(8,128)(2,1)} %bitcast.164), custom_call_target="tpu_custom_call" | custom-call | flops 4294967296 | bytes 25165824 | tf_op jit(solution)/shard_map/pallas_call | solution.py:1063
  259.4 4.2 fusion.20
  265.6 5.4 multiply_convert_fusion
  278.8 2.7 pad_maximum_fusion.2.table_ref
  281.6 20.2 %shard_map.258 = (bf16[512,4096]{1,0:T(8,128)(2,1)}, bf16[1024,1024]{1,0:T(8,128)(2,1)}) custom-call(s32[4,512]{1,0:T(4,128)} %reshape.318.ids_ref, f32[2,4,512,256]{3,2,1,0:T(8,128)} %get-tuple-element.65.weight_ref, bf16[2,512,1024]{2,1,0:T(8,128)(2,1)} %pad_maximum_fusion.2.table_ref, bf16[512,1024]{1,0:T(8,128)(2,1)} %copy-done.19, ...), custom_call_target="tpu_custom_call" | custom-call | flops 6442450944 | bytes 25165824 | tf_op jit(solution)/shard_map/pallas_call | solution.py:1131
  301.8 8.4 %fusion.46 = f32[512,1024]{1,0:T(8,128)S(1)} fusion(bf16[512,4096]{1,0:T(8,128)(2,1)} %get-tuple-element.66, bf16[1024,4096]{1,0:T(8,128)(2,1)} %bitcast.160), kind=kOutput, calls=%fused_computation.110 | convolution fusion | flops 4294967296 | bytes 14680064 | tf_op jit(solution)/shard_map/dot_general | solution.py:33
  310.2 2.6 convolution_convert_fusion.7
  312.9 2.9 multiply_reduce_fusion
  315.8 6.5 %all-to-all-start.3 = ((bf16[32,16,1024]{2,1,0:T(8,128)(2,1)}), bf16[32,16,1024]{2,1,0:T(8,128)(2,1)}, u32[]{:S(2)}, u32[]{:S(2)}) async-start(bf16[32,16,1024]{2,1,0:T(8,128)(2,1)} %bitcast.30), calls=%async_computation.3 | async-start | bytes 2097152 | tf_op jit(solution)/shard_map/all_to_all | solution.py:1194
  326.9 2.6 convolution_convert_fusion.5
  331.9 6.8 %convolution_convert_fusion = bf16[1024,4096]{1,0:T(8,128)(2,1)} fusion(bf16[512,1024]{1,0:T(8,128)(2,1)S(1)} %copy-done.23, bf16[512,4096]{1,0:T(8,128)(2,1)S(1)} %copy-done.45), kind=kOutput, calls=%fused_computation.4 | convolution fusion | flops 4299161600 | bytes 13631488 | tf_op jit(solution)/shard_map/dot_general | solution.py:37
  338.6 8.8 %all-to-all-done.3 = bf16[32,16,1024]{2,1,0:T(8,128)(2,1)} async-done(((bf16[32,16,1024]{2,1,0:T(8,128)(2,1)}), bf16[32,16,1024]{2,1,0:T(8,128)(2,1)}, u32[]{:S(2)}, u32[]{:S(2)}) %all-to-all-start.3) | async-done | bytes 1048608 | tf_op jit(solution)/shard_map/all_to_all | solution.py:1194
  347.4 121.6 %shard_map.259 = (bf16[512,1024]{1,0:T(8,128)(2,1)}, bf16[512,1024]{1,0:T(8,128)(2,1)}, bf16[512,1024]{1,0:T(8,128)(2,1)}, f32[32,4096]{1,0:T(8,128)}, f32[32,10...) custom-call(bf16[512,1024]{1,0:T(8,128)(2,1)} %convolution_convert_fusion.13.refs_0_, ...), custom_call_target="tpu_custom_call" | custom-call | tf_op jit(solution)/shard_map/pallas_call | solution.py:994
  469.1 4.7 fusion.47
  473.8 2.7 fusion.48
  476.4 2.7 convolution_convert_fusion.2
  479.2 3.6 all-to-all-start.4
  482.8 5.7 %fusion.12 = (f32[1024]{0:T(1024)S(1)}, f32[512]{0:T(512)S(1)}, f32[512,1024]{1,0:T(8,128)}) fusion(f32[512]{0:T(512)S(1)} %get-tuple-element.106, bf16[256,1024]{1,0:T(8,128)(2,1)S(1)} %bitcast.122, bf16[256,1024]{1,0:T(8,128)(2,1)S(1)} %bitcast.132, f32[1024]{0:T(1024)S(1)} %copy-done.36, bf16[512,1024]{1,0:T(8,128)(2,1)} %get-tuple-element.75, ...), kind=kOutput, calls=%fused_computation.23 | convolution fusion | flops 1080031744 | bytes 10498048 | tf_op jit(solution)/shard_map/dot_general | solution.py:33
  492.1 3.4 pad_maximum_fusion.refs_0_
  495.5 46.9 %shard_map.260 = (f32[3,32,1024]{2,1,0:T(8,128)}, f32[16,128]{1,0:T(8,128)}) custom-call(bf16[3,2,2,2,4,32,1024]{6,5,4,3,2,1,0:T(8,128)(2,1)} %pad_maximum_fusion.refs_0_, f32[16,128]{1,0:T(8,128)} %pad_maximum_fusion.7.refs_1_), custom_call_target="tpu_custom_call" | custom-call | tf_op jit(solution)/shard_map/pallas_call | solution.py:610
  548.9 8.4 %fusion = f32[2048,1024]{1,0:T(8,128)} fusion(pred[512,2048]{1,0:T(32,128)(4,1)S(1)} %copy-done.20, pred[512,2048]{1,0:T(32,128)(4,1)S(1)} %copy-done.21, bf16[512,1024]{1,0:T(8,128)(2,1)} %bitcast.31, bf16[512,1024]{1,0:T(8,128)(2,1)} %bitcast.49), kind=kOutput, calls=%fused_computation | convolution fusion | flops 4301258752 | bytes 12582912 | tf_op jit(solution)/shard_map/dot_general | solution.py:37
  (143 shorter events, 49.4 us)
Async XLA Ops:
  2.1 14.6 %all-to-all-start = ((s32[2,32,16]{2,0,1:T(2,128)}), s32[2,32,16]{2,0,1:T(2,128)S(1)}, u32[]{:S(2)}, u32[]{:S(2)}) async-start(s32[2,32,16]{2,0,1:T(2,128)} %bitcast.3), calls=%async_computation | async-start | bytes 65536 | tf_op jit(solution)/shard_map/all_to_all | solution.py:1189
  16.9 5.7 %copy-start.38 = (bf16[2048,1024]{1,0:T(8,128)(2,1)S(1)}, bf16[2048,1024]{1,0:T(8,128)(2,1)}, u32[]{:S(2)}) copy-start(bf16[2048,1024]{1,0:T(8,128)(2,1)} %param.28) | copy-start | bytes 12582916
  26.0 3.7 copy-start
  26.3 74.9 %all-to-all-start.1 = ((bf16[32,16,1024]{2,1,0:T(8,128)(2,1)}), bf16[32,16,1024]{2,1,0:T(8,128)(2,1)S(1)}, u32[]{:S(2)}, u32[]{:S(2)}) async-start(bf16[32,16,1024]{2,1,0:T(8,128)(2,1)} %bitcast.145), calls=%async_computation.1 | async-start | bytes 2097152 | tf_op jit(solution)/shard_map/all_to_all | solution.py:1194
  91.3 2.9 copy-start.15
  91.3 2.9 copy-start.13
  91.3 5.1 copy-start.11
  228.6 35.0 %all-to-all-start.2 = ((bf16[32,16,1024]{2,1,0:T(8,128)(2,1)}), bf16[32,16,1024]{2,1,0:T(8,128)(2,1)}, u32[]{:S(2)}, u32[]{:S(2)}) async-start(bf16[32,16,1024]{2,1,0:T(8,128)(2,1)} %bitcast.20), calls=%async_computation.2 | async-start | bytes 2097152 | tf_op jit(solution)/shard_map/all_to_all | solution.py:1194
  232.7 3.7 copy-start.35
  232.7 4.6 copy-start.37
  236.7 6.8 %copy-start.22 = (bf16[512,1024]{1,0:T(8,128)(2,1)}, bf16[512,1024]{1,0:T(8,128)(2,1)S(1)}, u32[]{:S(2)}) copy-start(bf16[512,1024]{1,0:T(8,128)(2,1)S(1)} %multiply_convert_fusion.3) | copy-start | bytes 3145732
  265.6 5.5 copy-start.40
  271.0 6.4 %copy-start.19 = (bf16[512,1024]{1,0:T(8,128)(2,1)}, bf16[512,1024]{1,0:T(8,128)(2,1)S(1)}, u32[]{:S(2)}) copy-start(bf16[512,1024]{1,0:T(8,128)(2,1)S(1)} %get-tuple-element.95.memory_ref) | copy-start | bytes 3145732
  301.8 8.4 %copy-start.18 = (bf16[512,1024]{1,0:T(8,128)(2,1)S(1)}, bf16[512,1024]{1,0:T(8,128)(2,1)}, u32[]{:S(2)}) copy-start(bf16[512,1024]{1,0:T(8,128)(2,1)} %get-tuple-element.94) | copy-start | bytes 3145732
  301.8 8.4 %copy-start.23 = (bf16[512,1024]{1,0:T(8,128)(2,1)S(1)}, bf16[512,1024]{1,0:T(8,128)(2,1)}, u32[]{:S(2)}) copy-start(bf16[512,1024]{1,0:T(8,128)(2,1)} %copy-done.22) | copy-start | bytes 3145732
  310.2 2.7 copy-start.5
  315.8 31.6 %all-to-all-start.3 = ((bf16[32,16,1024]{2,1,0:T(8,128)(2,1)}), bf16[32,16,1024]{2,1,0:T(8,128)(2,1)}, u32[]{:S(2)}, u32[]{:S(2)}) async-start(bf16[32,16,1024]{2,1,0:T(8,128)(2,1)} %bitcast.30), calls=%async_computation.3 | async-start | bytes 2097152 | tf_op jit(solution)/shard_map/all_to_all | solution.py:1194
  324.9 4.6 copy-start.2
  469.1 4.7 copy-start.14
  469.1 4.7 copy-start.42
  473.8 2.7 copy-start.8
  473.8 2.7 copy-start.10
  473.8 2.7 copy-start.44
  479.2 3.6 copy-start.12
  479.2 68.9 %all-to-all-start.4 = ((bf16[32,16,1024]{2,1,0:T(8,128)(2,1)}), bf16[32,16,1024]{2,1,0:T(8,128)(2,1)}, u32[]{:S(2)}, u32[]{:S(2)}) async-start(bf16[32,16,1024]{2,1,0:T(8,128)(2,1)} %bitcast.48), calls=%async_computation.4 | async-start | bytes 2097152 | tf_op jit(solution)/shard_map/all_to_all | solution.py:1194
  482.8 6.3 %copy-start.43 = (bf16[512,1024]{1,0:T(8,128)(2,1)S(1)}, bf16[512,1024]{1,0:T(8,128)(2,1)}, u32[]{:S(2)}) copy-start(bf16[512,1024]{1,0:T(8,128)(2,1)} %get-tuple-element.74) | copy-start | bytes 3145732
  495.5 47.7 %copy-start.34 = (f32[32,1024]{1,0:T(8,128)S(1)}, f32[32,1024]{1,0:T(8,128)}, u32[]{:S(2)}) copy-start(f32[32,1024]{1,0:T(8,128)} %get-tuple-element.80) | copy-start | bytes 393220
  495.5 49.0 %copy-start.3 = (f32[512,1024]{1,0:T(8,128)S(1)}, f32[512,1024]{1,0:T(8,128)}, u32[]{:S(2)}) copy-start(f32[512,1024]{1,0:T(8,128)} %copy-done.2) | copy-start | bytes 6291460
  548.9 8.5 %copy-start.30 = (f32[3,32,1024]{2,1,0:T(8,128)S(1)}, f32[3,32,1024]{2,1,0:T(8,128)}, u32[]{:S(2)}) copy-start(f32[3,32,1024]{2,1,0:T(8,128)} %get-tuple-element.134) | copy-start | bytes 1179652
  548.9 9.2 %copy-start.33 = (f32[32,1024]{1,0:T(8,128)S(1)}, f32[32,1024]{1,0:T(8,128)}, u32[]{:S(2)}) copy-start(f32[32,1024]{1,0:T(8,128)} %get-tuple-element.135) | copy-start | bytes 393220
  548.9 9.9 %copy-start.29 = (f32[32,4096]{1,0:T(8,128)S(1)}, f32[32,4096]{1,0:T(8,128)}, u32[]{:S(2)}) copy-start(f32[32,4096]{1,0:T(8,128)} %get-tuple-element.136) | copy-start | bytes 1572868
  557.3 2.9 copy-start.31
  (19 other events, 38.2 us)

commit v6 on v5

--- a/solution.py
+++ b/solution.py
@@ -11,12 +11,13 @@
 MESH = pl.DeviceIdType.MESH
 LAG = 2
 GATHER_LAG = 2
-GATHER_RATE = 1
+REST_START = 1
+REST_DELAY = 8
+DEEP_AT = 10
 COLLECT_LAG = 2
 AHEAD = 3
 HOP_LAG = 1
-FIRST_PIECE = 512
-LAST_PIECE = 512
+FIRST_PIECE = 1024
 PAIR = 128
 HDIM = 64
 MH = 4
@@ -199,19 +200,18 @@
         return pltpu.make_async_copy(self.holders[number].at[inner],
                                      self.cut(self.results, k, z), self.out_sem.at[k])
 
-    def start(self):
+    def start(self, k):
         y, x, core, z = place(self.side)
-        for k in range(self.count):
-            self.take(k).start()
-            own = self.cut(self.sources, k, y, x, core)
-
-            @pl.when(z < self.depth - 1)
-            def _(k=k, own=own):
-                self.along_z(k, z, 1, own).start()
-
-            @pl.when(z > 0)
-            def _(k=k, own=own):
-                self.along_z(k, z, -1, own).start()
+        self.take(k).start()
+        own = self.cut(self.sources, k, y, x, core)
+
+        @pl.when(z < self.depth - 1)
+        def _():
+            self.along_z(k, z, 1, own).start()
+
+        @pl.when(z > 0)
+        def _():
+            self.along_z(k, z, -1, own).start()
 
     def step(self, i):
         side, depth = self.side, self.depth
@@ -255,11 +255,14 @@
         else:
             self.core_copy(k, zp).wait_recv()
 
+    def settle(self):
+        for k in range(self.count):
+            self.put(k).wait()
+
     def finish(self):
         side, depth = self.side, self.depth
         z = place(side)[3]
         for k in range(self.count):
-            self.put(k).wait()
             for zp in range(depth):
                 @pl.when(jnp.logical_and(zp <= z, z < depth - 1))
                 def _(k=k, zp=zp):
@@ -278,8 +281,8 @@
 
 
 class Reduce:
-    def __init__(self, side, depth, grads, gains=None, piece=1024):
-        self.side, self.depth = side, depth
+    def __init__(self, side, depth, grads, piece, deep_at):
+        self.side, self.depth, self.deep_at = side, depth, deep_at
         self.layout, self.views, self.outs = [], [], []
         self.width = width = piece
         devices = 2 * side * side * depth
@@ -287,16 +290,14 @@
             rows, cols = grad.shape[-2:]
             self.block = block = rows // devices
             lead = grad.shape[:-2]
-            self.views.append(grad.reshape(lead + (side, side, 2, depth, block, cols)))
+            self.views.append(lead + (side, side, 2, depth, block, cols))
             leads = range(lead[0]) if lead else (None,)
-            self.layout.append(
-                [(number, start) for number in leads for start in range(0, cols, width)]
-            )
+            self.layout += [
+                (len(self.outs), number, start) for number in leads for start in range(0, cols, width)
+            ]
             self.outs.append(jax.ShapeDtypeStruct(lead + (block, cols), F32))
-        self.count = count = sum(len(columns) for columns in self.layout)
-        self.steps = count + 3 * LAG
-        self.gains = gains is not None
-        most = max(side, depth) - 1
+        self.count = count = len(self.layout)
+        self.steps = count + deep_at + LAG
         dma = pltpu.SemaphoreType.DMA
         self.scratch = [
             pltpu.VMEM((count, side, side, depth, block, width), BF),
@@ -315,48 +316,22 @@
             dma((count, depth - 1)),
             dma((count, depth - 1)),
         ]
-        if self.gains:
-            self.views.append(gains)
-            self.outs.append(jax.ShapeDtypeStruct(gains.shape, F32))
-            self.scratch += [
-                pltpu.VMEM((4,) + gains.shape, F32),
-                pltpu.VMEM((4, most) + gains.shape, F32),
-                dma((4, most)),
-                dma((4, most)),
-            ]
-        any_space, vmem = pl.BlockSpec(memory_space=pl.ANY), pl.BlockSpec(memory_space=pltpu.VMEM)
-        self.in_specs = [any_space] * len(self.layout) + [vmem] * self.gains
-        self.out_specs = [vmem] * len(self.views)
 
     def bind(self, sources, outs, scratch):
         (self.mine, self.got_core, self.got_one, self.got_two, self.got_deep, self.total,
          self.local_sem, self.core_send, self.core_recv, self.one_send, self.one_recv,
-         self.two_send, self.two_recv, self.deep_send, self.deep_recv) = scratch[:15]
-        self.results = outs
-        if self.gains:
-            self.gain_in, self.gain_out = sources[-1], outs[-1]
-            self.gain_sum, self.gain_got, self.gain_send, self.gain_recv = scratch[15:]
-        self.pieces = []
-        for number, columns in enumerate(self.layout):
-            for lead, start in columns:
-                ref = sources[number] if lead is None else sources[number].at[lead]
-                self.pieces.append((ref, number, lead, start))
-
-    def core_wait(self, k):
+         self.two_send, self.two_recv, self.deep_send, self.deep_recv) = scratch
+        self.results, self.sources = outs, sources
+
+    def core_copy(self, k, source):
         y, x, core, z = place(self.side)
-        return remote(self.got_core.at[k], self.got_core.at[k], self.core_send.at[k],
+        return remote(source, self.got_core.at[k], self.core_send.at[k],
                       self.core_recv.at[k], device_at(self.side, y, x, 1 - core, z))
 
-    def start(self):
-        y, x, core, z = place(self.side)
-        for k, (ref, _, _, start) in enumerate(self.pieces):
-            spot = pl.ds(start, self.width)
-            remote(ref.at[:, :, 1 - core, :, :, spot], self.got_core.at[k], self.core_send.at[k],
-                   self.core_recv.at[k], device_at(self.side, y, x, 1 - core, z)).start()
-            pltpu.make_async_copy(ref.at[:, :, core, :, :, spot], self.mine.at[k],
-                                  self.local_sem.at[k]).start()
-        if self.gains:
-            self.gain_copy(0, 0).start()
+    def start(self, k):
+        core = place(self.side)[2]
+        self.core_copy(k, self.sources(k, 1 - core)).start()
+        pltpu.make_async_copy(self.sources(k, core), self.mine.at[k], self.local_sem.at[k]).start()
 
     def one_copy(self, k, hop, x_first):
         side = self.side
@@ -385,22 +360,6 @@
                       self.deep_send.at[k, hop - 1], self.deep_recv.at[k, hop - 1],
                       device_at(self.side, y, x, core, there))
 
-    def gain_count(self, stage):
-        return (1, self.side - 1, self.side - 1, self.depth - 1)[stage]
-
-    def gain_copy(self, stage, number):
-        side, depth, hop = self.side, self.depth, number + 1
-        y, x, core, z = place(side)
-        peer = (
-            device_at(side, y, x, 1 - core, z),
-            device_at(side, y, (x + hop) % side, core, z),
-            device_at(side, (y + hop) % side, x, core, z),
-            device_at(side, y, x, core, (z + hop) % depth),
-        )[stage]
-        source = self.gain_in if stage == 0 else self.gain_sum.at[stage - 1]
-        return remote(source, self.gain_got.at[stage, number], self.gain_send.at[stage, number],
-                      self.gain_recv.at[stage, number], peer)
-
     def both_orders(self, k, action):
         @pl.when(k % 2 == 0)
         def _():
@@ -420,7 +379,7 @@
 
     def after_core(self, k):
         side, depth, mine, got = self.side, self.depth, self.mine, self.got_core
-        self.core_wait(k).wait_recv()
+        self.core_copy(k, got.at[k]).wait_recv()
         pltpu.make_async_copy(got.at[k], mine.at[k], self.local_sem.at[k]).wait()
 
         def add(index, carry):
@@ -475,7 +434,9 @@
             return carry
 
         lax.fori_loop(0, depth, add, 0)
-        for hop in range(1, depth):
+
+    def send_deep(self, k):
+        for hop in range(1, self.depth):
             self.deep_copy(k, hop).start()
 
     def after_deep(self, k):
@@ -488,30 +449,20 @@
         self.total[k] = value
 
     def step(self, i):
-        stages = (self.after_core, self.after_one, self.after_two, self.after_deep)
-        for number, action in enumerate(stages):
-            lag = number * LAG
-
+        stages = (
+            (0, self.after_core),
+            (LAG, self.after_one),
+            (2 * LAG, self.after_two),
+            (self.deep_at, self.send_deep),
+            (self.deep_at + LAG, self.after_deep),
+        )
+        for lag, action in stages:
             @pl.when(jnp.logical_and(i >= lag, i < self.count + lag))
             def _(lag=lag, action=action):
                 action(i - lag)
 
-        for stage in range(4 if self.gains else 0):
-            @pl.when(i == stage + 1)
-            def _(stage=stage):
-                value = self.gain_in[...] if stage == 0 else self.gain_sum[stage - 1]
-                for number in range(self.gain_count(stage)):
-                    self.gain_copy(stage, number).wait_recv()
-                    value = value + self.gain_got[stage, number]
-                self.gain_sum[stage] = value
-                if stage < 3:
-                    for number in range(self.gain_count(stage + 1)):
-                        self.gain_copy(stage + 1, number).start()
-
     def finish(self):
-        if self.gains:
-            self.gain_out[...] = self.gain_sum[3]
-        for k, (_, number, lead, start) in enumerate(self.pieces):
+        for k, (number, lead, start) in enumerate(self.layout):
             spot = (slice(None), pl.ds(start, self.width))
             if lead is None:
                 self.results[number][spot] = self.total[k]
@@ -519,7 +470,7 @@
                 self.results[number][(lead,) + spot] = self.total[k]
 
         def drain(k, carry):
-            self.core_wait(k).wait_send()
+            self.core_copy(k, self.got_core.at[k]).wait_send()
 
             def sent(x_first):
                 for hop in range(1, self.side):
@@ -532,9 +483,6 @@
             return carry
 
         lax.fori_loop(0, self.count, drain, 0)
-        for stage in range(4 if self.gains else 0):
-            for number in range(self.gain_count(stage)):
-                self.gain_copy(stage, number).wait_send()
 
 
 def split_refs(refs, *counts):
@@ -549,72 +497,6 @@
     return pltpu.CompilerParams(
         collective_id=call_id, has_side_effects=True, vmem_limit_bytes=mib * 1024 * 1024
     )
-
-
-def gather_kernel(plan, slots, rows, *refs):
-    n = len(plan.views)
-    (picks_ref,), sources, (counts_ref,), outs, scratch = split_refs(refs, 1, n, 1, n)
-    plan.bind(sources, outs, scratch)
-    blocks = picks_ref.shape[1] // 128
-    turns = max(plan.steps, blocks)
-    greet(plan.side, plan.depth)
-    plan.start()
-
-    def run(i, carry):
-        for number in range(plan.steps):
-            @pl.when(i == number)
-            def _(number=number):
-                plan.step(number)
-
-        @pl.when(i < blocks)
-        def _():
-            count_block(i, rows, slots, picks_ref, counts_ref)
-
-        return carry
-
-    lax.fori_loop(0, turns, run, 0)
-    plan.finish()
-
-
-def gather_and_count(side, depth, shards, picks, slots, rows, call_id):
-    plan = Gather(side, depth, shards, FIRST_PIECE)
-    any_space, vmem = pl.BlockSpec(memory_space=pl.ANY), pl.BlockSpec(memory_space=pltpu.VMEM)
-    results = pl.pallas_call(
-        functools.partial(gather_kernel, plan, slots, rows),
-        out_shape=(jax.ShapeDtypeStruct((2, MH, slots, rows), BF),) + tuple(plan.outs),
-        in_specs=[vmem] + [any_space] * len(plan.views),
-        out_specs=(vmem,) + (any_space,) * len(plan.views),
-        scratch_shapes=plan.scratch,
-        compiler_params=params(call_id, 32),
-    )(picks, *plan.views)
-    return results[0], plan.restore(results[1:])
-
-
-def reduce_kernel(plan, *refs):
-    n = len(plan.views)
-    sources, outs, scratch = split_refs(refs, n, n)
-    plan.bind(sources, outs, scratch)
-    greet(plan.side, plan.depth)
-    plan.start()
-
-    def run(i, carry):
-        plan.step(i)
-        return carry
-
-    lax.fori_loop(0, max(plan.steps, 5), run, 0)
-    plan.finish()
-
-
-def reduce_grads(side, depth, grads, gains, call_id):
-    plan = Reduce(side, depth, grads, gains, LAST_PIECE)
-    return pl.pallas_call(
-        functools.partial(reduce_kernel, plan),
-        out_shape=tuple(plan.outs),
-        in_specs=plan.in_specs,
-        out_specs=tuple(plan.out_specs),
-        scratch_shapes=plan.scratch,
-        compiler_params=params(call_id, 60),
-    )(*plan.views)
 
 
 def half_masks(width):
@@ -793,19 +675,64 @@
         lax.fori_loop(0, self.pairs, drain, 0)
 
 
-def forward_kernel(gather, exchange, *refs):
+def project(normed_ref, weight, out_ref):
+    width = 2 * PAIR
+
+    def run(part, carry):
+        cols = pl.ds(pl.multiple_of(part * width, width), width)
+        piece = weight[..., cols].reshape(normed_ref.shape[1], width)
+        out_ref[:, cols] = dot_plain(normed_ref[...], piece).astype(BF)
+        return carry
+
+    lax.fori_loop(0, out_ref.shape[1] // width, run, 0)
+
+
+def forward_kernel(first, rest, exchange, slots, *refs):
     depth, rows, pairs = exchange.depth, exchange.rows, exchange.pairs
-    n = len(gather.views)
-    (q_ref, k_ref, v_ref), shards, (att_ref, lse_ref, keys, vals), full, swap, rest = split_refs(
-        refs, 3, n, 4, n, len(exchange.scratch))
-    gather.bind(shards, full, rest)
+    n = len(rest.views)
+    ((picks_ref, normed_ref), shard, shards, outs, (qkv,), full, swap, held,
+     others) = split_refs(refs, 2, 1, n, 8, 1, n, len(exchange.scratch), len(first.scratch))
+    counts_ref, q_ref, k_ref, v_ref, att_ref, lse_ref, keys, vals = outs
+    first.bind(shard, (qkv,), held)
+    rest.bind(shards, full, others)
     exchange.bind((k_ref, v_ref), (keys, vals), swap)
     z = lax.axis_index("fsdp")
-    greet(gather.side, depth)
+    blocks = picks_ref.shape[1] // 128
+    per_turn = -(-blocks // first.steps)
+    greet(first.side, depth)
+    for k in range(first.count):
+        first.start(k)
+
+    def gather(i, carry):
+        for turn in range(first.steps):
+            @pl.when(i == turn)
+            def _(turn=turn):
+                first.step(turn)
+                if 0 <= turn - REST_START < rest.count:
+                    rest.start(turn - REST_START)
+                if turn >= REST_DELAY:
+                    rest.step(turn - REST_DELAY)
+
+        for inner in range(per_turn):
+            block = i * per_turn + inner
+
+            @pl.when(block < blocks)
+            def _(block=block):
+                count_block(block, rows, slots, picks_ref, counts_ref)
+
+        return carry
+
+    lax.fori_loop(0, first.steps, gather, 0)
+    for k in range(max(0, first.steps - REST_START), rest.count):
+        rest.start(k)
+    first.settle()
+    project(normed_ref, qkv.at[1], k_ref)
+    project(normed_ref, qkv.at[2], v_ref)
     ahead = min(AHEAD, pairs)
     for p in range(ahead):
         exchange.offer(p)
-    gather.start()
+    project(normed_ref, qkv.at[0], q_ref)
+    done = max(0, first.steps - REST_DELAY)
     delay = (depth - 2) * HOP_LAG + 1
     turns = pairs + delay
 
@@ -816,10 +743,11 @@
 
         exchange.step(i)
         for turn in range(turns):
-            @pl.when(i == turn)
-            def _(turn=turn):
-                for number in range(turn * GATHER_RATE, min((turn + 1) * GATHER_RATE, gather.steps)):
-                    gather.step(number)
+            number = done + turn
+            if number < rest.steps:
+                @pl.when(i == turn)
+                def _(number=number):
+                    rest.step(number)
 
         @pl.when(i >= delay)
         def _():
@@ -829,33 +757,42 @@
         return carry
 
     lax.fori_loop(0, turns, run, 0)
-    for number in range(turns * GATHER_RATE, gather.steps):
-        gather.step(number)
+    for number in range(done + turns, rest.steps):
+        rest.step(number)
     exchange.finish()
-    gather.finish()
-
-
-def attention_forward(side, depth, q, k, v, shards, call_id):
-    rows, width = q.shape[0] // 2, q.shape[1]
+    rest.settle()
+    first.finish()
+    rest.finish()
+
+
+def attention_forward(side, depth, picks, normed, w_qkv, shards, slots, call_id):
+    rows, width = normed.shape[0] // 2, normed.shape[1]
     pairs = width // PAIR
-    gather, exchange = Gather(side, depth, shards), Exchange(depth, rows, pairs)
+    first, rest = Gather(side, depth, (w_qkv,), FIRST_PIECE), Gather(side, depth, shards)
+    exchange = Exchange(depth, rows, pairs)
     any_space, vmem = pl.BlockSpec(memory_space=pl.ANY), pl.BlockSpec(memory_space=pltpu.VMEM)
     spread = jax.ShapeDtypeStruct((pairs, depth, rows, PAIR), BF)
+    flat = jax.ShapeDtypeStruct(normed.shape, BF)
     results = pl.pallas_call(
-        functools.partial(forward_kernel, gather, exchange),
+        functools.partial(forward_kernel, first, rest, exchange, slots),
         out_shape=(
-            jax.ShapeDtypeStruct(q.shape, BF),
+            jax.ShapeDtypeStruct((2, MH, slots, rows), BF),
+            flat,
+            flat,
+            flat,
+            flat,
             jax.ShapeDtypeStruct((2 * pairs, 2 * rows), F32),
             spread,
             spread,
         )
-        + tuple(gather.outs),
-        in_specs=[vmem] * 3 + [any_space] * len(gather.views),
-        out_specs=(vmem,) * 4 + (any_space,) * len(gather.views),
-        scratch_shapes=exchange.scratch + gather.scratch,
+        + tuple(first.outs)
+        + tuple(rest.outs),
+        in_specs=[vmem] * 2 + [any_space] * (1 + len(rest.views)),
+        out_specs=(vmem,) * 9 + (any_space,) * len(rest.views),
+        scratch_shapes=exchange.scratch + first.scratch + rest.scratch,
         compiler_params=params(call_id, 56),
-    )(q, k, v, *gather.views)
-    return results[:4], gather.restore(results[4:])
+    )(picks, normed, *first.views, *rest.views)
+    return results[:8], first.restore(results[8:9])[0], rest.restore(results[9:])
 
 
 class Collect:
@@ -866,7 +803,7 @@
         self.scratch = [
             pltpu.VMEM(shape, BF),
             pltpu.VMEM(shape, BF),
-            pltpu.VMEM(shape, BF),
+            pltpu.VMEM((pairs, 2, rows, PAIR), BF),
             pltpu.VMEM((2, rows, PAIR), F32),
             dma((2, pairs, depth)),
             dma((2, pairs, depth)),
@@ -874,39 +811,44 @@
         self.steps = pairs + (depth - 1) * COLLECT_LAG + 1
 
     def bind(self, scratch):
-        (self.part, self.from_left, self.from_right, self.whole, self.send_sem,
+        (self.part, self.arrived, self.second, self.whole, self.send_sem,
          self.recv_sem) = scratch
 
-    def hop(self, p, zd, move):
+    def hop(self, p, zd, move, final):
         z = lax.axis_index("fsdp")
-        target = self.from_left if move > 0 else self.from_right
         way = (move + 1) // 2
-        return remote(self.part.at[p, zd], target.at[p, zd], self.send_sem.at[way, p, zd],
+        target = self.second.at[p] if final and move < 0 else self.arrived.at[p, zd]
+        return remote(self.part.at[p, zd], target, self.send_sem.at[way, p, zd],
                       self.recv_sem.at[way, p, zd], (lax.axis_index("dp"), z + move))
 
     def flow(self, p, move):
         depth = self.depth
         z = lax.axis_index("fsdp")
         first = z == 0 if move > 0 else z == depth - 1
-        arrived = self.from_left if move > 0 else self.from_right
         for zd in range(depth - 1, -1, -1) if move > 0 else range(depth):
             beyond = zd > z if move > 0 else zd < z
 
-            @pl.when(jnp.logical_and(jnp.logical_not(first), jnp.logical_or(beyond, zd == z)))
+            @pl.when(jnp.logical_and(jnp.logical_not(first), beyond))
             def _(zd=zd):
-                self.hop(p, zd, move).wait_recv()
+                self.hop(p, zd, move, False).wait_recv()
 
                 def add(part, carry):
-                    self.part[p, zd, part] = self.part[p, zd, part] + arrived[p, zd, part]
+                    self.part[p, zd, part] = self.part[p, zd, part] + self.arrived[p, zd, part]
                     return carry
 
-                @pl.when(zd != z)
-                def _():
-                    lax.fori_loop(0, 2, add, 0)
-
-            @pl.when(beyond)
+                lax.fori_loop(0, 2, add, 0)
+
+            @pl.when(jnp.logical_and(jnp.logical_not(first), zd == z))
             def _(zd=zd):
-                self.hop(p, zd, move).start()
+                self.hop(p, zd, move, True).wait_recv()
+
+            @pl.when(zd == z + move)
+            def _(zd=zd):
+                self.hop(p, zd, move, True).start()
+
+            @pl.when(jnp.logical_and(beyond, zd != z + move))
+            def _(zd=zd):
+                self.hop(p, zd, move, False).start()
 
     def step(self, i):
         depth = self.depth
@@ -927,11 +869,11 @@
 
         @pl.when(z > 0)
         def _():
-            whole[...] = whole[...] + self.from_left[p, z].astype(F32)
+            whole[...] = whole[...] + self.arrived[p, z].astype(F32)
 
         @pl.when(z < depth - 1)
         def _():
-            whole[...] = whole[...] + self.from_right[p, z].astype(F32)
+            whole[...] = whole[...] + self.second[p].astype(F32)
 
         return whole[...]
 
@@ -944,24 +886,57 @@
                 for move in (1, -1):
                     @pl.when(zd > z if move > 0 else zd < z)
                     def _(zd=zd, move=move):
-                        self.hop(p, zd, move).wait_send()
+                        self.hop(p, zd, move, False).wait_send()
             return carry
 
         lax.fori_loop(0, self.pairs, drain, 0)
 
 
-def backward_kernel(plan, collect, *refs):
-    depth, rows, pairs = collect.depth, collect.rows, collect.pairs
-    n = len(plan.views)
-    ins, sources, (dq_ref, dk_ref, dv_ref), sums, swap, rest = split_refs(
-        refs, 8, n, 3, n, len(collect.scratch))
-    q_ref, k_ref, v_ref, keys, vals, lse_ref, att_ref, g_ref = ins
-    plan.bind(sources, sums, rest)
+def produce(late, stage, kind, half, normed_ref, grad_ref):
+    side, depth, block, width = late.side, late.depth, late.block, late.width
+    k = 2 * kind + half
+    run = depth * block
+    for start in range(0, normed_ref.shape[1], 2 * PAIR):
+        value = dot_first(
+            normed_ref[:, start : start + 2 * PAIR], grad_ref[:, half * width : (half + 1) * width]
+        ).astype(BF)
+        for row in range(0, 2 * PAIR, run):
+            number = (start + row) // run
+            y, x, core = number // (2 * side), (number // 2) % side, number % 2
+            stage[k, y, x, :, :, core * width : (core + 1) * width] = value[row : row + run].reshape(
+                depth, block, width)
+
+
+def backward_kernel(early, late, collect, *refs):
+    side, depth, rows, pairs = early.side, collect.depth, collect.rows, collect.pairs
+    n = len(early.views)
+    ins, grads, (dq_ref, dk_ref, dv_ref), sums, (qkv_sum,), swap, first, second = split_refs(
+        refs, 9, n, 3, n, 1, len(collect.scratch), len(early.scratch))
+    q_ref, k_ref, v_ref, keys, vals, lse_ref, att_ref, g_ref, normed_ref = ins
+
+    def part_of(k, half):
+        number, lead, start = early.layout[k]
+        ref = grads[number] if lead is None else grads[number].at[lead]
+        return ref.at[:, :, half, :, :, pl.ds(start, early.width)]
+
+    early.bind(part_of, sums, first)
+    stage = early.got_core
+
+    def late_part(k, half):
+        lanes = pl.ds(pl.multiple_of(half * late.width, late.width), late.width)
+        return stage.at[k, :, :, :, :, lanes]
+
+    late.bind(late_part, (qkv_sum,), second)
     collect.bind(swap)
     z = lax.axis_index("fsdp")
-    greet(plan.side, depth)
-    plan.start()
+    greet(side, depth)
+    for k in range(early.count):
+        early.start(k)
     last = (depth - 1) * COLLECT_LAG
+    ready = max(pairs, early.count)
+    settled = max(pairs + last, ready + 2)
+    late_at = settled - 1
+    due = [ready, ready + 1, settled, settled + 1, settled + 2, settled + 3]
 
     def run(i, carry):
         @pl.when(i < pairs)
@@ -970,7 +945,7 @@
                           g_ref, dq_ref, dk_ref, dv_ref, collect.part)
 
         collect.step(i)
-        plan.step(i)
+        early.step(i)
 
         @pl.when(jnp.logical_and(i >= last, i < last + pairs))
         def _():
@@ -980,26 +955,49 @@
             dk_ref[pl.ds(0, rows), cols] = value[0].astype(BF)
             dv_ref[pl.ds(0, rows), cols] = value[1].astype(BF)
 
+        late.step(i - late_at)
+        for number, when in enumerate(due):
+            @pl.when(i == when)
+            def _(number=number):
+                kind = number // 2
+                produce(late, stage, kind, number % 2, normed_ref, (dq_ref, dk_ref, dv_ref)[kind])
+                late.start(number)
+
         return carry
 
-    lax.fori_loop(0, max(pairs + last, plan.steps), run, 0)
+    lax.fori_loop(0, max(early.steps, late_at + late.steps), run, 0)
     collect.finish()
-    plan.finish()
-
-
-def attention_backward(side, depth, q, k, v, keys, vals, lse, att, grad_att, grads, call_id):
+    early.finish()
+    late.finish()
+
+
+def attention_backward(side, depth, q, k, v, keys, vals, lse, att, grad_att, normed, grads, w_qkv,
+                       call_id):
     rows, width = q.shape[0] // 2, q.shape[1]
-    plan, collect = Reduce(side, depth, grads), Collect(depth, rows, width // PAIR)
-    vmem = pl.BlockSpec(memory_space=pltpu.VMEM)
+    early = Reduce(side, depth, grads, width, DEEP_AT)
+    late = Reduce(side, depth, (w_qkv,), width // 2, 2 * LAG)
+    collect = Collect(depth, rows, width // PAIR)
+    any_space, vmem = pl.BlockSpec(memory_space=pl.ANY), pl.BlockSpec(memory_space=pltpu.VMEM)
     results = pl.pallas_call(
-        functools.partial(backward_kernel, plan, collect),
-        out_shape=(jax.ShapeDtypeStruct(q.shape, BF),) * 3 + tuple(plan.outs),
-        in_specs=[vmem] * 8 + plan.in_specs,
-        out_specs=(vmem,) * 3 + tuple(plan.out_specs),
-        scratch_shapes=collect.scratch + plan.scratch,
-        compiler_params=params(call_id, 62),
-    )(q, k, v, keys, vals, lse, att, grad_att, *plan.views)
-    return results[:3], results[3:]
+        functools.partial(backward_kernel, early, late, collect),
+        out_shape=(jax.ShapeDtypeStruct(q.shape, BF),) * 3 + tuple(early.outs) + tuple(late.outs),
+        in_specs=[vmem] * 9 + [any_space] * len(grads),
+        out_specs=(vmem,) * (4 + len(grads)),
+        scratch_shapes=collect.scratch + early.scratch + late.scratch,
+        compiler_params=params(call_id, 63),
+    )(
+        q,
+        k,
+        v,
+        keys,
+        vals,
+        lse,
+        att,
+        grad_att,
+        normed,
+        *[grad.reshape(view) for grad, view in zip(grads, early.views)],
+    )
+    return results[:3], results[3:-1], results[-1]
 
 
 def count_block(b, rows, slots, picks_ref, counts_ref):
@@ -1198,32 +1196,26 @@
     offsets = jnp.maximum(request[:, 0].reshape(2, slots), 0)
     picked = (jnp.arange(slots, dtype=jnp.int32) // capacity)[None] * shard_rows + offsets
     ids = jnp.stack([picked // SUB, picked % SUB], axis=1).reshape(4, slots)
-    picks = jnp.stack([slot_prompt[0], slot_cont[0]]).transpose(3, 0, 2, 1)
-    picks, served = lax.optimization_barrier((picks, served))
-    tables = [swap(served[0])]
-    counts, (qkv_full,) = gather_and_count(
-        side, depth, (w_qkv,), picks.reshape(picks.shape[0], -1), slots, rows, 0
-    )
-
     x_rows = jnp.concatenate([x_prompt[0], x_cont[0]], axis=0).astype(F32)
     dy_low = jnp.concatenate([cot_prompt[0], cot_cont[0]], axis=0)
     normed, inverse = normalize(x_rows, gain_attn)
     normed = normed.astype(BF)
-    queries = mm(normed, qkv_full[0]).astype(BF)
-    keys = mm(normed, qkv_full[1]).astype(BF)
-    vals = mm(normed, qkv_full[2]).astype(BF)
-    queries, tables[0] = lax.optimization_barrier((queries, tables[0]))
-    (att, lse, all_keys, all_vals), full = attention_forward(
+    picks = jnp.stack([slot_prompt[0], slot_cont[0]]).transpose(3, 0, 2, 1)
+    picks, served = lax.optimization_barrier((picks.reshape(picks.shape[0], -1), served))
+    tables = [swap(served[0])]
+    results, qkv_full, full = attention_forward(
         side,
         depth,
-        queries,
-        keys,
-        vals,
+        picks,
+        normed,
+        w_qkv,
         (w_attn_out, w_mem_query, sub_keys, w_gate, w_mem_out),
-        1,
+        slots,
+        0,
     )
+    counts, queries, keys, vals, att, lse, all_keys, all_vals = results
     attn_out_full, query_full, keys_full, gate_full, mem_out_full = full
-    att, late = lax.optimization_barrier((att, served[1]))
+    att, late, tables[0] = lax.optimization_barrier((att, served[1], tables[0]))
     tables.append(swap(late))
     hidden = x_rows + mm(att, attn_out_full)
     normed2, inverse2 = normalize(hidden, gain_mem)
@@ -1247,10 +1239,12 @@
         mm(mixing[part], grad_memory[part * rows : (part + 1) * rows]).astype(BF)
         for part in range(2)
     ]
-    arrived = swap(slot_grads[1])
+    arrived = [None, swap(slot_grads[1])]
     grad_query, grad_keys = slot_weights_back(
         ids, weights, jnp.stack(tables), grad_memory, mquery, keys_full, block
     )
+    grad_query, arrived[1], late = lax.optimization_barrier((grad_query, arrived[1], slot_grads[0]))
+    arrived[0] = swap(late)
     grad_normed2 = mm_t(grad_query, query_full) + mm_t(grad_gate, gate_full)
     grad_query_w = mm_l(normed2, grad_query).astype(BF)
     grad_gate_w = mm_l(normed2, grad_gate).astype(BF)
@@ -1260,7 +1254,7 @@
     grad_attn_out = mm_l(att, hidden_low).astype(BF)
     grad_att = mm_t(hidden_low, attn_out_full).astype(BF)
     grad_att, arrived = lax.optimization_barrier((grad_att, arrived))
-    (grad_q, grad_k, grad_v), early = attention_backward(
+    (grad_q, grad_k, grad_v), early, qkv_shard = attention_backward(
         side,
         depth,
         queries,
@@ -1271,25 +1265,20 @@
         lse,
         att,
         grad_att,
+        normed,
         (grad_query_w, grad_keys, grad_gate_w, grad_mem_out.astype(BF), grad_attn_out),
-        2,
+        qkv_full,
+        1,
     )
-    grad_q, late = lax.optimization_barrier((grad_q, slot_grads[0]))
-    grad_rows = mm_l(
-        jnp.concatenate(serve_picks, axis=0), jnp.concatenate([swap(late), arrived], axis=0)
-    )
+    grad_rows = mm_l(jnp.concatenate(serve_picks, axis=0), jnp.concatenate(arrived, axis=0))
     grad_normed = (
         mm_t(grad_q, qkv_full[0]) + mm_t(grad_k, qkv_full[1]) + mm_t(grad_v, qkv_full[2])
     )
     grad_x, gain_attn_part = norm_backward(x_rows, inverse, gain_attn, grad_normed)
     grad_x = grad_hidden + grad_x
-    grad_qkv = jnp.stack([mm_l(normed, piece).astype(BF) for piece in (grad_q, grad_k, grad_v)])
-    gains = jnp.concatenate([gain_attn_part, gain_mem_part]).reshape(2 * cols // 128, 128)
-    qkv_shard, gain_sums = reduce_grads(side, depth, (grad_qkv,), gains, 3)
-    own = lax.axis_index("dp") * depth + lax.axis_index("fsdp")
-    gain_shards = lax.dynamic_index_in_dim(
-        gain_sums.reshape(2, owners, block), own, axis=1, keepdims=False
-    )
+    gains = jnp.stack([gain_attn_part, gain_mem_part]).reshape(2, owners, block)
+    gains = lax.all_to_all(gains.transpose(1, 0, 2), ALL, split_axis=0, concat_axis=0, tiled=True)
+    gain_shards = jnp.sum(gains, axis=0)
     sub_shard = early[1].reshape(block, 2, HALF).transpose(1, 0, 2).reshape(2 * block, HALF)
     return (
         out[None, :rows],

time: 566 us -> 520 us (0.919)
  Pallas kernels: 388 us -> 351 us
  matrix products: 101 us -> 88.8 us
    pallas_call x4 -> x2, Pallas kernels: 355 us -> 318 us  [the longest x1 163 us: attention_forward(): pl.pallas_call(functools.partial(forward_kernel, first, rest, exchange, s...]
    dot_general x10 -> x7, matrix products: 33.1 us -> 29.1 us  [mm_l(): lax.dot_general(left, right, (((0,), (0,)), ((), ())), preferred_element_...]
    dot_general x11 -> x8, matrix products: 36.8 us -> 34.1 us  [mm(): return jnp.dot(left, right, preferred_element_type=F32)]
  transfers between devices with their start and end apart: 5 -> 6, of which waited for: 2 -> 2; matrix products, arithmetic and copies ran while one was open for 12% -> 15% of each run, Pallas kernels for 21% -> 38%
where the time goes in v6:
time: 520 us; the launch traced here: 515 us
  Pallas kernels  351 us (68%)
  matrix products  88.8 us (17%)
  starting transfers between devices  30 us (6%)
  local copies, waits for them, and re-layouts  16.3 us (3%)
  other arithmetic  15.8 us (3%)
  waiting for transfers between devices  11.5 us (2%)
    pallas_call x1, Pallas kernels, attention_forward(): pl.pallas_call(functools.partial(forward_kernel, first, rest, exchange, s...  163 us
    pallas_call x1, Pallas kernels, attention_backward(): pl.pallas_call(functools.partial(backward_kernel, early, late, collect),...  155 us
    dot_general x8, matrix products, mm(): return jnp.dot(left, right, preferred_element_type=F32)  34.1 us
    dot_general x7, matrix products, mm_l(): lax.dot_general(left, right, (((0,), (0,)), ((), ())), preferred_element_...  29.1 us
    dot_general x7, matrix products, mm_t(): lax.dot_general(left, right, (((1,), (1,)), ((), ())), preferred_element_...  25.6 us
    pallas_call x1, Pallas kernels, slot_weights_back(): pl.pallas_call(functools.partial(picks_back_kernel, block), grid=(MH, 2),...  19.8 us
    all_to_all x4, starting transfers between devices, swap(): lax.all_to_all(values, ALL, split_axis=0, concat_axis=0, tiled=True)  19.7 us
    pallas_call x1, Pallas kernels, slot_weights(): pl.pallas_call(picks_kernel, grid=(2, MH), out_shape=(jax.ShapeDtypeStruc...  13.4 us
  transfers between devices with their start and end apart: 6, of which 2 were waited for; matrix products, arithmetic and copies ran while one was open for 15% of the time, Pallas kernels for 38%

profile of v6, /device:TPU:0, one launch (start us, length us, event | category | flops | bytes accessed | tf_op | source)
XLA Modules:
  0.0 514.6 jit_solution(5596192840000206409)
XLA Ops:
  2.1 7.3 %all-to-all-start = ((s32[2,32,16]{2,0,1:T(2,128)}), s32[2,32,16]{2,0,1:T(2,128)S(1)}, u32[]{:S(2)}, u32[]{:S(2)}) async-start(s32[2,32,16]{2,0,1:T(2,128)} %bitcast.3), calls=%async_computation | async-start | bytes 65536 | tf_op jit(solution)/shard_map/all_to_all | solution.py:1187
  12.3 4.4 all-to-all-done
  16.9 5.7 %convolution_convert_fusion.9 = bf16[512,1024]{1,0:T(8,128)(2,1)} fusion(bf16[2048,1024]{1,0:T(8,128)(2,1)} %param.28, s32[512]{0:T(512)S(1)} %eq.32), kind=kOutput, calls=%fused_computation.47 | convolution fusion | flops 2149056512 | bytes 5244928 | tf_op jit(solution)/shard_map/dot_general | solution.py:30
  22.6 3.4 convolution_convert_fusion.8
  26.0 3.3 all-to-all-start.1
  31.6 163.2 %shard_map.255 = (bf16[2,4,512,256]{3,2,1,0:T(8,128)(2,1)}, bf16[512,1024]{1,0:T(8,128)(2,1)}, bf16[512,1024]{1,0:T(8,128)(2,1)}, bf16[512,1024]{1,0:T(8,128)(2,...) custom-call(s32[32,2048]{1,0:T(8,128)} %reshape.296.refs_0_, ...), custom_call_target="tpu_custom_call" | custom-call | tf_op jit(solution)/shard_map/pallas_call | solution.py:776
  194.8 4.4 fusion.20
  199.1 3.0 fusion.39
  202.2 2.7 iota_compare_fusion
  204.8 4.0 all-to-all-start.2
  208.8 3.5 multiply_reduce_fusion.2
  212.6 9.8 %convolution_convert_fusion.1.query_ref = bf16[512,4096]{1,0:T(8,128)(2,1)} fusion(bf16[512,1024]{1,0:T(8,128)(2,1)S(1)} %multiply_convert_fusion.3, bf16[1024,4096]{1,0:T(8,128)(2,1)} %bitcast.133), kind=kOutput, calls=%fused_computation.5 | convolution fusion | flops 4297064448 | bytes 13631488 | tf_op jit(solution)/shard_map/dot_general | solution.py:30
  222.4 13.4 %shard_map.256 = (f32[2,4,512,256]{3,2,1,0:T(8,128)}, bf16[2,512,256]{2,1,0:T(8,128)(2,1)}) custom-call(s32[4,512]{1,0:T(4,128)} %reshape.306.ids_ref, bf16[2,4,512,256]{3,2,1,0:T(8,128)(2,1)} %get-tuple-element.58.counts_ref, bf16[512,4096]{1,0:T(8,128)(2,1)} %convolution_convert_fusion.1.query_ref, bf16[2048,512]{1,0:T(8,128)(2,1)} %bitcast.137), custom_call_target="tpu_custom_call" | custom-call | flops 4294967296 | bytes 25165824 | tf_op jit(solution)/shard_map/pallas_call | solution.py:1061
  240.2 5.7 %multiply_convert_fusion = (bf16[512,1024]{1,0:T(8,128)(2,1)}, bf16[512,1024]{1,0:T(8,128)(2,1)S(1)}, bf16[512,1024]{1,0:T(8,128)(2,1)}) fusion(f32[512,1024]{1,0:T(8,128)} %fusion.20, f32[256,1024]{1,0:T(8,128)S(1)} %fusion.22, f32[256,1024]{1,0:T(8,128)} %fusion.25, bf16[512,1024]{1,0:T(8,128)(2,1)} %copy-done.18, bf16[1024,1024]{1,0:T(8,128)(2,1)S(1)} %bitcast.111), kind=kOutput, calls=%fused_computation.32 | convolution fusion | flops 1082654720 | bytes 10485760 | tf_op jit(solution)/shard_map/dot_general | solution.py:30
  247.3 6.1 %all-to-all-start.3 = ((bf16[32,16,1024]{2,1,0:T(8,128)(2,1)}), bf16[32,16,1024]{2,1,0:T(8,128)(2,1)}, u32[]{:S(2)}, u32[]{:S(2)}) async-start(bf16[32,16,1024]{2,1,0:T(8,128)(2,1)} %bitcast.109), calls=%async_computation.3 | async-start | bytes 2097152 | tf_op jit(solution)/shard_map/all_to_all | solution.py:1192
  253.5 3.2 add_convert_fusion
  256.6 2.8 pad_maximum_fusion.1.table_ref
  262.7 2.6 convolution_convert_fusion.3
  265.3 2.6 convolution_convert_fusion.4
  267.9 19.8 %shard_map.257 = (bf16[512,4096]{1,0:T(8,128)(2,1)}, bf16[1024,1024]{1,0:T(8,128)(2,1)}) custom-call(s32[4,512]{1,0:T(4,128)} %reshape.306.ids_ref, f32[2,4,512,256]{3,2,1,0:T(8,128)} %get-tuple-element.66.weight_ref, bf16[2,512,1024]{2,1,0:T(8,128)(2,1)} %pad_maximum_fusion.1.table_ref, bf16[512,1024]{1,0:T(8,128)(2,1)} %copy-done.14, ...), custom_call_target="tpu_custom_call" | custom-call | flops 6442450944 | bytes 25165824 | tf_op jit(solution)/shard_map/pallas_call | solution.py:1129
  287.8 8.4 %fusion.40 = f32[512,1024]{1,0:T(8,128)S(1)} fusion(bf16[512,4096]{1,0:T(8,128)(2,1)} %get-tuple-element.68, bf16[1024,4096]{1,0:T(8,128)(2,1)} %bitcast.134), kind=kOutput, calls=%fused_computation.103 | convolution fusion | flops 4294967296 | bytes 14680064 | tf_op jit(solution)/shard_map/dot_general | solution.py:34
  296.2 3.0 multiply_reduce_fusion
  299.1 6.3 %all-to-all-start.4 = ((bf16[32,16,1024]{2,1,0:T(8,128)(2,1)}), bf16[32,16,1024]{2,1,0:T(8,128)(2,1)}, u32[]{:S(2)}, u32[]{:S(2)}) async-start(bf16[32,16,1024]{2,1,0:T(8,128)(2,1)} %bitcast.29), calls=%async_computation.4 | async-start | bytes 2097152 | tf_op jit(solution)/shard_map/all_to_all | solution.py:1192
  305.5 3.8 subtract_add_fusion
  309.4 4.4 convolution_convert_fusion.2
  316.7 6.8 %convolution_convert_fusion = bf16[1024,4096]{1,0:T(8,128)(2,1)} fusion(bf16[512,1024]{1,0:T(8,128)(2,1)S(1)} %copy-done.20, bf16[512,4096]{1,0:T(8,128)(2,1)S(1)} %copy-done.39), kind=kOutput, calls=%fused_computation.4 | convolution fusion | flops 4299161600 | bytes 13631488 | tf_op jit(solution)/shard_map/dot_general | solution.py:38
  323.4 7.1 %all-to-all-done.4 = bf16[32,16,1024]{2,1,0:T(8,128)(2,1)} async-done(((bf16[32,16,1024]{2,1,0:T(8,128)(2,1)}), bf16[32,16,1024]{2,1,0:T(8,128)(2,1)}, u32[]{:S(2)}, u32[]{:S(2)}) %all-to-all-start.4) | async-done | bytes 1048608 | tf_op jit(solution)/shard_map/all_to_all | solution.py:1192
  330.5 154.5 %shard_map.258 = (bf16[512,1024]{1,0:T(8,128)(2,1)}, bf16[512,1024]{1,0:T(8,128)(2,1)}, bf16[512,1024]{1,0:T(8,128)(2,1)}, f32[32,4096]{1,0:T(8,128)}, f32[32,10...) custom-call(bf16[512,1024]{1,0:T(8,128)(2,1)} %get-tuple-element.69.ref, ...), custom_call_target="tpu_custom_call" | custom-call | tf_op jit(solution)/shard_map/pallas_call | solution.py:981
  485.1 3.3 fusion.41
  490.6 3.0 fusion.12
  494.4 2.9 all-to-all-start.5
  499.7 8.4 %fusion = f32[2048,1024]{1,0:T(8,128)} fusion(pred[512,2048]{1,0:T(32,128)(4,1)S(1)} %copy-done.16, pred[512,2048]{1,0:T(32,128)(4,1)S(1)} %copy-done.17, bf16[512,1024]{1,0:T(8,128)(2,1)} %bitcast.28, bf16[512,1024]{1,0:T(8,128)(2,1)} %bitcast.30), kind=kOutput, calls=%fused_computation | convolution fusion | flops 4301258752 | bytes 12582912 | tf_op jit(solution)/shard_map/dot_general | solution.py:38
  (127 shorter events, 30.6 us)
Async XLA Ops:
  2.1 14.6 %all-to-all-start = ((s32[2,32,16]{2,0,1:T(2,128)}), s32[2,32,16]{2,0,1:T(2,128)S(1)}, u32[]{:S(2)}, u32[]{:S(2)}) async-start(s32[2,32,16]{2,0,1:T(2,128)} %bitcast.3), calls=%async_computation | async-start | bytes 65536 | tf_op jit(solution)/shard_map/all_to_all | solution.py:1187
  16.9 5.7 %copy-start.34 = (bf16[2048,1024]{1,0:T(8,128)(2,1)S(1)}, bf16[2048,1024]{1,0:T(8,128)(2,1)}, u32[]{:S(2)}) copy-start(bf16[2048,1024]{1,0:T(8,128)(2,1)} %param.28) | copy-start | bytes 12582916
  26.0 4.0 copy-start.3
  26.0 4.0 copy-start.5
  26.0 4.3 copy-start.33
  26.0 178.8 %all-to-all-start.1 = ((bf16[32,16,1024]{2,1,0:T(8,128)(2,1)}), bf16[32,16,1024]{2,1,0:T(8,128)(2,1)S(1)}, u32[]{:S(2)}, u32[]{:S(2)}) async-start(bf16[32,16,1024]{2,1,0:T(8,128)(2,1)} %bitcast.10), calls=%async_computation.1 | async-start | bytes 2097152 | tf_op jit(solution)/shard_map/all_to_all | solution.py:1192
  31.6 163.2 %copy-start.22 = (bf16[1,256,1024]{2,1,0:T(8,128)(2,1)S(1)}, bf16[1,256,1024]{2,1,0:T(8,128)(2,1)}, u32[]{:S(2)}) copy-start(bf16[1,256,1024]{2,1,0:T(8,128)(2,1)} %param.19) | copy-start | bytes 1572868
  31.6 163.2 %copy-start.24 = (bf16[1,256,1024]{2,1,0:T(8,128)(2,1)S(1)}, bf16[1,256,1024]{2,1,0:T(8,128)(2,1)}, u32[]{:S(2)}) copy-start(bf16[1,256,1024]{2,1,0:T(8,128)(2,1)} %param.18) | copy-start | bytes 1572868
  194.7 4.4 copy-start.2
  204.8 33.4 %all-to-all-start.2 = ((bf16[32,16,1024]{2,1,0:T(8,128)(2,1)}), bf16[32,16,1024]{2,1,0:T(8,128)(2,1)}, u32[]{:S(2)}, u32[]{:S(2)}) async-start(bf16[32,16,1024]{2,1,0:T(8,128)(2,1)} %bitcast.17), calls=%async_computation.2 | async-start | bytes 2097152 | tf_op jit(solution)/shard_map/all_to_all | solution.py:1192
  208.8 3.5 copy-start.32
  212.6 9.8 %copy-start.18 = (bf16[512,1024]{1,0:T(8,128)(2,1)}, bf16[512,1024]{1,0:T(8,128)(2,1)S(1)}, u32[]{:S(2)}) copy-start(bf16[512,1024]{1,0:T(8,128)(2,1)S(1)} %multiply_convert_fusion.3) | copy-start | bytes 3145732
  240.2 5.7 %copy-start.9 = (bf16[2,512,256]{2,1,0:T(8,128)(2,1)S(1)}, bf16[2,512,256]{2,1,0:T(8,128)(2,1)}, u32[]{:S(2)}) copy-start(bf16[2,512,256]{2,1,0:T(8,128)(2,1)} %get-tuple-element.61) | copy-start | bytes 1572868
  247.3 40.4 %all-to-all-start.3 = ((bf16[32,16,1024]{2,1,0:T(8,128)(2,1)}), bf16[32,16,1024]{2,1,0:T(8,128)(2,1)}, u32[]{:S(2)}, u32[]{:S(2)}) async-start(bf16[32,16,1024]{2,1,0:T(8,128)(2,1)} %bitcast.109), calls=%async_computation.3 | async-start | bytes 2097152 | tf_op jit(solution)/shard_map/all_to_all | solution.py:1192
  259.4 3.2 copy-start.23
  259.4 3.2 copy-start.25
  259.4 3.2 copy-start.38
  287.8 8.4 %copy-start.8 = (bf16[4,2,2,2,32,1024]{5,4,3,2,1,0:T(8,128)(2,1)S(1)}, bf16[4,2,2,2,32,1024]{5,4,3,2,1,0:T(8,128)(2,1)}, u32[]{:S(2)}) copy-start(bf16[4,2,2,2,32,1024]{5,4,3,2,1,0:T(8,128)(2,1)} %get-tuple-element.64) | copy-start | bytes 6291460
  299.1 31.4 %all-to-all-start.4 = ((bf16[32,16,1024]{2,1,0:T(8,128)(2,1)}), bf16[32,16,1024]{2,1,0:T(8,128)(2,1)}, u32[]{:S(2)}, u32[]{:S(2)}) async-start(bf16[32,16,1024]{2,1,0:T(8,128)(2,1)} %bitcast.29), calls=%async_computation.4 | async-start | bytes 2097152 | tf_op jit(solution)/shard_map/all_to_all | solution.py:1192
  305.5 3.9 copy-start.21
  309.4 4.4 copy-start
  309.4 4.4 copy-start.35
  313.8 2.9 copy-start.39
  485.1 3.4 copy-start.12
  485.1 3.4 copy-start.37
  490.6 6.7 %copy-start.1 = (f32[512,1024]{1,0:T(8,128)S(1)}, f32[512,1024]{1,0:T(8,128)}, u32[]{:S(2)}) copy-start(f32[512,1024]{1,0:T(8,128)} %subtract_add_fusion) | copy-start | bytes 6291460
  494.4 16.0 %all-to-all-start.5 = ((f32[32,2,32]{2,1,0:T(2,128)}), f32[32,2,32]{2,1,0:T(2,128)S(1)}, u32[]{:S(2)}, u32[]{:S(2)}) async-start(f32[32,2,32]{2,1,0:T(2,128)} %maximum_bitcast_fusion), calls=%async_computation.5 | async-start | bytes 65536 | tf_op jit(solution)/shard_map/all_to_all | solution.py:1280
  508.1 2.8 copy-start.27
  508.1 3.6 copy-start.30
  508.1 4.2 copy-start.26
  509.5 3.6 copy-start.29
  509.5 4.2 copy-start.28
  (14 other events, 26.8 us)

commit v7 on v6

--- a/solution.py
+++ b/solution.py
@@ -9,15 +9,14 @@
 F32 = jnp.float32
 ALL = ("dp", "fsdp")
 MESH = pl.DeviceIdType.MESH
-LAG = 2
-GATHER_LAG = 2
+LAG = 3
+GATHER_LAG = 3
 REST_START = 1
 REST_DELAY = 8
 DEEP_AT = 10
 COLLECT_LAG = 2
 AHEAD = 3
 HOP_LAG = 1
-FIRST_PIECE = 1024
 PAIR = 128
 HDIM = 64
 MH = 4
@@ -690,28 +689,32 @@
 def forward_kernel(first, rest, exchange, slots, *refs):
     depth, rows, pairs = exchange.depth, exchange.rows, exchange.pairs
     n = len(rest.views)
-    ((picks_ref, normed_ref), shard, shards, outs, (qkv,), full, swap, held,
-     others) = split_refs(refs, 2, 1, n, 8, 1, n, len(exchange.scratch), len(first.scratch))
+    ((picks_ref, normed_ref), shard, shards, outs, weights, full, swap, held,
+     others) = split_refs(refs, 2, 3, n, 8, 3, n, len(exchange.scratch), len(first.scratch))
     counts_ref, q_ref, k_ref, v_ref, att_ref, lse_ref, keys, vals = outs
-    first.bind(shard, (qkv,), held)
+    first.bind(shard, weights, held)
     rest.bind(shards, full, others)
     exchange.bind((k_ref, v_ref), (keys, vals), swap)
     z = lax.axis_index("fsdp")
     blocks = picks_ref.shape[1] // 128
-    per_turn = -(-blocks // first.steps)
+    head = depth - 2 + 3 * GATHER_LAG
+    per_turn = -(-blocks // head)
     greet(first.side, depth)
     for k in range(first.count):
         first.start(k)
 
+    def both(turn):
+        first.step(turn)
+        if 0 <= turn - REST_START < rest.count:
+            rest.start(turn - REST_START)
+        if turn >= REST_DELAY:
+            rest.step(turn - REST_DELAY)
+
     def gather(i, carry):
-        for turn in range(first.steps):
+        for turn in range(head):
             @pl.when(i == turn)
             def _(turn=turn):
-                first.step(turn)
-                if 0 <= turn - REST_START < rest.count:
-                    rest.start(turn - REST_START)
-                if turn >= REST_DELAY:
-                    rest.step(turn - REST_DELAY)
+                both(turn)
 
         for inner in range(per_turn):
             block = i * per_turn + inner
@@ -722,16 +725,17 @@
 
         return carry
 
-    lax.fori_loop(0, first.steps, gather, 0)
+    lax.fori_loop(0, head, gather, 0)
+    ahead = min(AHEAD, pairs)
+    for k, out_ref in enumerate((k_ref, v_ref, q_ref)):
+        both(head + k)
+        first.put(k).wait()
+        project(normed_ref, weights[k], out_ref)
+        if k == 1:
+            for p in range(ahead):
+                exchange.offer(p)
     for k in range(max(0, first.steps - REST_START), rest.count):
         rest.start(k)
-    first.settle()
-    project(normed_ref, qkv.at[1], k_ref)
-    project(normed_ref, qkv.at[2], v_ref)
-    ahead = min(AHEAD, pairs)
-    for p in range(ahead):
-        exchange.offer(p)
-    project(normed_ref, qkv.at[0], q_ref)
     done = max(0, first.steps - REST_DELAY)
     delay = (depth - 2) * HOP_LAG + 1
     turns = pairs + delay
@@ -765,10 +769,10 @@
     rest.finish()
 
 
-def attention_forward(side, depth, picks, normed, w_qkv, shards, slots, call_id):
+def attention_forward(side, depth, picks, normed, projections, shards, slots, call_id):
     rows, width = normed.shape[0] // 2, normed.shape[1]
     pairs = width // PAIR
-    first, rest = Gather(side, depth, (w_qkv,), FIRST_PIECE), Gather(side, depth, shards)
+    first, rest = Gather(side, depth, projections), Gather(side, depth, shards)
     exchange = Exchange(depth, rows, pairs)
     any_space, vmem = pl.BlockSpec(memory_space=pl.ANY), pl.BlockSpec(memory_space=pltpu.VMEM)
     spread = jax.ShapeDtypeStruct((pairs, depth, rows, PAIR), BF)
@@ -787,12 +791,12 @@
         )
         + tuple(first.outs)
         + tuple(rest.outs),
-        in_specs=[vmem] * 2 + [any_space] * (1 + len(rest.views)),
-        out_specs=(vmem,) * 9 + (any_space,) * len(rest.views),
+        in_specs=[vmem] * 2 + [any_space] * (3 + len(rest.views)),
+        out_specs=(vmem,) * 11 + (any_space,) * len(rest.views),
         scratch_shapes=exchange.scratch + first.scratch + rest.scratch,
         compiler_params=params(call_id, 56),
     )(picks, normed, *first.views, *rest.views)
-    return results[:8], first.restore(results[8:9])[0], rest.restore(results[9:])
+    return results[:8], first.restore(results[8:11]), rest.restore(results[11:])
 
 
 class Collect:
@@ -1084,13 +1088,14 @@
     )(ids, counts, mquery, keys_full)
 
 
-def picks_back_kernel(block, ids_ref, weight_ref, table_ref, memory_ref, query_ref, keys_ref,
-                      grad_query_ref, grad_keys_ref, grad_mixing, total):
+def picks_back_kernel(block, ids_ref, weight_ref, first_ref, second_ref, memory_ref, query_ref,
+                      keys_ref, grad_query_ref, grad_keys_ref, grad_mixing, total):
     head, part = pl.program_id(0), pl.program_id(1)
 
-    @pl.when(head == 0)
-    def _():
-        grad_mixing[part] = dot_rows(table_ref[0], memory_ref[...])
+    for number, table_ref in enumerate((first_ref, second_ref)):
+        @pl.when(jnp.logical_and(head == 0, part == number))
+        def _(number=number, table_ref=table_ref):
+            grad_mixing[number] = dot_rows(table_ref[...], memory_ref[...])
 
     weight = weight_ref[0, 0]
     pulled = weight * grad_mixing[part]
@@ -1123,9 +1128,9 @@
                     total[start : start + block].astype(BF))
 
 
-def slot_weights_back(ids, weights, table, grad_memory, mquery, keys_full, block):
+def slot_weights_back(ids, weights, tables, grad_memory, mquery, keys_full, block):
     slots, rows = weights.shape[2:]
-    width = table.shape[2]
+    width = tables[0].shape[1]
     return pl.pallas_call(
         functools.partial(picks_back_kernel, block),
         grid=(MH, 2),
@@ -1136,7 +1141,8 @@
         in_specs=[
             pl.BlockSpec(ids.shape, lambda m, u: (0, 0)),
             pl.BlockSpec((1, 1, slots, rows), lambda m, u: (u, m, 0, 0)),
-            pl.BlockSpec((1, slots, width), lambda m, u: (jnp.where(m == 0, u, 1), 0, 0)),
+            pl.BlockSpec((slots, width), lambda m, u: (0, 0)),
+            pl.BlockSpec((slots, width), lambda m, u: (0, 0)),
             pl.BlockSpec((rows, width), lambda m, u: (jnp.where(m == 0, u, 1), 0)),
             pl.BlockSpec((rows, 2 * HALF), lambda m, u: (u, m)),
             pl.BlockSpec((2 * SUB, HALF), lambda m, u: (m, 0)),
@@ -1151,7 +1157,7 @@
             bytes_accessed=24 * 2**20,
             transcendentals=0,
         ),
-    )(ids, weights, table, grad_memory, mquery, keys_full)
+    )(ids, weights, *tables, grad_memory, mquery, keys_full)
 
 
 def one_hot(ids, count):
@@ -1185,14 +1191,11 @@
     side, depth = grid_of(lax.axis_size("dp"), lax.axis_size("fsdp"))
 
     asked = lax.all_to_all(request[:, 0], ALL, split_axis=1, concat_axis=1, tiled=True)
-    serve_picks = [one_hot(asked[part].reshape(-1), shard_rows) for part in range(2)]
-
     def swap(values):
         values = values.reshape(owners, capacity, width)
         swapped = lax.all_to_all(values, ALL, split_axis=0, concat_axis=0, tiled=True)
         return swapped.reshape(slots, width)
 
-    served = [mm(pick, value_rows).astype(BF) for pick in serve_picks]
     offsets = jnp.maximum(request[:, 0].reshape(2, slots), 0)
     picked = (jnp.arange(slots, dtype=jnp.int32) // capacity)[None] * shard_rows + offsets
     ids = jnp.stack([picked // SUB, picked % SUB], axis=1).reshape(4, slots)
@@ -1201,22 +1204,24 @@
     normed, inverse = normalize(x_rows, gain_attn)
     normed = normed.astype(BF)
     picks = jnp.stack([slot_prompt[0], slot_cont[0]]).transpose(3, 0, 2, 1)
-    picks, served = lax.optimization_barrier((picks.reshape(picks.shape[0], -1), served))
-    tables = [swap(served[0])]
-    results, qkv_full, full = attention_forward(
+    picks = picks.reshape(picks.shape[0], -1)
+    results, (key_full, value_full, ask_full), full = attention_forward(
         side,
         depth,
         picks,
         normed,
-        w_qkv,
+        (w_qkv[1], w_qkv[2], w_qkv[0]),
         (w_attn_out, w_mem_query, sub_keys, w_gate, w_mem_out),
         slots,
         0,
     )
     counts, queries, keys, vals, att, lse, all_keys, all_vals = results
     attn_out_full, query_full, keys_full, gate_full, mem_out_full = full
-    att, late, tables[0] = lax.optimization_barrier((att, served[1], tables[0]))
-    tables.append(swap(late))
+    att, asked = lax.optimization_barrier((att, asked))
+    serve_pick = one_hot(asked.reshape(-1), shard_rows)
+    served = mm(serve_pick, value_rows).astype(BF).reshape(2, owners, capacity, width)
+    tables = lax.all_to_all(served, ALL, split_axis=1, concat_axis=1, tiled=True)
+    tables = tables.reshape(2, slots, width)
     hidden = x_rows + mm(att, attn_out_full)
     normed2, inverse2 = normalize(hidden, gain_mem)
     normed2 = normed2.astype(BF)
@@ -1241,7 +1246,7 @@
     ]
     arrived = [None, swap(slot_grads[1])]
     grad_query, grad_keys = slot_weights_back(
-        ids, weights, jnp.stack(tables), grad_memory, mquery, keys_full, block
+        ids, weights, tables, grad_memory, mquery, keys_full, block
     )
     grad_query, arrived[1], late = lax.optimization_barrier((grad_query, arrived[1], slot_grads[0]))
     arrived[0] = swap(late)
@@ -1267,12 +1272,12 @@
         grad_att,
         normed,
         (grad_query_w, grad_keys, grad_gate_w, grad_mem_out.astype(BF), grad_attn_out),
-        qkv_full,
+        jax.ShapeDtypeStruct((3, cols, cols), BF),
         1,
     )
-    grad_rows = mm_l(jnp.concatenate(serve_picks, axis=0), jnp.concatenate(arrived, axis=0))
+    grad_rows = mm_l(serve_pick, jnp.concatenate(arrived, axis=0))
     grad_normed = (
-        mm_t(grad_q, qkv_full[0]) + mm_t(grad_k, qkv_full[1]) + mm_t(grad_v, qkv_full[2])
+        mm_t(grad_q, ask_full) + mm_t(grad_k, key_full) + mm_t(grad_v, value_full)
     )
     grad_x, gain_attn_part = norm_backward(x_rows, inverse, gain_attn, grad_normed)
     grad_x = grad_hidden + grad_x

time: 520 us -> 492 us (0.946)
  Pallas kernels: 351 us -> 326 us
  waiting for transfers between devices: 11.5 us -> 27.5 us
  matrix products: 88.8 us -> 74.8 us
  other arithmetic: 15.8 us -> 7.94 us
  local copies, waits for them, and re-layouts: 16.3 us -> 22.1 us
    pallas_call x1, Pallas kernels: 163 us -> 143 us  [attention_forward(): pl.pallas_call(functools.partial(forward_kernel, first, rest, exchange, s...]
    all_to_all x0 -> x1, waiting for transfers between devices: none -> 20.5 us  [per_device(): lax.all_to_all(served, ALL, split_axis=1, concat_axis=1, tiled=True)]
    dot_general x8 -> x7, matrix products: 34.1 us -> 24 us  [mm(): return jnp.dot(left, right, preferred_element_type=F32)]
    all_to_all x4 -> x2, starting transfers between devices: 19.7 us -> 10.8 us  [swap(): lax.all_to_all(values, ALL, split_axis=0, concat_axis=0, tiled=True)]
  transfers between devices with their start and end apart: 6 -> 5, of which waited for: 2 -> 2; matrix products, arithmetic and copies ran while one was open for 15% -> 12% of each run, Pallas kernels for 38% -> 36%
where the time goes in v7:
time: 492 us; the launch traced here: 488 us
  Pallas kernels  326 us (66%)
  matrix products  74.8 us (15%)
  waiting for transfers between devices  27.5 us (6%)
  starting transfers between devices  27.3 us (6%)
  local copies, waits for them, and re-layouts  22.1 us (4%)
  other arithmetic  7.94 us (2%)
    pallas_call x1, Pallas kernels, attention_backward(): pl.pallas_call(functools.partial(backward_kernel, early, late, collect),...  150 us
    pallas_call x1, Pallas kernels, attention_forward(): pl.pallas_call(functools.partial(forward_kernel, first, rest, exchange, s...  143 us
    dot_general x7, matrix products, mm_l(): lax.dot_general(left, right, (((0,), (0,)), ((), ())), preferred_element_...  26.3 us
    dot_general x7, matrix products, mm_t(): lax.dot_general(left, right, (((1,), (1,)), ((), ())), preferred_element_...  24.4 us
    dot_general x7, matrix products, mm(): return jnp.dot(left, right, preferred_element_type=F32)  24 us
    all_to_all x1, waiting for transfers between devices, per_device(): lax.all_to_all(served, ALL, split_axis=1, concat_axis=1, tiled=True)  20.5 us
    pallas_call x1, Pallas kernels, slot_weights_back(): pl.pallas_call(functools.partial(picks_back_kernel, block), grid=(MH, 2),...  20.1 us
    pallas_call x1, Pallas kernels, slot_weights(): pl.pallas_call(picks_kernel, grid=(2, MH), out_shape=(jax.ShapeDtypeStruc...  13.4 us
  transfers between devices with their start and end apart: 5, of which 2 were waited for; matrix products, arithmetic and copies ran while one was open for 12% of the time, Pallas kernels for 36%

profile of v7, /device:TPU:0, one launch (start us, length us, event | category | flops | bytes accessed | tf_op | source)
XLA Modules:
  0.0 487.6 jit_solution(11672226207279861885)
XLA Ops:
  2.1 7.3 %all-to-all-start = ((s32[2,32,16]{2,0,1:T(2,128)}), s32[2,32,16]{2,0,1:T(2,128)S(1)}, u32[]{:S(2)}, u32[]{:S(2)}) async-start(s32[2,32,16]{2,0,1:T(2,128)} %bitcast.11), calls=%async_computation | async-start | bytes 65536 | tf_op jit(solution)/shard_map/all_to_all | solution.py:1193
  9.4 1.6 fusion.4
  11.0 2.6 fusion.40
  15.9 142.5 %shard_map.255 = (bf16[2,4,512,256]{3,2,1,0:T(8,128)(2,1)}, bf16[512,1024]{1,0:T(8,128)(2,1)}, bf16[512,1024]{1,0:T(8,128)(2,1)}, bf16[512,1024]{1,0:T(8,128)(2,...) custom-call(s32[32,2048]{1,0:T(8,128)} %reshape.290.refs_0_, ...), custom_call_target="tpu_custom_call" | custom-call | tf_op jit(solution)/shard_map/pallas_call | solution.py:780
  158.5 7.1 %fusion.16 = bf16[1024,1024]{1,0:T(8,128)(2,1)S(1)} fusion(bf16[2048,1024]{1,0:T(8,128)(2,1)} %param.28, s32[1024]{0:T(1024)S(1)} %eq.17), kind=kOutput, calls=%fused_computation.37 | convolution fusion | flops 4298113024 | bytes 6295552 | tf_op jit(solution)/shard_map/dot_general | solution.py:29
  165.6 1.6 copy.41
  167.2 4.1 all-to-all-start.1
  172.2 4.4 fusion.21
  178.8 6.1 %convolution_convert_fusion.1.query_ref = bf16[512,4096]{1,0:T(8,128)(2,1)} fusion(bf16[512,1024]{1,0:T(8,128)(2,1)S(1)} %multiply_convert_fusion.3, bf16[1024,4096]{1,0:T(8,128)(2,1)S(1)} %bitcast.137), kind=kOutput, calls=%fused_computation.4 | convolution fusion | flops 4297064448 | bytes 13631488 | tf_op jit(solution)/shard_map/dot_general | solution.py:29
  184.9 13.4 %shard_map.256 = (f32[2,4,512,256]{3,2,1,0:T(8,128)}, bf16[2,512,256]{2,1,0:T(8,128)(2,1)}) custom-call(s32[4,512]{1,0:T(4,128)} %reshape.297.ids_ref, bf16[2,4,512,256]{3,2,1,0:T(8,128)(2,1)} %get-tuple-element.53.counts_ref, bf16[512,4096]{1,0:T(8,128)(2,1)} %convolution_convert_fusion.1.query_ref, bf16[2048,512]{1,0:T(8,128)(2,1)} %bitcast.143), custom_call_target="tpu_custom_call" | custom-call | flops 4294967296 | bytes 25165824 | tf_op jit(solution)/shard_map/pallas_call | solution.py:1065
  198.3 20.5 %all-to-all-done.1 = bf16[2,32,16,1024]{3,2,0,1:T(8,128)(2,1)} async-done(((bf16[2,32,16,1024]{3,2,0,1:T(8,128)(2,1)}), bf16[2,32,16,1024]{3,2,0,1:T(8,128)(2,1)}, u32[]{:S(2)}, u32[]{:S(2)}) %all-to-all-start.1) | async-done | bytes 2097184 | tf_op jit(solution)/shard_map/all_to_all | solution.py:1223
  218.8 1.9 fusion.39
  223.4 3.5 multiply_convert_fusion
  229.3 4.5 all-to-all-start.2
  233.8 3.2 add_convert_fusion
  240.0 2.7 convolution_convert_fusion.3
  242.7 2.6 convolution_convert_fusion.4
  245.3 20.1 %shard_map.257 = (bf16[512,4096]{1,0:T(8,128)(2,1)}, bf16[1024,1024]{1,0:T(8,128)(2,1)}) custom-call(s32[4,512]{1,0:T(4,128)} %reshape.297.ids_ref, f32[2,4,512,256]{3,2,1,0:T(8,128)} %get-tuple-element.60.weight_ref, bf16[512,1024]{1,0:T(8,128)(2,1)} %bitcast.108, bf16[512,1024]{1,0:T(8,128)(2,1)} %bitcast.110, bf16[512,1024]{1,0:T(8,128)(2,1)} %copy-done.13, ...), custom_call_target="tpu_custom_call" | custom-call | flops 6442450944 | bytes 25165824 | tf_op jit(solution)/shard_map/pallas_call | solution.py:1134
  265.5 8.4 %fusion.41 = f32[512,1024]{1,0:T(8,128)S(1)} fusion(bf16[512,4096]{1,0:T(8,128)(2,1)} %get-tuple-element.62, bf16[1024,4096]{1,0:T(8,128)(2,1)} %bitcast.134), kind=kOutput, calls=%fused_computation.98 | convolution fusion | flops 4294967296 | bytes 14680064 | tf_op jit(solution)/shard_map/dot_general | solution.py:33
  273.9 2.9 multiply_reduce_fusion
  276.8 6.3 %all-to-all-start.3 = ((bf16[32,16,1024]{2,1,0:T(8,128)(2,1)}), bf16[32,16,1024]{2,1,0:T(8,128)(2,1)}, u32[]{:S(2)}, u32[]{:S(2)}) async-start(bf16[32,16,1024]{2,1,0:T(8,128)(2,1)} %bitcast.105), calls=%async_computation.3 | async-start | bytes 2097152 | tf_op jit(solution)/shard_map/all_to_all | solution.py:1196
  283.1 3.5 subtract_add_fusion
  286.8 4.7 convolution_convert_fusion.2
  291.4 2.3 convolution_convert_fusion.5.refs_7_
  294.3 6.8 %convolution_convert_fusion = bf16[1024,4096]{1,0:T(8,128)(2,1)} fusion(bf16[512,1024]{1,0:T(8,128)(2,1)S(1)} %copy-done.18, bf16[512,4096]{1,0:T(8,128)(2,1)S(1)} %copy-done.44), kind=kOutput, calls=%fused_computation.3 | convolution fusion | flops 4299161600 | bytes 13631488 | tf_op jit(solution)/shard_map/dot_general | solution.py:37
  301.1 7.0 %all-to-all-done.3 = bf16[32,16,1024]{2,1,0:T(8,128)(2,1)} async-done(((bf16[32,16,1024]{2,1,0:T(8,128)(2,1)}), bf16[32,16,1024]{2,1,0:T(8,128)(2,1)}, u32[]{:S(2)}, u32[]{:S(2)}) %all-to-all-start.3) | async-done | bytes 1048608 | tf_op jit(solution)/shard_map/all_to_all | solution.py:1196
  308.1 150.1 %shard_map.258 = (bf16[512,1024]{1,0:T(8,128)(2,1)}, bf16[512,1024]{1,0:T(8,128)(2,1)}, bf16[512,1024]{1,0:T(8,128)(2,1)}, f32[32,4096]{1,0:T(8,128)}, f32[32,10...) custom-call(bf16[512,1024]{1,0:T(8,128)(2,1)} %get-tuple-element.63.ref, ...), custom_call_target="tpu_custom_call" | custom-call | tf_op jit(solution)/shard_map/pallas_call | solution.py:985
  458.3 3.3 fusion.42
  463.7 1.8 fusion.12
  466.3 5.1 %all-to-all-start.4 = ((f32[32,2,32]{2,1,0:T(2,128)}), f32[32,2,32]{2,1,0:T(2,128)S(1)}, u32[]{:S(2)}, u32[]{:S(2)}) async-start(f32[32,2,32]{2,1,0:T(2,128)} %maximum_bitcast_fusion), calls=%async_computation.4 | async-start | bytes 65536 | tf_op jit(solution)/shard_map/all_to_all | solution.py:1285
  471.4 8.7 %fusion = f32[2048,1024]{1,0:T(8,128)} fusion(s32[1024]{0:T(1024)S(1)} %eq.17, bf16[512,1024]{1,0:T(8,128)(2,1)} %bitcast.27, bf16[512,1024]{1,0:T(8,128)(2,1)} %bitcast.29), kind=kOutput, calls=%fused_computation.1 | convolution fusion | flops 4301258752 | bytes 10489856 | tf_op jit(solution)/shard_map/dot_general | solution.py:37
  480.6 1.6 slice_bitcast_fusion
  (138 shorter events, 23.8 us)
Async XLA Ops:
  2.1 156.4 %all-to-all-start = ((s32[2,32,16]{2,0,1:T(2,128)}), s32[2,32,16]{2,0,1:T(2,128)S(1)}, u32[]{:S(2)}, u32[]{:S(2)}) async-start(s32[2,32,16]{2,0,1:T(2,128)} %bitcast.11), calls=%async_computation | async-start | bytes 65536 | tf_op jit(solution)/shard_map/all_to_all | solution.py:1193
  9.4 4.2 copy-start.2
  9.4 4.2 copy-start.3
  9.4 4.2 copy-start.35
  11.0 3.9 copy-start.31
  11.0 3.9 copy-start.32
  167.2 4.2 copy-start.33
  167.2 5.0 %copy-start.20 = (bf16[1,256,1024]{2,1,0:T(8,128)(2,1)S(1)}, bf16[1,256,1024]{2,1,0:T(8,128)(2,1)}, u32[]{:S(2)}) copy-start(bf16[1,256,1024]{2,1,0:T(8,128)(2,1)} %param.19) | copy-start | bytes 1572868
  167.2 5.0 %copy-start.23 = (bf16[1,256,1024]{2,1,0:T(8,128)(2,1)S(1)}, bf16[1,256,1024]{2,1,0:T(8,128)(2,1)}, u32[]{:S(2)}) copy-start(bf16[1,256,1024]{2,1,0:T(8,128)(2,1)} %param.18) | copy-start | bytes 1572868
  167.2 51.6 %all-to-all-start.1 = ((bf16[2,32,16,1024]{3,2,0,1:T(8,128)(2,1)}), bf16[2,32,16,1024]{3,2,0,1:T(8,128)(2,1)}, u32[]{:S(2)}, u32[]{:S(2)}) async-start(bf16[2,32,16,1024]{3,2,0,1:T(8,128)(2,1)} %copy.41), calls=%async_computation.1 | async-start | bytes 4194304 | tf_op jit(solution)/shard_map/all_to_all | solution.py:1223
  172.2 4.4 copy-start.4
  172.2 4.4 copy-start.19
  172.2 4.4 copy-start.38
  172.2 6.1 %slice-start = ((s8[8388608]{0:T(1024)(128)(4,1)}), s8[4194304]{0:T(1024)(128)(4,1)S(1)}, s32[]{:S(2)}) async-start(s8[8388608]{0:T(1024)(128)(4,1)} %bitcast.135), calls=%async_computation.5 | async-start | bytes 8388608
  178.3 6.6 %copy-start.15 = (bf16[512,1024]{1,0:T(8,128)(2,1)}, bf16[512,1024]{1,0:T(8,128)(2,1)S(1)}, u32[]{:S(2)}) copy-start(bf16[512,1024]{1,0:T(8,128)(2,1)S(1)} %multiply_convert_fusion.3) | copy-start | bytes 3145732
  198.3 22.4 %copy-start.10 = (bf16[2,512,256]{2,1,0:T(8,128)(2,1)S(1)}, bf16[2,512,256]{2,1,0:T(8,128)(2,1)}, u32[]{:S(2)}) copy-start(bf16[2,512,256]{2,1,0:T(8,128)(2,1)} %get-tuple-element.56) | copy-start | bytes 1572868
  218.8 3.2 copy-start.43
  229.3 36.1 %all-to-all-start.2 = ((bf16[32,16,1024]{2,1,0:T(8,128)(2,1)}), bf16[32,16,1024]{2,1,0:T(8,128)(2,1)}, u32[]{:S(2)}, u32[]{:S(2)}) async-start(bf16[32,16,1024]{2,1,0:T(8,128)(2,1)} %bitcast.106), calls=%async_computation.2 | async-start | bytes 2097152 | tf_op jit(solution)/shard_map/all_to_all | solution.py:1196
  265.4 8.4 %copy-start.9 = (bf16[4,2,2,2,32,1024]{5,4,3,2,1,0:T(8,128)(2,1)S(1)}, bf16[4,2,2,2,32,1024]{5,4,3,2,1,0:T(8,128)(2,1)}, u32[]{:S(2)}) copy-start(bf16[4,2,2,2,32,1024]{5,4,3,2,1,0:T(8,128)(2,1)} %get-tuple-element.58) | copy-start | bytes 6291460
  265.5 8.4 %copy-start.12 = (bf16[512,1024]{1,0:T(8,128)(2,1)S(1)}, bf16[512,1024]{1,0:T(8,128)(2,1)}, u32[]{:S(2)}) copy-start(bf16[512,1024]{1,0:T(8,128)(2,1)} %get-tuple-element.91) | copy-start | bytes 3145732
  276.8 6.3 %copy-start.22 = (bf16[1,256,1024]{2,1,0:T(8,128)(2,1)S(1)}, bf16[1,256,1024]{2,1,0:T(8,128)(2,1)}, u32[]{:S(2)}) copy-start(bf16[1,256,1024]{2,1,0:T(8,128)(2,1)} %param.19) | copy-start | bytes 1572868
  276.8 31.3 %all-to-all-start.3 = ((bf16[32,16,1024]{2,1,0:T(8,128)(2,1)}), bf16[32,16,1024]{2,1,0:T(8,128)(2,1)}, u32[]{:S(2)}, u32[]{:S(2)}) async-start(bf16[32,16,1024]{2,1,0:T(8,128)(2,1)} %bitcast.105), calls=%async_computation.3 | async-start | bytes 2097152 | tf_op jit(solution)/shard_map/all_to_all | solution.py:1196
  286.7 4.7 copy-start
  286.8 4.7 copy-start.39
  458.3 3.4 copy-start.37
  458.3 3.4 copy-start.41
  466.3 16.8 %all-to-all-start.4 = ((f32[32,2,32]{2,1,0:T(2,128)}), f32[32,2,32]{2,1,0:T(2,128)S(1)}, u32[]{:S(2)}, u32[]{:S(2)}) async-start(f32[32,2,32]{2,1,0:T(2,128)} %maximum_bitcast_fusion), calls=%async_computation.4 | async-start | bytes 65536 | tf_op jit(solution)/shard_map/all_to_all | solution.py:1285
  471.4 8.7 %copy-start.1 = (f32[512,1024]{1,0:T(8,128)S(1)}, f32[512,1024]{1,0:T(8,128)}, u32[]{:S(2)}) copy-start(f32[512,1024]{1,0:T(8,128)} %subtract_add_fusion) | copy-start | bytes 6291460
  480.6 3.7 copy-start.29
  480.6 4.4 copy-start.25
  482.2 3.6 copy-start.28
  482.2 4.2 copy-start.27
  (20 other events, 42.9 us)

commit v8 on v7

--- a/solution.py
+++ b/solution.py
@@ -9,10 +9,10 @@
 F32 = jnp.float32
 ALL = ("dp", "fsdp")
 MESH = pl.DeviceIdType.MESH
-LAG = 3
+LAG = 4
 GATHER_LAG = 3
 REST_START = 1
-REST_DELAY = 8
+REST_DELAY = 6
 DEEP_AT = 10
 COLLECT_LAG = 2
 AHEAD = 3
@@ -1033,53 +1033,56 @@
 
 
 def picks_kernel(ids_ref, counts_ref, query_ref, keys_ref, weight_ref, mixing_ref, total):
-    part, head = pl.program_id(0), pl.program_id(1)
-    scores = None
-    for half in range(2):
-        pick = selector(ids_ref, 2 * part + half, SUB)
-        slot_keys = dot_first(pick, keys_ref[half * SUB : (half + 1) * SUB]).astype(BF)
-        piece = dot_rows(slot_keys, query_ref[:, half * HALF : (half + 1) * HALF])
-        scores = piece if scores is None else scores + piece
-    count = counts_ref[0, 0].astype(F32)
-    named = count > 0.0
-    top = jnp.max(jnp.where(named, scores, -jnp.inf), axis=0, keepdims=True)
-    raised = jnp.where(named, count * jnp.exp(scores - top), 0.0)
-    weight = raised / jnp.sum(raised, axis=0, keepdims=True)
-    weight_ref[0, 0] = weight
-
-    @pl.when(head == 0)
-    def _():
-        total[...] = weight
-
-    @pl.when(head > 0)
-    def _():
-        total[...] = total[...] + weight
+    head = pl.program_id(0)
+    rows = counts_ref.shape[3]
+    for part in range(2):
+        scores = None
+        for half in range(2):
+            pick = selector(ids_ref, 2 * part + half, SUB)
+            slot_keys = dot_first(pick, keys_ref[half * SUB : (half + 1) * SUB]).astype(BF)
+            query = query_ref[part * rows : (part + 1) * rows, half * HALF : (half + 1) * HALF]
+            piece = dot_rows(slot_keys, query)
+            scores = piece if scores is None else scores + piece
+        count = counts_ref[part, 0].astype(F32)
+        named = count > 0.0
+        top = jnp.max(jnp.where(named, scores, -jnp.inf), axis=0, keepdims=True)
+        raised = jnp.where(named, count * jnp.exp(scores - top), 0.0)
+        weight = raised / jnp.sum(raised, axis=0, keepdims=True)
+        weight_ref[part, 0] = weight
+
+        @pl.when(head == 0)
+        def _(part=part, weight=weight):
+            total[part] = weight
+
+        @pl.when(head > 0)
+        def _(part=part, weight=weight):
+            total[part] = total[part] + weight
 
     @pl.when(head == MH - 1)
     def _():
-        mixing_ref[0] = total[...].astype(BF)
+        mixing_ref[...] = total[...].astype(BF)
 
 
 def slot_weights(ids, counts, mquery, keys_full):
     slots, rows = counts.shape[2:]
     return pl.pallas_call(
         picks_kernel,
-        grid=(2, MH),
+        grid=(MH,),
         out_shape=(
             jax.ShapeDtypeStruct(counts.shape, F32),
             jax.ShapeDtypeStruct((2, slots, rows), BF),
         ),
         in_specs=[
-            pl.BlockSpec(ids.shape, lambda u, m: (0, 0)),
-            pl.BlockSpec((1, 1, slots, rows), lambda u, m: (u, m, 0, 0)),
-            pl.BlockSpec((rows, 2 * HALF), lambda u, m: (u, m)),
-            pl.BlockSpec((2 * SUB, HALF), lambda u, m: (m, 0)),
+            pl.BlockSpec(ids.shape, lambda m: (0, 0)),
+            pl.BlockSpec((2, 1, slots, rows), lambda m: (0, m, 0, 0)),
+            pl.BlockSpec((2 * rows, 2 * HALF), lambda m: (0, m)),
+            pl.BlockSpec((2 * SUB, HALF), lambda m: (m, 0)),
         ],
         out_specs=(
-            pl.BlockSpec((1, 1, slots, rows), lambda u, m: (u, m, 0, 0)),
-            pl.BlockSpec((1, slots, rows), lambda u, m: (u, 0, 0)),
+            pl.BlockSpec((2, 1, slots, rows), lambda m: (0, m, 0, 0)),
+            pl.BlockSpec((2, slots, rows), lambda m: (0, 0, 0)),
         ),
-        scratch_shapes=[pltpu.VMEM((slots, rows), F32)],
+        scratch_shapes=[pltpu.VMEM((2, slots, rows), F32)],
         cost_estimate=pl.CostEstimate(
             flops=2 * 2 * MH * slots * 2 * HALF * (SUB + rows),
             bytes_accessed=24 * 2**20,
@@ -1088,76 +1091,73 @@
     )(ids, counts, mquery, keys_full)
 
 
-def picks_back_kernel(block, ids_ref, weight_ref, first_ref, second_ref, memory_ref, query_ref,
-                      keys_ref, grad_query_ref, grad_keys_ref, grad_mixing, total):
-    head, part = pl.program_id(0), pl.program_id(1)
-
-    for number, table_ref in enumerate((first_ref, second_ref)):
-        @pl.when(jnp.logical_and(head == 0, part == number))
-        def _(number=number, table_ref=table_ref):
-            grad_mixing[number] = dot_rows(table_ref[...], memory_ref[...])
-
-    weight = weight_ref[0, 0]
-    pulled = weight * grad_mixing[part]
-    grad = pulled - weight * jnp.sum(pulled, axis=0, keepdims=True)
-    high = grad.astype(BF)
-    low = (grad - high.astype(F32)).astype(BF)
+def picks_back_kernel(block, ids_ref, weight_ref, table_ref, memory_ref, query_ref, keys_ref,
+                      grad_query_ref, grad_keys_ref, grad_mixing):
+    head = pl.program_id(0)
+    rows = weight_ref.shape[3]
+
+    @pl.when(head == 0)
+    def _():
+        for part in range(2):
+            grad_mixing[part] = dot_rows(
+                table_ref[part], memory_ref[part * rows : (part + 1) * rows]
+            )
+
+    splits = []
+    for part in range(2):
+        weight = weight_ref[part, 0]
+        pulled = weight * grad_mixing[part]
+        grad = pulled - weight * jnp.sum(pulled, axis=0, keepdims=True)
+        high = grad.astype(BF)
+        splits.append((high, (grad - high.astype(F32)).astype(BF)))
     for half in range(2):
-        pick = selector(ids_ref, 2 * part + half, SUB)
-        sub = (dot_plain(pick, high) + dot_plain(pick, low)).astype(BF)
         span = slice(half * HALF, (half + 1) * HALF)
         keys = keys_ref[half * SUB : (half + 1) * SUB]
+        subs = []
+        for part, (high, low) in enumerate(splits):
+            pick = selector(ids_ref, 2 * part + half, SUB)
+            subs.append((dot_plain(pick, high) + dot_plain(pick, low)).astype(BF))
+        sub = jnp.concatenate(subs, axis=1)
         grad_query_ref[:, span] = dot_first(sub, keys).astype(BF)
-        piece = dot_plain(sub, query_ref[:, span])
-        rows = slice(half * SUB, (half + 1) * SUB)
-
-        @pl.when(part == 0)
-        def _(piece=piece, rows=rows):
-            total[rows] = piece
-
-        @pl.when(part == 1)
-        def _(piece=piece, rows=rows):
-            total[rows] = total[rows] + piece
-
-    @pl.when(part == 1)
-    def _():
-        for shard in range(SUB // block):
+        total = dot_plain(sub, query_ref[:, span]).astype(BF)
+        for shard in range(SUB // (2 * block)):
             for side in range(2):
                 start = (2 * shard + side) * block
-                grad_keys_ref[shard * block : (shard + 1) * block, side * HALF : (side + 1) * HALF] = (
-                    total[start : start + block].astype(BF))
+                row = half * (SUB // 2) + shard * block
+                grad_keys_ref[row : row + block, side * HALF : (side + 1) * HALF] = total[
+                    start : start + block
+                ]
 
 
 def slot_weights_back(ids, weights, tables, grad_memory, mquery, keys_full, block):
     slots, rows = weights.shape[2:]
-    width = tables[0].shape[1]
+    width = tables.shape[2]
     return pl.pallas_call(
         functools.partial(picks_back_kernel, block),
-        grid=(MH, 2),
+        grid=(MH,),
         out_shape=(
             jax.ShapeDtypeStruct(mquery.shape, BF),
             jax.ShapeDtypeStruct((MH * SUB, 2 * HALF), BF),
         ),
         in_specs=[
-            pl.BlockSpec(ids.shape, lambda m, u: (0, 0)),
-            pl.BlockSpec((1, 1, slots, rows), lambda m, u: (u, m, 0, 0)),
-            pl.BlockSpec((slots, width), lambda m, u: (0, 0)),
-            pl.BlockSpec((slots, width), lambda m, u: (0, 0)),
-            pl.BlockSpec((rows, width), lambda m, u: (jnp.where(m == 0, u, 1), 0)),
-            pl.BlockSpec((rows, 2 * HALF), lambda m, u: (u, m)),
-            pl.BlockSpec((2 * SUB, HALF), lambda m, u: (m, 0)),
+            pl.BlockSpec(ids.shape, lambda m: (0, 0)),
+            pl.BlockSpec((2, 1, slots, rows), lambda m: (0, m, 0, 0)),
+            pl.BlockSpec((2, slots, width), lambda m: (0, 0, 0)),
+            pl.BlockSpec((2 * rows, width), lambda m: (0, 0)),
+            pl.BlockSpec((2 * rows, 2 * HALF), lambda m: (0, m)),
+            pl.BlockSpec((2 * SUB, HALF), lambda m: (m, 0)),
         ],
         out_specs=(
-            pl.BlockSpec((rows, 2 * HALF), lambda m, u: (u, m)),
-            pl.BlockSpec((SUB, 2 * HALF), lambda m, u: (m, 0)),
+            pl.BlockSpec((2 * rows, 2 * HALF), lambda m: (0, m)),
+            pl.BlockSpec((SUB, 2 * HALF), lambda m: (m, 0)),
         ),
-        scratch_shapes=[pltpu.VMEM((2, slots, rows), F32), pltpu.VMEM((2 * SUB, HALF), F32)],
+        scratch_shapes=[pltpu.VMEM((2, slots, rows), F32)],
         cost_estimate=pl.CostEstimate(
             flops=2 * 2 * MH * slots * rows * (4 * SUB + 4 * HALF),
             bytes_accessed=24 * 2**20,
             transcendentals=0,
         ),
-    )(ids, weights, *tables, grad_memory, mquery, keys_full)
+    )(ids, weights, tables, grad_memory, mquery, keys_full)
 
 
 def one_hot(ids, count):
@@ -1229,7 +1229,9 @@
     mquery = mm(normed2, query_full).astype(BF)
     gate_pre = mm(normed2, gate_full)
     weights, mixing = slot_weights(ids, counts, mquery, keys_full)
-    memory_out = jnp.concatenate([mm_l(mixing[part], tables[part]) for part in range(2)], axis=0)
+    memory_out = lax.dot_general(
+        mixing, tables, (((1,), (1,)), ((0,), (0,))), preferred_element_type=F32
+    ).reshape(2 * rows, width)
     sigmoid_gate = jax.nn.sigmoid(gate_pre)
     blended = (memory_out * (gate_pre * sigmoid_gate)).astype(BF)
     out = (hidden + mm(blended, mem_out_full)).astype(BF)
@@ -1240,10 +1242,12 @@
     grad_gate = (
         grad_blend * memory_out * sigmoid_gate * (1.0 + gate_pre * (1.0 - sigmoid_gate))
     ).astype(BF)
-    slot_grads = [
-        mm(mixing[part], grad_memory[part * rows : (part + 1) * rows]).astype(BF)
-        for part in range(2)
-    ]
+    slot_grads = lax.dot_general(
+        mixing,
+        grad_memory.reshape(2, rows, width),
+        (((2,), (1,)), ((0,), (0,))),
+        preferred_element_type=F32,
+    ).astype(BF)
     arrived = [None, swap(slot_grads[1])]
     grad_query, grad_keys = slot_weights_back(
         ids, weights, tables, grad_memory, mquery, keys_full, block

time: 492 us -> 481 us (0.978)
  Pallas kernels: 326 us -> 316 us
    pallas_call x2, Pallas kernels: 33.5 us -> 25.9 us  [the longest x1 13.5 us: slot_weights(): pl.pallas_call(picks_kernel, grid=(MH,), out_shape=(jax.ShapeDtypeStruct(...]
    dot_general x7 -> x5, matrix products: 24 us -> 22.4 us  [mm(): return jnp.dot(left, right, preferred_element_type=F32)]
    dot_general x7 -> x5, matrix products: 26.3 us -> 25.4 us  [mm_l(): lax.dot_general(left, right, (((0,), (0,)), ((), ())), preferred_element_...]
    unnamed x100 -> x90, local copies, waits for them, and re-layouts: 10.1 us -> 10.9 us
  transfers between devices with their start and end apart: 5 -> 5, of which waited for: 2 -> 3; matrix products, arithmetic and copies ran while one was open for 12% -> 12% of each run, Pallas kernels for 36% -> 35%
where the time goes in v8:
time: 481 us; the launch traced here: 476 us
  Pallas kernels  316 us (66%)
  matrix products  73.8 us (15%)
  waiting for transfers between devices  28 us (6%)
  starting transfers between devices  24.9 us (5%)
  local copies, waits for them, and re-layouts  24.5 us (5%)
  other arithmetic  8.12 us (2%)
    pallas_call x1, Pallas kernels, attention_backward(): pl.pallas_call(functools.partial(backward_kernel, early, late, collect),...  151 us
    pallas_call x1, Pallas kernels, attention_forward(): pl.pallas_call(functools.partial(forward_kernel, first, rest, exchange, s...  139 us
    dot_general x5, matrix products, mm_l(): lax.dot_general(left, right, (((0,), (0,)), ((), ())), preferred_element_...  25.4 us
    dot_general x7, matrix products, mm_t(): lax.dot_general(left, right, (((1,), (1,)), ((), ())), preferred_element_...  24.5 us
    dot_general x5, matrix products, mm(): return jnp.dot(left, right, preferred_element_type=F32)  22.4 us
    all_to_all x1, waiting for transfers between devices, per_device(): lax.all_to_all(served, ALL, split_axis=1, concat_axis=1, tiled=True)  18.9 us
    pallas_call x1, Pallas kernels, slot_weights(): pl.pallas_call(picks_kernel, grid=(MH,), out_shape=(jax.ShapeDtypeStruct(...  13.5 us
    pallas_call x1, Pallas kernels, slot_weights_back(): pl.pallas_call(functools.partial(picks_back_kernel, block), grid=(MH,), o...  12.4 us
  transfers between devices with their start and end apart: 5, of which 3 were waited for; matrix products, arithmetic and copies ran while one was open for 12% of the time, Pallas kernels for 35%

profile of v8, /device:TPU:0, one launch (start us, length us, event | category | flops | bytes accessed | tf_op | source)
XLA Modules:
  0.0 476.3 jit_solution(15883204492548040535)
XLA Ops:
  2.1 7.3 %all-to-all-start = ((s32[2,32,16]{2,0,1:T(2,128)}), s32[2,32,16]{2,0,1:T(2,128)S(1)}, u32[]{:S(2)}, u32[]{:S(2)}) async-start(s32[2,32,16]{2,0,1:T(2,128)} %bitcast.11), calls=%async_computation | async-start | bytes 65536 | tf_op jit(solution)/shard_map/all_to_all | solution.py:1193
  11.0 2.6 fusion.31
  15.9 139.0 %shard_map.255 = (bf16[2,4,512,256]{3,2,1,0:T(8,128)(2,1)}, bf16[512,1024]{1,0:T(8,128)(2,1)}, bf16[512,1024]{1,0:T(8,128)(2,1)}, bf16[512,1024]{1,0:T(8,128)(2,...) custom-call(s32[32,2048]{1,0:T(8,128)} %reshape.291.refs_0_, ...), custom_call_target="tpu_custom_call" | custom-call | tf_op jit(solution)/shard_map/pallas_call | solution.py:780
  155.0 7.1 %fusion.20 = bf16[1024,1024]{1,0:T(8,128)(2,1)S(1)} fusion(bf16[2048,1024]{1,0:T(8,128)(2,1)} %param.28, s32[1024]{0:T(1024)S(1)} %eq.17), kind=kOutput, calls=%fused_computation.41 | convolution fusion | flops 4298113024 | bytes 6295552 | tf_op jit(solution)/shard_map/dot_general | solution.py:29
  163.7 3.8 all-to-all-start.1
  168.4 3.5 multiply_reduce_fusion.2
  172.2 1.7 copy-done.6
  173.9 2.6 fusion.33
  176.5 6.1 %convolution_convert_fusion.1.query_ref = bf16[512,4096]{1,0:T(8,128)(2,1)} fusion(bf16[512,1024]{1,0:T(8,128)(2,1)S(1)} %multiply_convert_fusion.1, bf16[1024,4096]{1,0:T(8,128)(2,1)S(1)} %bitcast.141), kind=kOutput, calls=%fused_computation.4 | convolution fusion | flops 4297064448 | bytes 13631488 | tf_op jit(solution)/shard_map/dot_general | solution.py:29
  182.6 13.5 %shard_map.256 = (f32[2,4,512,256]{3,2,1,0:T(8,128)}, bf16[2,512,256]{2,1,0:T(8,128)(2,1)}) custom-call(s32[4,512]{1,0:T(4,128)} %reshape.298.ids_ref, bf16[2,4,512,256]{3,2,1,0:T(8,128)(2,1)} %get-tuple-element.53.counts_ref, bf16[512,4096]{1,0:T(8,128)(2,1)} %convolution_convert_fusion.1.query_ref, bf16[2048,512]{1,0:T(8,128)(2,1)} %bitcast.147), custom_call_target="tpu_custom_call" | custom-call | flops 4294967296 | bytes 25165824 | tf_op jit(solution)/shard_map/pallas_call | solution.py:1068
  196.1 18.9 %all-to-all-done.1 = bf16[2,32,16,1024]{3,2,0,1:T(8,128)(2,1)} async-done(((bf16[2,32,16,1024]{3,2,0,1:T(8,128)(2,1)}), bf16[2,32,16,1024]{3,2,0,1:T(8,128)(2,1)}, u32[]{:S(2)}, u32[]{:S(2)}) %all-to-all-start.1) | async-done | bytes 2097184 | tf_op jit(solution)/shard_map/all_to_all | solution.py:1223
  215.0 1.9 copy.44
  219.7 3.3 fusion.19
  225.3 4.5 all-to-all-start.2
  229.8 3.2 add_convert_fusion
  234.9 2.7 convolution_convert_fusion.4
  237.6 2.6 convolution_convert_fusion.5
  240.2 12.4 %shard_map.257 = (bf16[512,4096]{1,0:T(8,128)(2,1)}, bf16[1024,1024]{1,0:T(8,128)(2,1)}) custom-call(s32[4,512]{1,0:T(4,128)} %reshape.298.ids_ref, f32[2,4,512,256]{3,2,1,0:T(8,128)} %get-tuple-element.60.weight_ref, bf16[2,512,1024]{2,1,0:T(8,128)(2,1)} %bitcast.100, bf16[512,1024]{1,0:T(8,128)(2,1)} %copy-done.12, ...), custom_call_target="tpu_custom_call" | custom-call | flops 6442450944 | bytes 25165824 | tf_op jit(solution)/shard_map/pallas_call | solution.py:1135
  252.5 2.3 all-to-all-done.2
  254.8 8.4 %fusion.34 = f32[512,1024]{1,0:T(8,128)S(1)} fusion(bf16[512,4096]{1,0:T(8,128)(2,1)} %get-tuple-element.62, bf16[1024,4096]{1,0:T(8,128)(2,1)} %bitcast.138), kind=kOutput, calls=%fused_computation.90 | convolution fusion | flops 4294967296 | bytes 14680064 | tf_op jit(solution)/shard_map/dot_general | solution.py:33
  263.2 2.9 multiply_reduce_fusion
  266.1 4.6 all-to-all-start.3
  270.7 3.7 subtract_add_fusion
  274.6 4.7 convolution_convert_fusion.3
  279.2 2.3 convolution_convert_fusion.6.refs_7_
  282.1 6.8 %convolution_convert_fusion = bf16[1024,4096]{1,0:T(8,128)(2,1)} fusion(bf16[512,1024]{1,0:T(8,128)(2,1)S(1)} %copy-done.15, bf16[512,4096]{1,0:T(8,128)(2,1)S(1)} %copy-done.39), kind=kOutput, calls=%fused_computation.3 | convolution fusion | flops 4299161600 | bytes 13631488 | tf_op jit(solution)/shard_map/dot_general | solution.py:37
  288.9 6.9 %all-to-all-done.3 = bf16[32,16,1024]{2,1,0:T(8,128)(2,1)} async-done(((bf16[32,16,1024]{2,1,0:T(8,128)(2,1)}), bf16[32,16,1024]{2,1,0:T(8,128)(2,1)}, u32[]{:S(2)}, u32[]{:S(2)}) %all-to-all-start.3) | async-done | bytes 1048608 | tf_op jit(solution)/shard_map/all_to_all | solution.py:1196
  295.8 150.7 %shard_map.258 = (bf16[512,1024]{1,0:T(8,128)(2,1)}, bf16[512,1024]{1,0:T(8,128)(2,1)}, bf16[512,1024]{1,0:T(8,128)(2,1)}, f32[32,4096]{1,0:T(8,128)}, f32[32,10...) custom-call(bf16[512,1024]{1,0:T(8,128)(2,1)} %get-tuple-element.63.ref, ...), custom_call_target="tpu_custom_call" | custom-call | tf_op jit(solution)/shard_map/pallas_call | solution.py:985
  446.5 3.3 fusion.35
  451.9 3.0 fusion.12
  455.7 4.7 all-to-all-start.4
  460.4 8.7 %fusion = f32[2048,1024]{1,0:T(8,128)} fusion(s32[1024]{0:T(1024)S(1)} %eq.17, bf16[512,1024]{1,0:T(8,128)(2,1)} %bitcast.26, bf16[512,1024]{1,0:T(8,128)(2,1)} %bitcast.29), kind=kOutput, calls=%fused_computation.1 | convolution fusion | flops 4301258752 | bytes 10489856 | tf_op jit(solution)/shard_map/dot_general | solution.py:37
  (127 shorter events, 25.5 us)
Async XLA Ops:
  2.1 152.9 %all-to-all-start = ((s32[2,32,16]{2,0,1:T(2,128)}), s32[2,32,16]{2,0,1:T(2,128)S(1)}, u32[]{:S(2)}, u32[]{:S(2)}) async-start(s32[2,32,16]{2,0,1:T(2,128)} %bitcast.11), calls=%async_computation | async-start | bytes 65536 | tf_op jit(solution)/shard_map/all_to_all | solution.py:1193
  9.4 4.2 copy-start.3
  9.4 4.2 copy-start.4
  9.4 4.2 copy-start.30
  11.0 3.9 copy-start.26
  11.0 3.9 copy-start.27
  163.7 3.8 copy-start.28
  163.7 51.2 %all-to-all-start.1 = ((bf16[2,32,16,1024]{3,2,0,1:T(8,128)(2,1)}), bf16[2,32,16,1024]{3,2,0,1:T(8,128)(2,1)}, u32[]{:S(2)}, u32[]{:S(2)}) async-start(bf16[2,32,16,1024]{3,2,0,1:T(8,128)(2,1)} %copy.43), calls=%async_computation.1 | async-start | bytes 4194304 | tf_op jit(solution)/shard_map/all_to_all | solution.py:1223
  168.4 3.5 copy-start.29
  168.4 8.1 %slice-start = ((s8[8388608]{0:T(1024)(128)(4,1)}), s8[4194304]{0:T(1024)(128)(4,1)S(1)}, s32[]{:S(2)}) async-start(s8[8388608]{0:T(1024)(128)(4,1)} %bitcast.139), calls=%async_computation.5 | async-start | bytes 8388608
  171.9 4.6 slice-start.1
  172.2 4.3 copy-start.13
  215.0 3.3 copy-start.37
  217.0 2.7 copy-start.34
  225.3 29.5 %all-to-all-start.2 = ((bf16[32,16,1024]{2,1,0:T(8,128)(2,1)}), bf16[32,16,1024]{2,1,0:T(8,128)(2,1)}, u32[]{:S(2)}, u32[]{:S(2)}) async-start(bf16[32,16,1024]{2,1,0:T(8,128)(2,1)} %bitcast.113), calls=%async_computation.2 | async-start | bytes 2097152 | tf_op jit(solution)/shard_map/all_to_all | solution.py:1196
  234.9 2.7 copy-start.14
  254.8 8.4 %copy-start.7 = (bf16[4,2,2,2,32,1024]{5,4,3,2,1,0:T(8,128)(2,1)S(1)}, bf16[4,2,2,2,32,1024]{5,4,3,2,1,0:T(8,128)(2,1)}, u32[]{:S(2)}) copy-start(bf16[4,2,2,2,32,1024]{5,4,3,2,1,0:T(8,128)(2,1)} %get-tuple-element.58) | copy-start | bytes 6291460
  254.8 8.4 %copy-start.11 = (bf16[512,1024]{1,0:T(8,128)(2,1)S(1)}, bf16[512,1024]{1,0:T(8,128)(2,1)}, u32[]{:S(2)}) copy-start(bf16[512,1024]{1,0:T(8,128)(2,1)} %get-tuple-element.91) | copy-start | bytes 3145732
  266.1 29.6 %all-to-all-start.3 = ((bf16[32,16,1024]{2,1,0:T(8,128)(2,1)}), bf16[32,16,1024]{2,1,0:T(8,128)(2,1)}, u32[]{:S(2)}, u32[]{:S(2)}) async-start(bf16[32,16,1024]{2,1,0:T(8,128)(2,1)} %bitcast.112), calls=%async_computation.3 | async-start | bytes 2097152 | tf_op jit(solution)/shard_map/all_to_all | solution.py:1196
  274.5 4.7 copy-start
  274.5 4.7 copy-start.33
  279.2 2.9 copy-start.39
  446.5 3.4 copy-start.32
  446.5 3.4 copy-start.36
  455.7 16.4 %all-to-all-start.4 = ((f32[32,2,32]{2,1,0:T(2,128)}), f32[32,2,32]{2,1,0:T(2,128)S(1)}, u32[]{:S(2)}, u32[]{:S(2)}) async-start(f32[32,2,32]{2,1,0:T(2,128)} %maximum_bitcast_fusion), calls=%async_computation.4 | async-start | bytes 65536 | tf_op jit(solution)/shard_map/all_to_all | solution.py:1289
  460.4 8.7 %copy-start.1 = (f32[512,1024]{1,0:T(8,128)S(1)}, f32[512,1024]{1,0:T(8,128)}, u32[]{:S(2)}) copy-start(f32[512,1024]{1,0:T(8,128)} %subtract_add_fusion) | copy-start | bytes 6291460
  460.4 8.7 %copy-start.8 = (f32[512,1024]{1,0:T(8,128)S(1)}, f32[512,1024]{1,0:T(8,128)}, u32[]{:S(2)}) copy-start(f32[512,1024]{1,0:T(8,128)} %get-tuple-element.114) | copy-start | bytes 6291460
  469.7 3.0 copy-start.21
  469.7 3.7 copy-start.24
  469.7 4.4 copy-start.20
  471.3 3.6 copy-start.23
  471.3 4.2 copy-start.22
  (15 other events, 27.4 us)

commit v9 on v8

--- a/solution.py
+++ b/solution.py
@@ -13,7 +13,9 @@
 GATHER_LAG = 3
 REST_START = 1
 REST_DELAY = 6
-DEEP_AT = 10
+DEEP_AT = 8
+LATE_LAG = 4
+LAST_LAG = 14
 COLLECT_LAG = 2
 AHEAD = 3
 HOP_LAG = 1
@@ -23,6 +25,7 @@
 HALF = 512
 SUB = 256
 NEVER = -1e30
+PROJECTION_ORDER = ((0, 0), (0, 1), (1, 0), (2, 0), (1, 1), (2, 1))
 
 
 def mm(left, right):
@@ -280,8 +283,9 @@
 
 
 class Reduce:
-    def __init__(self, side, depth, grads, piece, deep_at):
-        self.side, self.depth, self.deep_at = side, depth, deep_at
+    def __init__(self, side, depth, grads, piece, lag, deep_at, last_at):
+        self.side, self.depth, self.lag = side, depth, lag
+        self.deep_at, self.last_at = deep_at, last_at
         self.layout, self.views, self.outs = [], [], []
         self.width = width = piece
         devices = 2 * side * side * depth
@@ -296,7 +300,7 @@
             ]
             self.outs.append(jax.ShapeDtypeStruct(lead + (block, cols), F32))
         self.count = count = len(self.layout)
-        self.steps = count + deep_at + LAG
+        self.steps = count + last_at
         dma = pltpu.SemaphoreType.DMA
         self.scratch = [
             pltpu.VMEM((count, side, side, depth, block, width), BF),
@@ -450,10 +454,10 @@
     def step(self, i):
         stages = (
             (0, self.after_core),
-            (LAG, self.after_one),
-            (2 * LAG, self.after_two),
+            (self.lag, self.after_one),
+            (2 * self.lag, self.after_two),
             (self.deep_at, self.send_deep),
-            (self.deep_at + LAG, self.after_deep),
+            (self.last_at, self.after_deep),
         )
         for lag, action in stages:
             @pl.when(jnp.logical_and(i >= lag, i < self.count + lag))
@@ -896,9 +900,8 @@
         lax.fori_loop(0, self.pairs, drain, 0)
 
 
-def produce(late, stage, kind, half, normed_ref, grad_ref):
+def produce(late, stage, k, half, normed_ref, grad_ref):
     side, depth, block, width = late.side, late.depth, late.block, late.width
-    k = 2 * kind + half
     run = depth * block
     for start in range(0, normed_ref.shape[1], 2 * PAIR):
         value = dot_first(
@@ -938,9 +941,10 @@
         early.start(k)
     last = (depth - 1) * COLLECT_LAG
     ready = max(pairs, early.count)
-    settled = max(pairs + last, ready + 2)
-    late_at = settled - 1
-    due = [ready, ready + 1, settled, settled + 1, settled + 2, settled + 3]
+    halfway = max(ready + 2, last + pairs // 2 - 1)
+    settled = max(halfway + 2, last + pairs - 1)
+    due = [ready, ready + 1, halfway, halfway + 1, settled, settled + 1]
+    late_at = 1 + max(when - number for number, when in enumerate(due))
 
     def run(i, carry):
         @pl.when(i < pairs)
@@ -963,8 +967,8 @@
         for number, when in enumerate(due):
             @pl.when(i == when)
             def _(number=number):
-                kind = number // 2
-                produce(late, stage, kind, number % 2, normed_ref, (dq_ref, dk_ref, dv_ref)[kind])
+                kind, half = PROJECTION_ORDER[number]
+                produce(late, stage, number, half, normed_ref, (dq_ref, dk_ref, dv_ref)[kind])
                 late.start(number)
 
         return carry
@@ -978,8 +982,9 @@
 def attention_backward(side, depth, q, k, v, keys, vals, lse, att, grad_att, normed, grads, w_qkv,
                        call_id):
     rows, width = q.shape[0] // 2, q.shape[1]
-    early = Reduce(side, depth, grads, width, DEEP_AT)
-    late = Reduce(side, depth, (w_qkv,), width // 2, 2 * LAG)
+    early = Reduce(side, depth, grads, width, LAG, DEEP_AT, DEEP_AT + LAST_LAG)
+    late = Reduce(side, depth, (w_qkv,), width // 2, LATE_LAG, 2 * LATE_LAG, 3 * LATE_LAG)
+    late.layout = [(0, kind, half * (width // 2)) for kind, half in PROJECTION_ORDER]
     collect = Collect(depth, rows, width // PAIR)
     any_space, vmem = pl.BlockSpec(memory_space=pl.ANY), pl.BlockSpec(memory_space=pltpu.VMEM)
     results = pl.pallas_call(

time: 481 us -> 477 us (level)
  no operation moved by 1% of the time
where the time goes in v9:
time: 477 us; the launch traced here: 472 us
  Pallas kernels  313 us (66%)
  matrix products  73.8 us (15%)
  waiting for transfers between devices  28 us (6%)
  local copies, waits for them, and re-layouts  24.5 us (5%)
  starting transfers between devices  23.3 us (5%)
  other arithmetic  8.12 us (2%)
    pallas_call x1, Pallas kernels, attention_backward(): pl.pallas_call(functools.partial(backward_kernel, early, late, collect),...  148 us
    pallas_call x1, Pallas kernels, attention_forward(): pl.pallas_call(functools.partial(forward_kernel, first, rest, exchange, s...  139 us
    dot_general x5, matrix products, mm_l(): lax.dot_general(left, right, (((0,), (0,)), ((), ())), preferred_element_...  25.4 us
    dot_general x7, matrix products, mm_t(): lax.dot_general(left, right, (((1,), (1,)), ((), ())), preferred_element_...  24.5 us
    dot_general x5, matrix products, mm(): return jnp.dot(left, right, preferred_element_type=F32)  22.4 us
    all_to_all x1, waiting for transfers between devices, per_device(): lax.all_to_all(served, ALL, split_axis=1, concat_axis=1, tiled=True)  18.9 us
    pallas_call x1, Pallas kernels, slot_weights(): pl.pallas_call(picks_kernel, grid=(MH,), out_shape=(jax.ShapeDtypeStruct(...  13.5 us
    pallas_call x1, Pallas kernels, slot_weights_back(): pl.pallas_call(functools.partial(picks_back_kernel, block), grid=(MH,), o...  12.4 us
  transfers between devices with their start and end apart: 5, of which 3 were waited for; matrix products, arithmetic and copies ran while one was open for 12% of the time, Pallas kernels for 35%

profile of v9, /device:TPU:0, one launch (start us, length us, event | category | flops | bytes accessed | tf_op | source)
XLA Modules:
  0.0 472.2 jit_solution(10109239343954151673)
XLA Ops:
  2.1 7.3 %all-to-all-start = ((s32[2,32,16]{2,0,1:T(2,128)}), s32[2,32,16]{2,0,1:T(2,128)S(1)}, u32[]{:S(2)}, u32[]{:S(2)}) async-start(s32[2,32,16]{2,0,1:T(2,128)} %bitcast.11), calls=%async_computation | async-start | bytes 65536 | tf_op jit(solution)/shard_map/all_to_all | solution.py:1198
  11.0 2.6 fusion.31
  15.9 139.0 %shard_map.255 = (bf16[2,4,512,256]{3,2,1,0:T(8,128)(2,1)}, bf16[512,1024]{1,0:T(8,128)(2,1)}, bf16[512,1024]{1,0:T(8,128)(2,1)}, bf16[512,1024]{1,0:T(8,128)(2,...) custom-call(s32[32,2048]{1,0:T(8,128)} %reshape.291.refs_0_, ...), custom_call_target="tpu_custom_call" | custom-call | tf_op jit(solution)/shard_map/pallas_call | solution.py:784
  155.0 7.1 %fusion.20 = bf16[1024,1024]{1,0:T(8,128)(2,1)S(1)} fusion(bf16[2048,1024]{1,0:T(8,128)(2,1)} %param.28, s32[1024]{0:T(1024)S(1)} %eq.17), kind=kOutput, calls=%fused_computation.41 | convolution fusion | flops 4298113024 | bytes 6295552 | tf_op jit(solution)/shard_map/dot_general | solution.py:32
  163.7 3.8 all-to-all-start.1
  168.4 3.5 multiply_reduce_fusion.2
  172.2 1.7 copy-done.6
  173.9 2.6 fusion.33
  176.5 6.1 %convolution_convert_fusion.1.query_ref = bf16[512,4096]{1,0:T(8,128)(2,1)} fusion(bf16[512,1024]{1,0:T(8,128)(2,1)S(1)} %multiply_convert_fusion.1, bf16[1024,4096]{1,0:T(8,128)(2,1)S(1)} %bitcast.141), kind=kOutput, calls=%fused_computation.4 | convolution fusion | flops 4297064448 | bytes 13631488 | tf_op jit(solution)/shard_map/dot_general | solution.py:32
  182.6 13.5 %shard_map.256 = (f32[2,4,512,256]{3,2,1,0:T(8,128)}, bf16[2,512,256]{2,1,0:T(8,128)(2,1)}) custom-call(s32[4,512]{1,0:T(4,128)} %reshape.298.ids_ref, bf16[2,4,512,256]{3,2,1,0:T(8,128)(2,1)} %get-tuple-element.53.counts_ref, bf16[512,4096]{1,0:T(8,128)(2,1)} %convolution_convert_fusion.1.query_ref, bf16[2048,512]{1,0:T(8,128)(2,1)} %bitcast.147), custom_call_target="tpu_custom_call" | custom-call | flops 4294967296 | bytes 25165824 | tf_op jit(solution)/shard_map/pallas_call | solution.py:1073
  196.1 18.9 %all-to-all-done.1 = bf16[2,32,16,1024]{3,2,0,1:T(8,128)(2,1)} async-done(((bf16[2,32,16,1024]{3,2,0,1:T(8,128)(2,1)}), bf16[2,32,16,1024]{3,2,0,1:T(8,128)(2,1)}, u32[]{:S(2)}, u32[]{:S(2)}) %all-to-all-start.1) | async-done | bytes 2097184 | tf_op jit(solution)/shard_map/all_to_all | solution.py:1228
  215.0 1.9 copy.44
  219.7 3.3 fusion.19
  225.3 4.5 all-to-all-start.2
  229.8 3.2 add_convert_fusion
  234.9 2.7 convolution_convert_fusion.4
  237.6 2.6 convolution_convert_fusion.5
  240.2 12.4 %shard_map.257 = (bf16[512,4096]{1,0:T(8,128)(2,1)}, bf16[1024,1024]{1,0:T(8,128)(2,1)}) custom-call(s32[4,512]{1,0:T(4,128)} %reshape.298.ids_ref, f32[2,4,512,256]{3,2,1,0:T(8,128)} %get-tuple-element.60.weight_ref, bf16[2,512,1024]{2,1,0:T(8,128)(2,1)} %bitcast.100, bf16[512,1024]{1,0:T(8,128)(2,1)} %copy-done.12, ...), custom_call_target="tpu_custom_call" | custom-call | flops 6442450944 | bytes 25165824 | tf_op jit(solution)/shard_map/pallas_call | solution.py:1140
  252.5 2.3 all-to-all-done.2
  254.8 8.4 %fusion.34 = f32[512,1024]{1,0:T(8,128)S(1)} fusion(bf16[512,4096]{1,0:T(8,128)(2,1)} %get-tuple-element.62, bf16[1024,4096]{1,0:T(8,128)(2,1)} %bitcast.138), kind=kOutput, calls=%fused_computation.90 | convolution fusion | flops 4294967296 | bytes 14680064 | tf_op jit(solution)/shard_map/dot_general | solution.py:36
  263.2 2.9 multiply_reduce_fusion
  266.1 4.6 all-to-all-start.3
  270.7 3.7 subtract_add_fusion
  274.6 4.7 convolution_convert_fusion.3
  279.2 2.3 convolution_convert_fusion.6.refs_7_
  282.1 6.8 %convolution_convert_fusion = bf16[1024,4096]{1,0:T(8,128)(2,1)} fusion(bf16[512,1024]{1,0:T(8,128)(2,1)S(1)} %copy-done.15, bf16[512,4096]{1,0:T(8,128)(2,1)S(1)} %copy-done.39), kind=kOutput, calls=%fused_computation.3 | convolution fusion | flops 4299161600 | bytes 13631488 | tf_op jit(solution)/shard_map/dot_general | solution.py:40
  288.9 6.9 %all-to-all-done.3 = bf16[32,16,1024]{2,1,0:T(8,128)(2,1)} async-done(((bf16[32,16,1024]{2,1,0:T(8,128)(2,1)}), bf16[32,16,1024]{2,1,0:T(8,128)(2,1)}, u32[]{:S(2)}, u32[]{:S(2)}) %all-to-all-start.3) | async-done | bytes 1048608 | tf_op jit(solution)/shard_map/all_to_all | solution.py:1201
  295.8 148.2 %shard_map.258 = (bf16[512,1024]{1,0:T(8,128)(2,1)}, bf16[512,1024]{1,0:T(8,128)(2,1)}, bf16[512,1024]{1,0:T(8,128)(2,1)}, f32[32,4096]{1,0:T(8,128)}, f32[32,10...) custom-call(bf16[512,1024]{1,0:T(8,128)(2,1)} %get-tuple-element.63.ref, ...), custom_call_target="tpu_custom_call" | custom-call | tf_op jit(solution)/shard_map/pallas_call | solution.py:990
  444.0 3.3 fusion.35
  449.4 3.0 fusion.12
  453.1 3.1 all-to-all-start.4
  456.3 8.7 %fusion = f32[2048,1024]{1,0:T(8,128)} fusion(s32[1024]{0:T(1024)S(1)} %eq.17, bf16[512,1024]{1,0:T(8,128)(2,1)} %bitcast.26, bf16[512,1024]{1,0:T(8,128)(2,1)} %bitcast.29), kind=kOutput, calls=%fused_computation.1 | convolution fusion | flops 4301258752 | bytes 10489856 | tf_op jit(solution)/shard_map/dot_general | solution.py:40
  (127 shorter events, 25.5 us)
Async XLA Ops:
  2.1 152.9 %all-to-all-start = ((s32[2,32,16]{2,0,1:T(2,128)}), s32[2,32,16]{2,0,1:T(2,128)S(1)}, u32[]{:S(2)}, u32[]{:S(2)}) async-start(s32[2,32,16]{2,0,1:T(2,128)} %bitcast.11), calls=%async_computation | async-start | bytes 65536 | tf_op jit(solution)/shard_map/all_to_all | solution.py:1198
  9.4 4.2 copy-start.3
  9.4 4.2 copy-start.4
  9.4 4.2 copy-start.30
  11.0 3.9 copy-start.26
  11.0 3.9 copy-start.27
  163.7 3.8 copy-start.28
  163.7 51.2 %all-to-all-start.1 = ((bf16[2,32,16,1024]{3,2,0,1:T(8,128)(2,1)}), bf16[2,32,16,1024]{3,2,0,1:T(8,128)(2,1)}, u32[]{:S(2)}, u32[]{:S(2)}) async-start(bf16[2,32,16,1024]{3,2,0,1:T(8,128)(2,1)} %copy.43), calls=%async_computation.1 | async-start | bytes 4194304 | tf_op jit(solution)/shard_map/all_to_all | solution.py:1228
  168.4 3.5 copy-start.29
  168.4 8.1 %slice-start = ((s8[8388608]{0:T(1024)(128)(4,1)}), s8[4194304]{0:T(1024)(128)(4,1)S(1)}, s32[]{:S(2)}) async-start(s8[8388608]{0:T(1024)(128)(4,1)} %bitcast.139), calls=%async_computation.5 | async-start | bytes 8388608
  171.9 4.6 slice-start.1
  172.2 4.3 copy-start.13
  215.0 3.3 copy-start.37
  217.0 2.7 copy-start.34
  225.3 29.5 %all-to-all-start.2 = ((bf16[32,16,1024]{2,1,0:T(8,128)(2,1)}), bf16[32,16,1024]{2,1,0:T(8,128)(2,1)}, u32[]{:S(2)}, u32[]{:S(2)}) async-start(bf16[32,16,1024]{2,1,0:T(8,128)(2,1)} %bitcast.113), calls=%async_computation.2 | async-start | bytes 2097152 | tf_op jit(solution)/shard_map/all_to_all | solution.py:1201
  234.9 2.7 copy-start.14
  254.8 8.4 %copy-start.7 = (bf16[4,2,2,2,32,1024]{5,4,3,2,1,0:T(8,128)(2,1)S(1)}, bf16[4,2,2,2,32,1024]{5,4,3,2,1,0:T(8,128)(2,1)}, u32[]{:S(2)}) copy-start(bf16[4,2,2,2,32,1024]{5,4,3,2,1,0:T(8,128)(2,1)} %get-tuple-element.58) | copy-start | bytes 6291460
  254.8 8.4 %copy-start.11 = (bf16[512,1024]{1,0:T(8,128)(2,1)S(1)}, bf16[512,1024]{1,0:T(8,128)(2,1)}, u32[]{:S(2)}) copy-start(bf16[512,1024]{1,0:T(8,128)(2,1)} %get-tuple-element.91) | copy-start | bytes 3145732
  266.1 29.6 %all-to-all-start.3 = ((bf16[32,16,1024]{2,1,0:T(8,128)(2,1)}), bf16[32,16,1024]{2,1,0:T(8,128)(2,1)}, u32[]{:S(2)}, u32[]{:S(2)}) async-start(bf16[32,16,1024]{2,1,0:T(8,128)(2,1)} %bitcast.112), calls=%async_computation.3 | async-start | bytes 2097152 | tf_op jit(solution)/shard_map/all_to_all | solution.py:1201
  274.5 4.7 copy-start
  274.5 4.7 copy-start.33
  279.2 2.9 copy-start.39
  443.9 3.4 copy-start.32
  443.9 3.4 copy-start.36
  453.1 14.8 %all-to-all-start.4 = ((f32[32,2,32]{2,1,0:T(2,128)}), f32[32,2,32]{2,1,0:T(2,128)S(1)}, u32[]{:S(2)}, u32[]{:S(2)}) async-start(f32[32,2,32]{2,1,0:T(2,128)} %maximum_bitcast_fusion), calls=%async_computation.4 | async-start | bytes 65536 | tf_op jit(solution)/shard_map/all_to_all | solution.py:1294
  456.3 8.7 %copy-start.1 = (f32[512,1024]{1,0:T(8,128)S(1)}, f32[512,1024]{1,0:T(8,128)}, u32[]{:S(2)}) copy-start(f32[512,1024]{1,0:T(8,128)} %subtract_add_fusion) | copy-start | bytes 6291460
  456.3 8.7 %copy-start.8 = (f32[512,1024]{1,0:T(8,128)S(1)}, f32[512,1024]{1,0:T(8,128)}, u32[]{:S(2)}) copy-start(f32[512,1024]{1,0:T(8,128)} %get-tuple-element.114) | copy-start | bytes 6291460
  465.5 3.0 copy-start.21
  465.5 3.7 copy-start.24
  465.5 4.4 copy-start.20
  467.1 3.6 copy-start.23
  467.1 4.2 copy-start.22
  (15 other events, 27.4 us)

commit v10 on v9

--- a/solution.py
+++ b/solution.py
@@ -694,9 +694,9 @@
     depth, rows, pairs = exchange.depth, exchange.rows, exchange.pairs
     n = len(rest.views)
     ((picks_ref, normed_ref), shard, shards, outs, weights, full, swap, held,
-     others) = split_refs(refs, 2, 3, n, 8, 3, n, len(exchange.scratch), len(first.scratch))
+     others) = split_refs(refs, 2, 1, n, 8, 3, n, len(exchange.scratch), len(first.scratch))
     counts_ref, q_ref, k_ref, v_ref, att_ref, lse_ref, keys, vals = outs
-    first.bind(shard, weights, held)
+    first.bind([shard[0].at[kind] for kind in (1, 2, 0)], weights, held)
     rest.bind(shards, full, others)
     exchange.bind((k_ref, v_ref), (keys, vals), swap)
     z = lax.axis_index("fsdp")
@@ -773,10 +773,11 @@
     rest.finish()
 
 
-def attention_forward(side, depth, picks, normed, projections, shards, slots, call_id):
+def attention_forward(side, depth, picks, normed, w_qkv, shards, slots, call_id):
     rows, width = normed.shape[0] // 2, normed.shape[1]
     pairs = width // PAIR
-    first, rest = Gather(side, depth, projections), Gather(side, depth, shards)
+    first, rest = Gather(side, depth, list(w_qkv)), Gather(side, depth, shards)
+    packed = w_qkv.reshape(w_qkv.shape[:1] + first.views[0].shape)
     exchange = Exchange(depth, rows, pairs)
     any_space, vmem = pl.BlockSpec(memory_space=pl.ANY), pl.BlockSpec(memory_space=pltpu.VMEM)
     spread = jax.ShapeDtypeStruct((pairs, depth, rows, PAIR), BF)
@@ -795,11 +796,11 @@
         )
         + tuple(first.outs)
         + tuple(rest.outs),
-        in_specs=[vmem] * 2 + [any_space] * (3 + len(rest.views)),
+        in_specs=[vmem] * 2 + [any_space] * (1 + len(rest.views)),
         out_specs=(vmem,) * 11 + (any_space,) * len(rest.views),
         scratch_shapes=exchange.scratch + first.scratch + rest.scratch,
         compiler_params=params(call_id, 56),
-    )(picks, normed, *first.views, *rest.views)
+    )(picks, normed, packed, *rest.views)
     return results[:8], first.restore(results[8:11]), rest.restore(results[11:])
 
 
@@ -1215,7 +1216,7 @@
         depth,
         picks,
         normed,
-        (w_qkv[1], w_qkv[2], w_qkv[0]),
+        w_qkv,
         (w_attn_out, w_mem_query, sub_keys, w_gate, w_mem_out),
         slots,
         0,

time: 477 us -> 474 us (level)
    unnamed x90 -> x88, local copies, waits for them, and re-layouts: 10.9 us -> 10.9 us
where the time goes in v10:
time: 474 us; the launch traced here: 469 us
  Pallas kernels  313 us (66%)
  matrix products  72.5 us (15%)
  waiting for transfers between devices  28.2 us (6%)
  starting transfers between devices  23.3 us (5%)
  local copies, waits for them, and re-layouts  21.9 us (5%)
  other arithmetic  9.11 us (2%)
    pallas_call x1, Pallas kernels, attention_backward(): pl.pallas_call(functools.partial(backward_kernel, early, late, collect),...  148 us
    pallas_call x1, Pallas kernels, attention_forward(): pl.pallas_call(functools.partial(forward_kernel, first, rest, exchange, s...  139 us
    dot_general x5, matrix products, mm_l(): lax.dot_general(left, right, (((0,), (0,)), ((), ())), preferred_element_...  25.4 us
    dot_general x7, matrix products, mm_t(): lax.dot_general(left, right, (((1,), (1,)), ((), ())), preferred_element_...  23.3 us
    dot_general x5, matrix products, mm(): return jnp.dot(left, right, preferred_element_type=F32)  22.3 us
    all_to_all x1, waiting for transfers between devices, per_device(): lax.all_to_all(served, ALL, split_axis=1, concat_axis=1, tiled=True)  19 us
    pallas_call x1, Pallas kernels, slot_weights(): pl.pallas_call(picks_kernel, grid=(MH,), out_shape=(jax.ShapeDtypeStruct(...  13.5 us
    pallas_call x1, Pallas kernels, slot_weights_back(): pl.pallas_call(functools.partial(picks_back_kernel, block), grid=(MH,), o...  12.4 us
  transfers between devices with their start and end apart: 5, of which 3 were waited for; matrix products, arithmetic and copies ran while one was open for 12% of the time, Pallas kernels for 35%

profile of v10, /device:TPU:0, one launch (start us, length us, event | category | flops | bytes accessed | tf_op | source)
XLA Modules:
  0.0 469.5 jit_solution(4283083574627254542)
XLA Ops:
  2.1 7.3 %all-to-all-start = ((s32[2,32,16]{2,0,1:T(2,128)}), s32[2,32,16]{2,0,1:T(2,128)S(1)}, u32[]{:S(2)}, u32[]{:S(2)}) async-start(s32[2,32,16]{2,0,1:T(2,128)} %bitcast.9), calls=%async_computation | async-start | bytes 65536 | tf_op jit(solution)/shard_map/all_to_all | solution.py:1199
  10.9 2.5 fusion.6.refs_1_.refs_8_
  14.5 139.0 %shard_map.255 = (bf16[2,4,512,256]{3,2,1,0:T(8,128)(2,1)}, bf16[512,1024]{1,0:T(8,128)(2,1)}, bf16[512,1024]{1,0:T(8,128)(2,1)}, bf16[512,1024]{1,0:T(8,128)(2,...) custom-call(s32[32,2048]{1,0:T(8,128)} %reshape.294.refs_0_, ...), custom_call_target="tpu_custom_call" | custom-call | tf_op jit(solution)/shard_map/pallas_call | solution.py:785
  153.6 7.1 %fusion.20 = bf16[1024,1024]{1,0:T(8,128)(2,1)S(1)} fusion(bf16[2048,1024]{1,0:T(8,128)(2,1)} %param.28, s32[1024]{0:T(1024)S(1)} %eq.17), kind=kOutput, calls=%fused_computation.41 | convolution fusion | flops 4298113024 | bytes 6295552 | tf_op jit(solution)/shard_map/dot_general | solution.py:32
  162.3 3.8 all-to-all-start.1
  166.9 3.4 multiply_reduce_fusion.2
  170.6 1.7 copy-done.6
  172.3 2.6 fusion.32
  174.9 6.1 %convolution_convert_fusion.1.query_ref = bf16[512,4096]{1,0:T(8,128)(2,1)} fusion(bf16[512,1024]{1,0:T(8,128)(2,1)S(1)} %multiply_convert_fusion.1, bf16[1024,4096]{1,0:T(8,128)(2,1)S(1)} %bitcast.137), kind=kOutput, calls=%fused_computation.4 | convolution fusion | flops 4297064448 | bytes 13631488 | tf_op jit(solution)/shard_map/dot_general | solution.py:32
  181.0 13.5 %shard_map.256 = (f32[2,4,512,256]{3,2,1,0:T(8,128)}, bf16[2,512,256]{2,1,0:T(8,128)(2,1)}) custom-call(s32[4,512]{1,0:T(4,128)} %reshape.302.ids_ref, bf16[2,4,512,256]{3,2,1,0:T(8,128)(2,1)} %get-tuple-element.53.counts_ref, bf16[512,4096]{1,0:T(8,128)(2,1)} %convolution_convert_fusion.1.query_ref, bf16[2048,512]{1,0:T(8,128)(2,1)} %bitcast.143), custom_call_target="tpu_custom_call" | custom-call | flops 4294967296 | bytes 25165824 | tf_op jit(solution)/shard_map/pallas_call | solution.py:1074
  194.5 19.0 %all-to-all-done.1 = bf16[2,32,16,1024]{3,2,0,1:T(8,128)(2,1)} async-done(((bf16[2,32,16,1024]{3,2,0,1:T(8,128)(2,1)}), bf16[2,32,16,1024]{3,2,0,1:T(8,128)(2,1)}, u32[]{:S(2)}, u32[]{:S(2)}) %all-to-all-start.1) | async-done | bytes 2097184 | tf_op jit(solution)/shard_map/all_to_all | solution.py:1229
  213.5 1.9 copy.44
  218.2 3.3 fusion.19
  223.7 4.5 all-to-all-start.2
  228.3 3.2 add_convert_fusion
  233.4 2.6 convolution_convert_fusion.4
  236.0 2.6 convolution_convert_fusion.5
  238.7 12.4 %shard_map.257 = (bf16[512,4096]{1,0:T(8,128)(2,1)}, bf16[1024,1024]{1,0:T(8,128)(2,1)}) custom-call(s32[4,512]{1,0:T(4,128)} %reshape.302.ids_ref, f32[2,4,512,256]{3,2,1,0:T(8,128)} %get-tuple-element.60.weight_ref, bf16[2,512,1024]{2,1,0:T(8,128)(2,1)} %bitcast.98, bf16[512,1024]{1,0:T(8,128)(2,1)} %copy-done.11, ...), custom_call_target="tpu_custom_call" | custom-call | flops 6442450944 | bytes 25165824 | tf_op jit(solution)/shard_map/pallas_call | solution.py:1141
  251.1 2.2 all-to-all-done.2
  253.3 8.4 %fusion.33 = f32[512,1024]{1,0:T(8,128)S(1)} fusion(bf16[512,4096]{1,0:T(8,128)(2,1)} %get-tuple-element.62, bf16[1024,4096]{1,0:T(8,128)(2,1)} %bitcast.134), kind=kOutput, calls=%fused_computation.89 | convolution fusion | flops 4294967296 | bytes 14680064 | tf_op jit(solution)/shard_map/dot_general | solution.py:36
  261.7 2.9 multiply_reduce_fusion
  264.6 4.6 all-to-all-start.3
  269.2 3.6 subtract_add_fusion
  272.9 4.6 convolution_convert_fusion.3
  277.6 2.3 convolution_convert_fusion.6.refs_7_
  280.4 6.8 %convolution_convert_fusion = bf16[1024,4096]{1,0:T(8,128)(2,1)} fusion(bf16[512,1024]{1,0:T(8,128)(2,1)S(1)} %copy-done.14, bf16[512,4096]{1,0:T(8,128)(2,1)S(1)} %copy-done.38), kind=kOutput, calls=%fused_computation.3 | convolution fusion | flops 4299161600 | bytes 13631488 | tf_op jit(solution)/shard_map/dot_general | solution.py:40
  287.2 7.0 %all-to-all-done.3 = bf16[32,16,1024]{2,1,0:T(8,128)(2,1)} async-done(((bf16[32,16,1024]{2,1,0:T(8,128)(2,1)}), bf16[32,16,1024]{2,1,0:T(8,128)(2,1)}, u32[]{:S(2)}, u32[]{:S(2)}) %all-to-all-start.3) | async-done | bytes 1048608 | tf_op jit(solution)/shard_map/all_to_all | solution.py:1202
  294.2 148.2 %shard_map.258 = (bf16[512,1024]{1,0:T(8,128)(2,1)}, bf16[512,1024]{1,0:T(8,128)(2,1)}, bf16[512,1024]{1,0:T(8,128)(2,1)}, f32[32,4096]{1,0:T(8,128)}, f32[32,10...) custom-call(bf16[512,1024]{1,0:T(8,128)(2,1)} %get-tuple-element.63.ref, ...), custom_call_target="tpu_custom_call" | custom-call | tf_op jit(solution)/shard_map/pallas_call | solution.py:991
  442.4 3.3 fusion.34
  447.9 1.8 fusion.12
  450.4 3.1 all-to-all-start.4
  453.6 8.7 %fusion = f32[2048,1024]{1,0:T(8,128)} fusion(s32[1024]{0:T(1024)S(1)} %eq.17, bf16[512,1024]{1,0:T(8,128)(2,1)} %bitcast.24, bf16[512,1024]{1,0:T(8,128)(2,1)} %bitcast.27), kind=kOutput, calls=%fused_computation.1 | convolution fusion | flops 4301258752 | bytes 10489856 | tf_op jit(solution)/shard_map/dot_general | solution.py:40
  (124 shorter events, 24.1 us)
Async XLA Ops:
  0.6 12.8 %copy-start.25 = (s32[1,256,4,32]{1,3,2,0:T(8,128)S(1)}, s32[1,256,4,32]{1,3,2,0:T(8,128)}, u32[]{:S(2)}) copy-start(s32[1,256,4,32]{1,3,2,0:T(8,128)} %param.31) | copy-start | bytes 393220
  0.7 12.8 %copy-start.26 = (s32[1,256,4,32]{1,3,2,0:T(8,128)S(1)}, s32[1,256,4,32]{1,3,2,0:T(8,128)}, u32[]{:S(2)}) copy-start(s32[1,256,4,32]{1,3,2,0:T(8,128)} %param.30) | copy-start | bytes 393220
  2.1 151.4 %all-to-all-start = ((s32[2,32,16]{2,0,1:T(2,128)}), s32[2,32,16]{2,0,1:T(2,128)S(1)}, u32[]{:S(2)}, u32[]{:S(2)}) async-start(s32[2,32,16]{2,0,1:T(2,128)} %bitcast.9), calls=%async_computation | async-start | bytes 65536 | tf_op jit(solution)/shard_map/all_to_all | solution.py:1199
  162.3 3.8 copy-start.27
  162.3 4.7 copy-start.3
  162.3 4.7 copy-start.4
  162.3 51.2 %all-to-all-start.1 = ((bf16[2,32,16,1024]{3,2,0,1:T(8,128)(2,1)}), bf16[2,32,16,1024]{3,2,0,1:T(8,128)(2,1)}, u32[]{:S(2)}, u32[]{:S(2)}) async-start(bf16[2,32,16,1024]{3,2,0,1:T(8,128)(2,1)} %copy.43), calls=%async_computation.1 | async-start | bytes 4194304 | tf_op jit(solution)/shard_map/all_to_all | solution.py:1229
  166.9 3.4 copy-start.28
  166.9 8.0 %slice-start = ((s8[8388608]{0:T(1024)(128)(4,1)}), s8[4194304]{0:T(1024)(128)(4,1)S(1)}, s32[]{:S(2)}) async-start(s8[8388608]{0:T(1024)(128)(4,1)} %bitcast.135), calls=%async_computation.5 | async-start | bytes 8388608
  170.4 4.5 slice-start.1
  170.6 4.3 copy-start.12
  194.5 20.9 %copy-start.8 = (bf16[2,512,256]{2,1,0:T(8,128)(2,1)S(1)}, bf16[2,512,256]{2,1,0:T(8,128)(2,1)}, u32[]{:S(2)}) copy-start(bf16[2,512,256]{2,1,0:T(8,128)(2,1)} %get-tuple-element.56) | copy-start | bytes 1572868
  213.5 3.3 copy-start.36
  215.5 2.7 copy-start.33
  223.7 29.5 %all-to-all-start.2 = ((bf16[32,16,1024]{2,1,0:T(8,128)(2,1)}), bf16[32,16,1024]{2,1,0:T(8,128)(2,1)}, u32[]{:S(2)}, u32[]{:S(2)}) async-start(bf16[32,16,1024]{2,1,0:T(8,128)(2,1)} %bitcast.111), calls=%async_computation.2 | async-start | bytes 2097152 | tf_op jit(solution)/shard_map/all_to_all | solution.py:1202
  233.4 2.7 copy-start.9
  233.4 2.7 copy-start.13
  253.3 8.4 %copy-start.7 = (bf16[4,2,2,2,32,1024]{5,4,3,2,1,0:T(8,128)(2,1)S(1)}, bf16[4,2,2,2,32,1024]{5,4,3,2,1,0:T(8,128)(2,1)}, u32[]{:S(2)}) copy-start(bf16[4,2,2,2,32,1024]{5,4,3,2,1,0:T(8,128)(2,1)} %get-tuple-element.58) | copy-start | bytes 6291460
  253.3 8.4 %copy-start.10 = (bf16[512,1024]{1,0:T(8,128)(2,1)S(1)}, bf16[512,1024]{1,0:T(8,128)(2,1)}, u32[]{:S(2)}) copy-start(bf16[512,1024]{1,0:T(8,128)(2,1)} %get-tuple-element.91) | copy-start | bytes 3145732
  264.6 29.6 %all-to-all-start.3 = ((bf16[32,16,1024]{2,1,0:T(8,128)(2,1)}), bf16[32,16,1024]{2,1,0:T(8,128)(2,1)}, u32[]{:S(2)}, u32[]{:S(2)}) async-start(bf16[32,16,1024]{2,1,0:T(8,128)(2,1)} %bitcast.110), calls=%async_computation.3 | async-start | bytes 2097152 | tf_op jit(solution)/shard_map/all_to_all | solution.py:1202
  272.9 4.7 copy-start
  272.9 4.7 copy-start.32
  277.6 2.9 copy-start.38
  442.4 3.4 copy-start.31
  442.4 3.4 copy-start.35
  450.4 14.8 %all-to-all-start.4 = ((f32[32,2,32]{2,1,0:T(2,128)}), f32[32,2,32]{2,1,0:T(2,128)S(1)}, u32[]{:S(2)}, u32[]{:S(2)}) async-start(f32[32,2,32]{2,1,0:T(2,128)} %maximum_bitcast_fusion), calls=%async_computation.4 | async-start | bytes 65536 | tf_op jit(solution)/shard_map/all_to_all | solution.py:1295
  453.6 8.7 %copy-start.1 = (f32[512,1024]{1,0:T(8,128)S(1)}, f32[512,1024]{1,0:T(8,128)}, u32[]{:S(2)}) copy-start(f32[512,1024]{1,0:T(8,128)} %subtract_add_fusion) | copy-start | bytes 6291460
  462.8 3.0 copy-start.20
  462.8 3.7 copy-start.23
  462.8 4.4 copy-start.19
  464.4 3.6 copy-start.22
  464.4 4.2 copy-start.21
  (14 other events, 24.1 us)
